TPU v7x, 512 devices: a whole 4x4x16 slice. The times are simulated.
512 devices in a mesh: blk: 128 (over y, z, x_lo), team: 4 (over x_hi, core).
Axes of the slice: x: 4 (x_hi: 2, x_lo: 2; x = x_hi * 2 + x_lo), y: 4, z: 16, core: 2. Of those that a mesh axis runs over, the one named last changes fastest.
Arguments:
- omega: float32 [128, 24, 128, 128], P('blk'), may hold values from -0.05 to 2, as said below
- dosage: float32 [128, 256, 128], P('blk', 'team'), may hold values from -6 to 6
- columns: int32 [128, 24], P('blk'), may hold values from 0 to 127, as said below
- counts: int32 [128], P('blk'), may hold values from 1 to 24, as said below
Outputs:
- new_omega: float32 [128, 24, 128, 128], P('blk')
- y_product: float32 [128, 256, 128], P('blk', 'team')
Inputs may be any that keep to these rules, and one draw needn't show every extreme that they name: The first counts[b] slots of row b hold distinct block columns in ascending order, b among them; the pattern is symmetric (c is listed in row b exactly when b is listed in row c); every live column c of row b has |c - b| <= 8, or (c - b) mod 128 equal to f or 128 - f for one of the offsets f = 64 - j * 13, j = 0 to 3, and every row is linked at all these distant offsets; the other slots hold b. `counts`: some block row has exactly 24 in every draw. `omega`: symmetric: the block in row b for column c is the transpose of the block in row c for column b; diagonal entries of diagonal blocks lie in 1 to 2, all other entries in -0.05 to 0.05.
All inputs are finite; a program needn't handle non-finite values.
Results may differ from a plain program's by a relative error of at most 0.0003.
Values sent between devices are 32-bit elements; how exact they have to be, the bound alone decides.
No kernel may reach another device: no remote copies, remote signals or barrier semaphores. Data moves between devices by JAX's collectives and lax.ppermute only.
A program may use at most 64 MiB of HBM per device.

v0:
```python
import functools

import jax
import jax.numpy as jnp
import numpy as np
from jax import lax
from jax.experimental import pallas as pl
from jax.experimental.pallas import tpu as pltpu
from jax.sharding import PartitionSpec as P


step_size = 0.1
penalty = 0.05


AXES = ("blk", "team")
NEAR_1, NEAR_2, SIDE_1, SIDE_2, FAR_1, FAR_2 = range(6)
PLACES = 6
OFFSETS = np.array(
    [
        [[2, 6, 3, 7, 38, 51], [-2, -6, -1, -5, -38, -51], [4, 8, 5, 0, 25, 1], [-4, -8, -3, -7, -25, 64]],
        [[2, 6, 1, 5, 38, 51], [-2, -6, -3, -7, -38, -51], [4, 8, 3, 7, 25, 64], [-4, -8, -5, 0, -25, -1]],
    ]
)
VMEM = pl.BlockSpec(memory_space=pltpu.VMEM)
SMEM = pl.BlockSpec(memory_space=pltpu.SMEM)
HBM = pl.BlockSpec(memory_space=pltpu.MemorySpace.HBM)


def split(x):
    high = x.astype(jnp.bfloat16)
    return high, (x - high.astype(jnp.float32)).astype(jnp.bfloat16)


def dot3(a, b, dims):
    def one(x, y):
        return lax.dot_general(x, y, (dims, ((), ())), preferred_element_type=jnp.float32)

    return one(a[0], b[0]) + (one(a[0], b[1]) + one(a[1], b[0]))


def pick_kernel(table, ids, columns, counts, omega, slots, old, sems):
    owner, member = ids[0], ids[1]
    count = counts[0]
    parity = lax.rem(owner, 2)
    total = table.shape[1]
    slot_count = columns.shape[1]
    for i in range(total):
        slots[i] = -1

    def match(s, carry):
        offset = lax.rem(columns[0, s] - owner + 128, 128)
        for i in range(total):

            @pl.when(table[parity, i] == offset)
            def _():
                slots[i] = s

        return carry

    lax.fori_loop(0, jnp.minimum(count, slot_count), match, 0)
    for k in range(PLACES):
        slot = slots[member * PLACES + k]

        @pl.when(slot >= 0)
        def _():
            pltpu.make_async_copy(omega.at[slot], old.at[k], sems.at[k]).start()

        @pl.when(slot < 0)
        def _():
            old[k] = jnp.zeros(old.shape[1:], jnp.float32)

    for k in range(PLACES):
        slot = slots[member * PLACES + k]

        @pl.when(slot >= 0)
        def _():
            pltpu.make_async_copy(omega.at[slot], old.at[k], sems.at[k]).wait()


def partial_kernel(own_side, old, full, *refs):
    column, out = refs[:PLACES], refs[PLACES]
    total = jnp.zeros(out.shape, jnp.float32)
    for k in range(PLACES):
        x = column[k][...]
        if k == SIDE_2:
            x = jnp.where(own_side[0] == 1, full[...], x)
        total = total + dot3(split(x), split(old[k]), ((1,), (1,)))
    out[...] = total


def tile_kernel(own_side, ids, half, other, full, *refs):
    column = refs[:PLACES]
    near_1, near_2, side, far_1, far_2, y_out = refs[PLACES:]
    product = half[...] + other[...]
    samples_here = y_out.shape[0]
    turned = split(product.T)
    for k in range(PLACES):
        x = column[k][...]
        if k == SIDE_2:
            x = jnp.where(own_side[0] == 1, full[...], x)
        tile = dot3(turned, split(x), ((1,), (0,)))
        if k in (SIDE_1, SIDE_2):
            side[k - SIDE_1] = tile
        else:
            {NEAR_1: near_1, NEAR_2: near_2, FAR_1: far_1, FAR_2: far_2}[k][...] = tile
    start = pl.multiple_of(ids[1] * samples_here, samples_here)
    y_out[...] = half[pl.ds(start, samples_here), :] + other[pl.ds(start, samples_here), :]


def update_kernel(samples, own_side, old, near_1, near_2, side, far_1, far_2, got_1, got_2, got_far_1, got_far_2, out):
    on_self = own_side[0] == 1
    shape = out.shape[1:]
    unit = lax.broadcasted_iota(jnp.int32, shape, 0) == lax.broadcasted_iota(jnp.int32, shape, 1)
    local = [near_1[...], near_2[...], side[0], side[1], far_1[...], far_2[...]]
    given = [got_1[0], got_2[0], got_1[1], got_2[1], got_far_1[...], got_far_2[...]]
    for k in range(PLACES):
        before = old[k]
        theirs = given[k]
        if k == SIDE_2:
            theirs = jnp.where(on_self, local[k], theirs)
        grad = (local[k] + theirs.T) / (2.0 * samples)
        if k == SIDE_2:
            corner = jnp.logical_and(unit, on_self)
            grad = grad - jnp.where(corner, 1.0 / jnp.where(corner, before, 1.0), 0.0)
        moved = before - step_size * grad
        size = jnp.maximum(jnp.abs(moved) - step_size * penalty, 0.0)
        shrunk = jnp.where(moved < 0.0, -size, size)
        out[k] = jnp.where(corner, moved, shrunk) if k == SIDE_2 else shrunk


def copies(groups, slots, ids, out, sems):
    found = []
    for n, (j, tiles) in enumerate(groups):
        for k in range(PLACES):
            slot = slots[lax.bitwise_xor(ids[1], j) * PLACES + k]
            target = jnp.maximum(slot, 0)
            found.append((slot >= 0, pltpu.make_async_copy(tiles.at[k], out.at[target], sems.at[n * PLACES + k])))
    return found


def place_kernel(which, slots, ids, counts, *refs):
    if which == 0:
        groups, (out, zero, sems, zero_sem) = list(zip((0, 1, 2), refs[:3])), refs[3:]
    else:
        groups, (out, sems) = [(3, refs[0])], refs[2:]
    found = copies(groups, slots, ids, out, sems)
    for condition, copy in found:
        pl.when(condition)(copy.start)
    if which == 0:
        zero[...] = jnp.zeros(zero.shape, jnp.float32)
        slot_count = out.shape[0]
        first = jnp.clip(counts[0], 0, slot_count)

        @pl.loop(first, slot_count)
        def _(s):
            pltpu.make_async_copy(zero, out.at[s], zero_sem).start()
            pltpu.make_async_copy(zero, out.at[s], zero_sem).wait()

    for condition, copy in found:
        pl.when(condition)(copy.wait)


PARAMS = pltpu.CompilerParams(vmem_limit_bytes=8 * 2**20)


def cost(flops, nbytes):
    return pl.CostEstimate(flops=flops, bytes_accessed=nbytes, transcendentals=0)


def step(omega, dosage, columns, counts):
    weights = omega[0]
    own_dosage = dosage[0]
    slot_count, block_size = weights.shape[:2]
    samples_here = own_dosage.shape[0]
    owner = lax.axis_index("blk")
    member = lax.axis_index("team")
    rows = lax.axis_size("blk")
    team = lax.axis_size("team")
    samples = samples_here * team
    f32 = jnp.float32

    def permute(x, target):
        pairs = []
        for b in range(rows):
            for t in range(team):
                b2, t2 = target(b, t)
                pairs.append((b * team + t, (b2 % rows) * team + t2))
        return lax.ppermute(x, AXES, pairs)

    def partner(b, t, k):
        there = b + OFFSETS[b % 2, t, k]
        found = [
            u for u in range(team) if (OFFSETS[there % 2, u, k] + OFFSETS[b % 2, t, k]) % rows == 0
        ]
        return there, found[0]

    def fetch(x, k):
        source = {}
        for b in range(rows):
            for t in range(team):
                b2, t2 = partner(b, t, k)
                source[b2 % rows, t2] = (b, t)
        return permute(x, lambda b, t: source[b, t])

    def beside(b, t):
        return b ^ 1, t

    ids = jnp.stack([owner, member]).astype(jnp.int32)
    own_side = jnp.logical_or(
        jnp.logical_and(owner % 2 == 0, member == 2), jnp.logical_and(owner % 2 == 1, member == 3)
    ).astype(jnp.int32)[None]
    table = jnp.asarray(np.mod(OFFSETS, rows).astype(np.int32).reshape(2, team * PLACES))
    tile_shape = jax.ShapeDtypeStruct((block_size, block_size), f32)
    tiles_shape = jax.ShapeDtypeStruct((PLACES, block_size, block_size), f32)
    tile_bytes = block_size * block_size * 4

    slots, old = pl.pallas_call(
        pick_kernel,
        name="pick",
        out_shape=(jax.ShapeDtypeStruct((team * PLACES,), jnp.int32), tiles_shape),
        in_specs=[SMEM, SMEM, SMEM, SMEM, HBM],
        out_specs=(SMEM, VMEM),
        scratch_shapes=[pltpu.SemaphoreType.DMA((PLACES,))],
        compiler_params=PARAMS,
        cost_estimate=cost(0, 2 * PLACES * tile_bytes),
    )(table, ids, columns, counts, weights)

    full = lax.all_gather(own_dosage, "team", axis=0, tiled=True)
    column = [None] * PLACES
    column[FAR_2] = fetch(full, FAR_2)
    column[NEAR_2] = fetch(full, NEAR_2)
    column[NEAR_1] = fetch(full, NEAR_1)
    column[FAR_1] = fetch(full, FAR_1)
    column[SIDE_2] = permute(column[NEAR_2], beside)
    column[SIDE_1] = permute(column[NEAR_1], beside)

    partial = pl.pallas_call(
        partial_kernel,
        name="partial",
        out_shape=jax.ShapeDtypeStruct((samples, block_size), f32),
        in_specs=[SMEM] + [VMEM] * (2 + PLACES),
        out_specs=VMEM,
        compiler_params=PARAMS,
        cost_estimate=cost(2 * PLACES * samples * block_size**2, 14 * samples * block_size * 4),
    )(own_side, old, full, *column)
    half = partial + permute(partial, lambda b, t: (b, t ^ 1))
    other = permute(half, lambda b, t: (b, t ^ 2))

    near_1, near_2, side, far_1, far_2, y_product = pl.pallas_call(
        tile_kernel,
        name="tiles",
        out_shape=(
            tile_shape,
            tile_shape,
            jax.ShapeDtypeStruct((2, block_size, block_size), f32),
            tile_shape,
            tile_shape,
            jax.ShapeDtypeStruct((samples_here, block_size), f32),
        ),
        in_specs=[SMEM, SMEM] + [VMEM] * (3 + PLACES),
        out_specs=(VMEM,) * 6,
        compiler_params=PARAMS,
        cost_estimate=cost(2 * PLACES * samples * block_size**2, 14 * samples * block_size * 4),
    )(own_side, ids, half, other, full, *column)

    handed = permute(side, beside)

    def back(x, k):
        return permute(x, lambda b, t: partner(b, t, k))

    got_far_2 = back(far_2, FAR_2)
    got_far_1 = back(far_1, FAR_1)
    got_2 = back(jnp.stack([near_2, handed[1]]), NEAR_2)
    got_1 = back(jnp.stack([near_1, handed[0]]), NEAR_1)

    tiles = pl.pallas_call(
        functools.partial(update_kernel, samples),
        name="update",
        out_shape=tiles_shape,
        in_specs=[SMEM] + [VMEM] * 10,
        out_specs=VMEM,
        compiler_params=PARAMS,
        cost_estimate=cost(0, 4 * PLACES * tile_bytes),
    )(own_side, old, near_1, near_2, side, far_1, far_2, got_1, got_2, got_far_1, got_far_2)

    across = permute(tiles, lambda b, t: (b, t ^ 2))
    mate = permute(tiles, lambda b, t: (b, t ^ 1))
    last = permute(across, lambda b, t: (b, t ^ 1))
    out_shape = jax.ShapeDtypeStruct((slot_count, block_size, block_size), f32)
    new_omega = pl.pallas_call(
        functools.partial(place_kernel, 0),
        name="place_1",
        out_shape=out_shape,
        in_specs=[SMEM] * 3 + [VMEM] * 3,
        out_specs=HBM,
        scratch_shapes=[
            pltpu.VMEM((block_size, block_size), f32),
            pltpu.SemaphoreType.DMA((3 * PLACES,)),
            pltpu.SemaphoreType.DMA,
        ],
        compiler_params=PARAMS,
        cost_estimate=cost(0, 6 * PLACES * tile_bytes),
    )(slots, ids, counts, tiles, mate, across)
    new_omega = pl.pallas_call(
        functools.partial(place_kernel, 1),
        name="place_2",
        out_shape=out_shape,
        in_specs=[SMEM] * 3 + [VMEM, HBM],
        out_specs=HBM,
        input_output_aliases={4: 0},
        scratch_shapes=[pltpu.SemaphoreType.DMA((PLACES,))],
        compiler_params=PARAMS,
        cost_estimate=cost(0, 2 * PLACES * tile_bytes),
    )(slots, ids, counts, last, new_omega)
    return (new_omega[None], y_product[None])


def solution(mesh):
    return jax.shard_map(
        step,
        mesh=mesh,
        in_specs=(P("blk", None, None, None), P("blk", "team", None), P("blk", None), P("blk")),
        out_specs=(P("blk", None, None, None), P("blk", "team", None)),
        check_vma=False,
    )
```

profile of v0, /device:TPU:1, one launch (start us, length us, event | category | flops | bytes accessed | tf_op | source)
XLA Modules:
  0.0 128.9 jit_solution(12507409656083837449)
XLA Ops:
  0.6 13.8 %all-gather = f32[1,256,128]{2,1,0:T(8,128)S(1)} all-gather(f32[1,64,128]{2,1,0:T(8,128)} %param.6), channel_id=2, replica_groups=mesh['blk'=128,'team'=4] {'team'}, dimensions={1}, use_global_device_ids=true | all-gather | bytes 163840 | tf_op jit(solution)/shard_map/all_gather | solution.py:229
  14.4 9.2 %collective-permute-start.1 = (f32[256,128]{1,0:T(8,128)S(1)}, f32[256,128]{1,0:T(8,128)S(1)}, u32[]{:S(2)}, u32[]{:S(2)}) collective-permute-start(f32[256,128]{1,0:T(8,128)S(1)} %bitcast.10), channel_id=1, source_target_pairs={{0,25},{1,488},{2,35},{3,482},{4,29},{5,492},{6,39},{7,486},{8,33}... | collective-permute-start | bytes 393224 | tf_op jit(solution)/shard_map/ppermute | solution.py:189
  23.6 1.9 %collective-permute-start = (f32[256,128]{1,0:T(8,128)S(1)}, f32[256,128]{1,0:T(8,128)S(1)}, u32[]{:S(2)}, u32[]{:S(2)}) collective-permute-start(f32[256,128]{1,0:T(8,128)S(1)} %bitcast.11), channel_id=1, source_target_pairs={{0,9},{1,504},{2,19},{3,498},{4,13},{5,508},{6,23},{7,502},{8,17},... | collective-permute-start | bytes 393224 | tf_op jit(solution)/shard_map/ppermute | solution.py:189
  25.5 7.4 %collective-permute-start.5 = (f32[256,128]{1,0:T(8,128)S(1)}, f32[256,128]{1,0:T(8,128)S(1)}, u32[]{:S(2)}, u32[]{:S(2)}) collective-permute-start(f32[256,128]{1,0:T(8,128)S(1)} %bitcast.12), channel_id=1, source_target_pairs={{0,205},{1,308},{2,7},{3,259},{4,209},{5,312},{6,262},{7,2},{8,213... | collective-permute-start | bytes 393224 | tf_op jit(solution)/shard_map/ppermute | solution.py:189
  33.0 6.0 %collective-permute-start.4 = (f32[256,128]{1,0:T(8,128)S(1)}, f32[256,128]{1,0:T(8,128)S(1)}, u32[]{:S(2)}, u32[]{:S(2)}) collective-permute-start(f32[256,128]{1,0:T(8,128)S(1)} %bitcast.13), channel_id=1, source_target_pairs={{0,153},{1,360},{2,103},{3,414},{4,157},{5,364},{6,107},{7,418},{8... | collective-permute-start | bytes 393224 | tf_op jit(solution)/shard_map/ppermute | solution.py:189
  38.9 1.9 %collective-permute-start.3 = (f32[256,128]{1,0:T(8,128)S(1)}, f32[256,128]{1,0:T(8,128)S(1)}, u32[]{:S(2)}, u32[]{:S(2)}) collective-permute-start(f32[256,128]{1,0:T(8,128)S(1)} %collective-permute-done.1.refs_1_), channel_id=1, source_target_pairs={{0,4},{1,5},{2,6},{3,7},{4,0},{5,1},{6,2},{7,3},{8,12},{9,13},{10,... | collective-permute-start | bytes 393224 | tf_op jit(solution)/shard_map/ppermute | solution.py:189
  40.9 3.4 %collective-permute-start.2 = (f32[256,128]{1,0:T(8,128)S(1)}, f32[256,128]{1,0:T(8,128)S(1)}, u32[]{:S(2)}, u32[]{:S(2)}) collective-permute-start(f32[256,128]{1,0:T(8,128)S(1)} %collective-permute-done.refs_0_), channel_id=1, source_target_pairs={{0,4},{1,5},{2,6},{3,7},{4,0},{5,1},{6,2},{7,3},{8,12},{9,13},{10,... | collective-permute-start | bytes 393224 | tf_op jit(solution)/shard_map/ppermute | solution.py:189
  45.0 1.4 %copy-done = f32[1,24,128,128]{3,2,1,0:T(8,128)S(1)} copy-done((f32[1,24,128,128]{3,2,1,0:T(8,128)S(1)}, f32[1,24,128,128]{3,2,1,0:T(8,128)}, u32[]{:S(2)}) %copy-start) | copy-done | bytes 1572888
  46.4 0.7 copy-done.1
  47.1 0.7 copy-done.2
  47.7 1.8 %pick.1 = (s32[24]{0:T(128)S(1)}, f32[6,128,128]{2,1,0:T(8,128)S(1)}) custom-call(s32[2,24]{1,0:T(2,128)S(1)} %copy-done.1, s32[2]{0:T(128)S(1)} %pad_add_fusion.ids, s32[1,24]{1,0:T(1,128)S(1)} %copy-done.2, s32[1]{0:T(128)S(6)} %copy.9.counts, f32[24,128,128]{2,1,0:T(8,128)S(1)} %bitcast.9), custom_call_target="tpu_custom_call" | custom-call | bytes 786432 | tf_op jit(solution)/shard_map/pick/pallas_call | solution.py:218
  49.6 1.1 collective-permute-done.5.refs_5_
  50.6 0.5 partial.1
  51.1 5.4 %collective-permute-start.6 = (f32[256,128]{1,0:T(8,128)S(1)}, f32[256,128]{1,0:T(8,128)S(1)}, u32[]{:S(2)}, u32[]{:S(2)}) collective-permute-start(f32[256,128]{1,0:T(8,128)S(1)} %partial.1), channel_id=1, source_target_pairs={{0,1},{1,0},{2,3},{3,2},{4,5},{5,4},{6,7},{7,6},{8,9},{9,8},{10,11... | collective-permute-start | bytes 393224 | tf_op jit(solution)/shard_map/ppermute | solution.py:189
  56.6 1.0 collective-permute-done.6
  57.5 1.9 %collective-permute-start.7 = (f32[256,128]{1,0:T(8,128)S(1)}, f32[256,128]{1,0:T(8,128)S(1)}, u32[]{:S(2)}, u32[]{:S(2)}) collective-permute-start(f32[256,128]{1,0:T(8,128)S(1)} %add.9.half), channel_id=1, source_target_pairs={{0,2},{1,3},{2,0},{3,1},{4,6},{5,7},{6,4},{7,5},{8,10},{9,11},{10,... | collective-permute-start | bytes 393224 | tf_op jit(solution)/shard_map/ppermute | solution.py:189
  59.5 6.2 %collective-permute-done.7.other = f32[256,128]{1,0:T(8,128)S(1)} collective-permute-done((f32[256,128]{1,0:T(8,128)S(1)}, f32[256,128]{1,0:T(8,128)S(1)}, u32[]{:S(2)}, u32[]{:S(2)}) %collective-permute-start.7) | collective-permute-done | bytes 131104 | tf_op jit(solution)/shard_map/ppermute | solution.py:189
  65.6 1.6 %tiles.1 = (f32[128,128]{1,0:T(8,128)S(1)}, f32[128,128]{1,0:T(8,128)S(1)}, f32[2,128,128]{2,1,0:T(8,128)S(1)}, f32[128,128]{1,0:T(8,128)S(1)}, f32[128,128]{1,0:T(8,128)S(1)}, /*index=5*/f32[64,128]{1,0:T(8,128)}) custom-call(s32[1]{0:T(128)} %bitcast.3.own_side, s32[2]{0:T(128)S(1)} %pad_add_fusion.ids, f32[256,128]{1,0:T(8,128)S(1)} %add.9.half, ...), custom_call_target="tpu_custom_call" | custom-call | flops 50331648 | bytes 1835008 | tf_op jit(solution)/shard_map/tiles/pallas_call | solution.py:250
  67.3 2.0 %collective-permute-start.8 = (f32[2,128,128]{2,1,0:T(8,128)S(1)}, f32[2,128,128]{2,1,0:T(8,128)S(1)}, u32[]{:S(2)}, u32[]{:S(2)}) collective-permute-start(f32[2,128,128]{2,1,0:T(8,128)S(1)} %get-tuple-element.14.side), channel_id=1, source_target_pairs={{0,4},{1,5},{2,6},{3,7},{4,0},{5,1},{6,2},{7,3},{8,12},{9,13},{10,... | collective-permute-start | bytes 393224 | tf_op jit(solution)/shard_map/ppermute | solution.py:189
  69.2 3.7 %collective-permute-done.8 = f32[2,128,128]{2,1,0:T(8,128)S(1)} collective-permute-done((f32[2,128,128]{2,1,0:T(8,128)S(1)}, f32[2,128,128]{2,1,0:T(8,128)S(1)}, u32[]{:S(2)}, u32[]{:S(2)}) %collective-permute-start.8) | collective-permute-done | bytes 131104 | tf_op jit(solution)/shard_map/ppermute | solution.py:189
  73.0 6.8 %collective-permute-start.9 = (f32[2,128,128]{2,1,0:T(8,128)S(1)}, f32[2,128,128]{2,1,0:T(8,128)S(1)}, u32[]{:S(2)}, u32[]{:S(2)}) collective-permute-start(f32[2,128,128]{2,1,0:T(8,128)S(1)} %pad_maximum_fusion), channel_id=1, source_target_pairs={{0,9},{1,504},{2,19},{3,498},{4,13},{5,508},{6,23},{7,502},{8,17},... | collective-permute-start | bytes 393224 | tf_op jit(solution)/shard_map/ppermute | solution.py:189
  79.9 1.9 %collective-permute-start.10 = (f32[2,128,128]{2,1,0:T(8,128)S(1)}, f32[2,128,128]{2,1,0:T(8,128)S(1)}, u32[]{:S(2)}, u32[]{:S(2)}) collective-permute-start(f32[2,128,128]{2,1,0:T(8,128)S(1)} %pad_maximum_fusion.1), channel_id=1, source_target_pairs={{0,25},{1,488},{2,35},{3,482},{4,29},{5,492},{6,39},{7,486},{8,33}... | collective-permute-start | bytes 393224 | tf_op jit(solution)/shard_map/ppermute | solution.py:189
  81.8 7.5 %collective-permute-start.11 = (f32[128,128]{1,0:T(8,128)S(1)}, f32[128,128]{1,0:T(8,128)S(1)}, u32[]{:S(2)}, u32[]{:S(2)}) collective-permute-start(f32[128,128]{1,0:T(8,128)S(1)} %get-tuple-element.15.far_1), channel_id=1, source_target_pairs={{0,153},{1,360},{2,103},{3,414},{4,157},{5,364},{6,107},{7,418},{8... | collective-permute-start | bytes 196616 | tf_op jit(solution)/shard_map/ppermute | solution.py:189
  89.3 5.6 %collective-permute-start.12 = (f32[128,128]{1,0:T(8,128)S(1)}, f32[128,128]{1,0:T(8,128)S(1)}, u32[]{:S(2)}, u32[]{:S(2)}) collective-permute-start(f32[128,128]{1,0:T(8,128)S(1)} %get-tuple-element.16.far_2), channel_id=1, source_target_pairs={{0,205},{1,308},{2,7},{3,259},{4,209},{5,312},{6,262},{7,2},{8,213... | collective-permute-start | bytes 196616 | tf_op jit(solution)/shard_map/ppermute | solution.py:189
  94.9 10.2 %collective-permute-done.12.got_far_2 = f32[128,128]{1,0:T(8,128)S(1)} collective-permute-done((f32[128,128]{1,0:T(8,128)S(1)}, f32[128,128]{1,0:T(8,128)S(1)}, u32[]{:S(2)}, u32[]{:S(2)}) %collective-permute-start.12) | collective-permute-done | bytes 65568 | tf_op jit(solution)/shard_map/ppermute | solution.py:189
  105.2 0.2 update.1.refs_0_
  105.4 1.9 %collective-permute-start.13 = (f32[6,128,128]{2,1,0:T(8,128)S(1)}, f32[6,128,128]{2,1,0:T(8,128)S(1)}, u32[]{:S(2)}, u32[]{:S(2)}) collective-permute-start(f32[6,128,128]{2,1,0:T(8,128)S(1)} %update.1.refs_0_), channel_id=1, source_target_pairs={{0,2},{1,3},{2,0},{3,1},{4,6},{5,7},{6,4},{7,5},{8,10},{9,11},{10,... | collective-permute-start | bytes 1179656 | tf_op jit(solution)/shard_map/ppermute | solution.py:189
  107.3 1.9 %collective-permute-start.15 = (f32[6,128,128]{2,1,0:T(8,128)S(1)}, f32[6,128,128]{2,1,0:T(8,128)S(1)}, u32[]{:S(2)}, u32[]{:S(2)}) collective-permute-start(f32[6,128,128]{2,1,0:T(8,128)S(1)} %update.1.refs_0_), channel_id=1, source_target_pairs={{0,1},{1,0},{2,3},{3,2},{4,5},{5,4},{6,7},{7,6},{8,9},{9,8},{10,11... | collective-permute-start | bytes 1179656 | tf_op jit(solution)/shard_map/ppermute | solution.py:189
  109.2 6.2 %collective-permute-done.13.refs_2_ = f32[6,128,128]{2,1,0:T(8,128)S(1)} collective-permute-done((f32[6,128,128]{2,1,0:T(8,128)S(1)}, f32[6,128,128]{2,1,0:T(8,128)S(1)}, u32[]{:S(2)}, u32[]{:S(2)}) %collective-permute-start.13) | collective-permute-done | bytes 393248 | tf_op jit(solution)/shard_map/ppermute | solution.py:189
  115.4 1.9 %collective-permute-start.14 = (f32[6,128,128]{2,1,0:T(8,128)S(1)}, f32[6,128,128]{2,1,0:T(8,128)S(1)}, u32[]{:S(2)}, u32[]{:S(2)}) collective-permute-start(f32[6,128,128]{2,1,0:T(8,128)S(1)} %collective-permute-done.13.refs_2_), channel_id=1, source_target_pairs={{0,1},{1,0},{2,3},{3,2},{4,5},{5,4},{6,7},{7,6},{8,9},{9,8},{10,11... | collective-permute-start | bytes 1179656 | tf_op jit(solution)/shard_map/ppermute | solution.py:189
  117.3 10.3 %place_1.1.refs_1_ = f32[24,128,128]{2,1,0:T(8,128)} custom-call(s32[24]{0:T(128)S(1)} %get-tuple-element.10.slots, s32[2]{0:T(128)S(1)} %pad_add_fusion.ids, s32[1]{0:T(128)S(6)} %copy.9.counts, f32[6,128,128]{2,1,0:T(8,128)S(1)} %update.1.refs_0_, f32[6,128,128]{2,1,0:T(8,128)S(1)} %collective-permute-done.15.refs_1_, ...), custom_call_target="tpu_custom_call" | custom-call | bytes 2359296 | tf_op jit(solution)/shard_map/place_1/pallas_call | solution.py:291
  127.7 1.3 place_2.1
  (18 shorter events, 0.2 us)
Async XLA Ops:
  14.4 24.5 %collective-permute-start.1 = (f32[256,128]{1,0:T(8,128)S(1)}, f32[256,128]{1,0:T(8,128)S(1)}, u32[]{:S(2)}, u32[]{:S(2)}) collective-permute-start(f32[256,128]{1,0:T(8,128)S(1)} %bitcast.10), channel_id=1, source_target_pairs={{0,25},{1,488},{2,35},{3,482},{4,29},{5,492},{6,39},{7,486},{8,33}... | collective-permute-start | bytes 393224 | tf_op jit(solution)/shard_map/ppermute | solution.py:189
  23.6 17.3 %collective-permute-start = (f32[256,128]{1,0:T(8,128)S(1)}, f32[256,128]{1,0:T(8,128)S(1)}, u32[]{:S(2)}, u32[]{:S(2)}) collective-permute-start(f32[256,128]{1,0:T(8,128)S(1)} %bitcast.11), channel_id=1, source_target_pairs={{0,9},{1,504},{2,19},{3,498},{4,13},{5,508},{6,23},{7,502},{8,17},... | collective-permute-start | bytes 393224 | tf_op jit(solution)/shard_map/ppermute | solution.py:189
  25.5 25.1 %collective-permute-start.5 = (f32[256,128]{1,0:T(8,128)S(1)}, f32[256,128]{1,0:T(8,128)S(1)}, u32[]{:S(2)}, u32[]{:S(2)}) collective-permute-start(f32[256,128]{1,0:T(8,128)S(1)} %bitcast.12), channel_id=1, source_target_pairs={{0,205},{1,308},{2,7},{3,259},{4,209},{5,312},{6,262},{7,2},{8,213... | collective-permute-start | bytes 393224 | tf_op jit(solution)/shard_map/ppermute | solution.py:189
  33.0 17.7 %collective-permute-start.4 = (f32[256,128]{1,0:T(8,128)S(1)}, f32[256,128]{1,0:T(8,128)S(1)}, u32[]{:S(2)}, u32[]{:S(2)}) collective-permute-start(f32[256,128]{1,0:T(8,128)S(1)} %bitcast.13), channel_id=1, source_target_pairs={{0,153},{1,360},{2,103},{3,414},{4,157},{5,364},{6,107},{7,418},{8... | collective-permute-start | bytes 393224 | tf_op jit(solution)/shard_map/ppermute | solution.py:189
  38.9 11.7 %collective-permute-start.3 = (f32[256,128]{1,0:T(8,128)S(1)}, f32[256,128]{1,0:T(8,128)S(1)}, u32[]{:S(2)}, u32[]{:S(2)}) collective-permute-start(f32[256,128]{1,0:T(8,128)S(1)} %collective-permute-done.1.refs_1_), channel_id=1, source_target_pairs={{0,4},{1,5},{2,6},{3,7},{4,0},{5,1},{6,2},{7,3},{8,12},{9,13},{10,... | collective-permute-start | bytes 393224 | tf_op jit(solution)/shard_map/ppermute | solution.py:189
  40.9 9.8 %collective-permute-start.2 = (f32[256,128]{1,0:T(8,128)S(1)}, f32[256,128]{1,0:T(8,128)S(1)}, u32[]{:S(2)}, u32[]{:S(2)}) collective-permute-start(f32[256,128]{1,0:T(8,128)S(1)} %collective-permute-done.refs_0_), channel_id=1, source_target_pairs={{0,4},{1,5},{2,6},{3,7},{4,0},{5,1},{6,2},{7,3},{8,12},{9,13},{10,... | collective-permute-start | bytes 393224 | tf_op jit(solution)/shard_map/ppermute | solution.py:189
  45.0 1.4 %copy-start = (f32[1,24,128,128]{3,2,1,0:T(8,128)S(1)}, f32[1,24,128,128]{3,2,1,0:T(8,128)}, u32[]{:S(2)}) copy-start(f32[1,24,128,128]{3,2,1,0:T(8,128)} %param.5) | copy-start | bytes 4718596
  46.4 0.7 copy-start.1
  47.1 0.7 copy-start.2
  51.1 6.4 %collective-permute-start.6 = (f32[256,128]{1,0:T(8,128)S(1)}, f32[256,128]{1,0:T(8,128)S(1)}, u32[]{:S(2)}, u32[]{:S(2)}) collective-permute-start(f32[256,128]{1,0:T(8,128)S(1)} %partial.1), channel_id=1, source_target_pairs={{0,1},{1,0},{2,3},{3,2},{4,5},{5,4},{6,7},{7,6},{8,9},{9,8},{10,11... | collective-permute-start | bytes 393224 | tf_op jit(solution)/shard_map/ppermute | solution.py:189
  57.5 8.1 %collective-permute-start.7 = (f32[256,128]{1,0:T(8,128)S(1)}, f32[256,128]{1,0:T(8,128)S(1)}, u32[]{:S(2)}, u32[]{:S(2)}) collective-permute-start(f32[256,128]{1,0:T(8,128)S(1)} %add.9.half), channel_id=1, source_target_pairs={{0,2},{1,3},{2,0},{3,1},{4,6},{5,7},{6,4},{7,5},{8,10},{9,11},{10,... | collective-permute-start | bytes 393224 | tf_op jit(solution)/shard_map/ppermute | solution.py:189
  67.3 5.7 %collective-permute-start.8 = (f32[2,128,128]{2,1,0:T(8,128)S(1)}, f32[2,128,128]{2,1,0:T(8,128)S(1)}, u32[]{:S(2)}, u32[]{:S(2)}) collective-permute-start(f32[2,128,128]{2,1,0:T(8,128)S(1)} %get-tuple-element.14.side), channel_id=1, source_target_pairs={{0,4},{1,5},{2,6},{3,7},{4,0},{5,1},{6,2},{7,3},{8,12},{9,13},{10,... | collective-permute-start | bytes 393224 | tf_op jit(solution)/shard_map/ppermute | solution.py:189
  73.0 32.2 %collective-permute-start.9 = (f32[2,128,128]{2,1,0:T(8,128)S(1)}, f32[2,128,128]{2,1,0:T(8,128)S(1)}, u32[]{:S(2)}, u32[]{:S(2)}) collective-permute-start(f32[2,128,128]{2,1,0:T(8,128)S(1)} %pad_maximum_fusion), channel_id=1, source_target_pairs={{0,9},{1,504},{2,19},{3,498},{4,13},{5,508},{6,23},{7,502},{8,17},... | collective-permute-start | bytes 393224 | tf_op jit(solution)/shard_map/ppermute | solution.py:189
  79.9 25.3 %collective-permute-start.10 = (f32[2,128,128]{2,1,0:T(8,128)S(1)}, f32[2,128,128]{2,1,0:T(8,128)S(1)}, u32[]{:S(2)}, u32[]{:S(2)}) collective-permute-start(f32[2,128,128]{2,1,0:T(8,128)S(1)} %pad_maximum_fusion.1), channel_id=1, source_target_pairs={{0,25},{1,488},{2,35},{3,482},{4,29},{5,492},{6,39},{7,486},{8,33}... | collective-permute-start | bytes 393224 | tf_op jit(solution)/shard_map/ppermute | solution.py:189
  81.8 13.1 %collective-permute-start.11 = (f32[128,128]{1,0:T(8,128)S(1)}, f32[128,128]{1,0:T(8,128)S(1)}, u32[]{:S(2)}, u32[]{:S(2)}) collective-permute-start(f32[128,128]{1,0:T(8,128)S(1)} %get-tuple-element.15.far_1), channel_id=1, source_target_pairs={{0,153},{1,360},{2,103},{3,414},{4,157},{5,364},{6,107},{7,418},{8... | collective-permute-start | bytes 196616 | tf_op jit(solution)/shard_map/ppermute | solution.py:189
  89.3 15.9 %collective-permute-start.12 = (f32[128,128]{1,0:T(8,128)S(1)}, f32[128,128]{1,0:T(8,128)S(1)}, u32[]{:S(2)}, u32[]{:S(2)}) collective-permute-start(f32[128,128]{1,0:T(8,128)S(1)} %get-tuple-element.16.far_2), channel_id=1, source_target_pairs={{0,205},{1,308},{2,7},{3,259},{4,209},{5,312},{6,262},{7,2},{8,213... | collective-permute-start | bytes 196616 | tf_op jit(solution)/shard_map/ppermute | solution.py:189
  105.4 10.0 %collective-permute-start.13 = (f32[6,128,128]{2,1,0:T(8,128)S(1)}, f32[6,128,128]{2,1,0:T(8,128)S(1)}, u32[]{:S(2)}, u32[]{:S(2)}) collective-permute-start(f32[6,128,128]{2,1,0:T(8,128)S(1)} %update.1.refs_0_), channel_id=1, source_target_pairs={{0,2},{1,3},{2,0},{3,1},{4,6},{5,7},{6,4},{7,5},{8,10},{9,11},{10,... | collective-permute-start | bytes 1179656 | tf_op jit(solution)/shard_map/ppermute | solution.py:189
  107.3 10.0 %collective-permute-start.15 = (f32[6,128,128]{2,1,0:T(8,128)S(1)}, f32[6,128,128]{2,1,0:T(8,128)S(1)}, u32[]{:S(2)}, u32[]{:S(2)}) collective-permute-start(f32[6,128,128]{2,1,0:T(8,128)S(1)} %update.1.refs_0_), channel_id=1, source_target_pairs={{0,1},{1,0},{2,3},{3,2},{4,5},{5,4},{6,7},{7,6},{8,9},{9,8},{10,11... | collective-permute-start | bytes 1179656 | tf_op jit(solution)/shard_map/ppermute | solution.py:189
  115.4 12.2 %collective-permute-start.14 = (f32[6,128,128]{2,1,0:T(8,128)S(1)}, f32[6,128,128]{2,1,0:T(8,128)S(1)}, u32[]{:S(2)}, u32[]{:S(2)}) collective-permute-start(f32[6,128,128]{2,1,0:T(8,128)S(1)} %collective-permute-done.13.refs_2_), channel_id=1, source_target_pairs={{0,1},{1,0},{2,3},{3,2},{4,5},{5,4},{6,7},{7,6},{8,9},{9,8},{10,11... | collective-permute-start | bytes 1179656 | tf_op jit(solution)/shard_map/ppermute | solution.py:189
where the time goes:
time: 130 us; the launch traced here: 129 us
  starting transfers between devices  66.7 us (51%)
  waiting for transfers between devices  28.3 us (22%)
  Pallas kernels  15.7 us (12%)
  blocking collectives  13.8 us (11%)
  local copies, waits for them, and re-layouts  2.75 us (2%)
  between operations  1.53 us (1%)
    ppermute x16, starting transfers between devices, permute(): return lax.ppermute(x, AXES, pairs)  66.7 us
    ppermute x16, waiting for transfers between devices, permute(): return lax.ppermute(x, AXES, pairs)  28.3 us
    all_gather x1, blocking collectives, step(): full = lax.all_gather(own_dosage, 'team', axis=0, tiled=True)  13.8 us
    pallas_call x1, Pallas kernels, step(): pl.pallas_call(functools.partial(place_kernel, 0), name='place_1', out_sh...  10.3 us
    unnamed x6, local copies, waits for them, and re-layouts  2.74 us
  transfers between devices with their start and end apart: 16, of which 6 were waited for; matrix products, arithmetic and copies ran while one was open for 0% of the time, Pallas kernels for 9%

commit v1 on v0

--- a/solution.py
+++ b/solution.py
@@ -18,8 +18,8 @@
 PLACES = 6
 OFFSETS = np.array(
     [
-        [[2, 6, 3, 7, 38, 51], [-2, -6, -1, -5, -38, -51], [4, 8, 5, 0, 25, 1], [-4, -8, -3, -7, -25, 64]],
-        [[2, 6, 1, 5, 38, 51], [-2, -6, -3, -7, -38, -51], [4, 8, 3, 7, 25, 64], [-4, -8, -5, 0, -25, -1]],
+        [[2, 4, 3, 5, 38, 51], [-2, -4, -1, -3, -38, -51], [6, 8, 7, 0, 25, 1], [-6, -8, -5, -7, -25, 64]],
+        [[2, 4, 1, 3, 38, 51], [-2, -4, -3, -5, -38, -51], [6, 8, 5, 7, 25, 64], [-6, -8, -7, 0, -25, -1]],
     ]
 )
 VMEM = pl.BlockSpec(memory_space=pltpu.VMEM)
@@ -108,54 +108,64 @@
     y_out[...] = half[pl.ds(start, samples_here), :] + other[pl.ds(start, samples_here), :]
 
 
-def update_kernel(samples, own_side, old, near_1, near_2, side, far_1, far_2, got_1, got_2, got_far_1, got_far_2, out):
+def update(before, ours, theirs, samples, corner=None):
+    grad = (ours + theirs.T) / (2.0 * samples)
+    if corner is not None:
+        grad = grad - jnp.where(corner, 1.0 / jnp.where(corner, before, 1.0), 0.0)
+    moved = before - step_size * grad
+    size = jnp.maximum(jnp.abs(moved) - step_size * penalty, 0.0)
+    shrunk = jnp.where(moved < 0.0, -size, size)
+    return shrunk if corner is None else jnp.where(corner, moved, shrunk)
+
+
+def update_far_kernel(samples, old, far_1, far_2, got_1, got_2, out):
+    out[0] = update(old[FAR_1], far_1[...], got_1[...], samples)
+    out[1] = update(old[FAR_2], far_2[...], got_2[...], samples)
+
+
+def update_near_kernel(samples, own_side, old, near_1, near_2, side, got_1, got_2, out):
     on_self = own_side[0] == 1
     shape = out.shape[1:]
     unit = lax.broadcasted_iota(jnp.int32, shape, 0) == lax.broadcasted_iota(jnp.int32, shape, 1)
-    local = [near_1[...], near_2[...], side[0], side[1], far_1[...], far_2[...]]
-    given = [got_1[0], got_2[0], got_1[1], got_2[1], got_far_1[...], got_far_2[...]]
-    for k in range(PLACES):
-        before = old[k]
-        theirs = given[k]
-        if k == SIDE_2:
-            theirs = jnp.where(on_self, local[k], theirs)
-        grad = (local[k] + theirs.T) / (2.0 * samples)
-        if k == SIDE_2:
-            corner = jnp.logical_and(unit, on_self)
-            grad = grad - jnp.where(corner, 1.0 / jnp.where(corner, before, 1.0), 0.0)
-        moved = before - step_size * grad
-        size = jnp.maximum(jnp.abs(moved) - step_size * penalty, 0.0)
-        shrunk = jnp.where(moved < 0.0, -size, size)
-        out[k] = jnp.where(corner, moved, shrunk) if k == SIDE_2 else shrunk
-
-
-def copies(groups, slots, ids, out, sems):
+    out[NEAR_1] = update(old[NEAR_1], near_1[...], got_1[0], samples)
+    out[NEAR_2] = update(old[NEAR_2], near_2[...], got_2[0], samples)
+    out[SIDE_1] = update(old[SIDE_1], side[0], got_1[1], samples)
+    theirs = jnp.where(on_self, side[1], got_2[1])
+    out[SIDE_2] = update(old[SIDE_2], side[1], theirs, samples, jnp.logical_and(unit, on_self))
+
+
+NEAR_PLACES = (NEAR_1, NEAR_2, SIDE_1, SIDE_2)
+FAR_PLACES = (FAR_1, FAR_2)
+
+
+def place_kernel(groups, places, fill, slots, ids, counts, *refs):
+    n = len(groups)
+    if fill:
+        out, zero, sems, zero_sems = refs[n:]
+    else:
+        out, sems = refs[n + 1 :]
     found = []
-    for n, (j, tiles) in enumerate(groups):
-        for k in range(PLACES):
+    for g, j in enumerate(groups):
+        for i, k in enumerate(places):
             slot = slots[lax.bitwise_xor(ids[1], j) * PLACES + k]
-            target = jnp.maximum(slot, 0)
-            found.append((slot >= 0, pltpu.make_async_copy(tiles.at[k], out.at[target], sems.at[n * PLACES + k])))
-    return found
-
-
-def place_kernel(which, slots, ids, counts, *refs):
-    if which == 0:
-        groups, (out, zero, sems, zero_sem) = list(zip((0, 1, 2), refs[:3])), refs[3:]
-    else:
-        groups, (out, sems) = [(3, refs[0])], refs[2:]
-    found = copies(groups, slots, ids, out, sems)
+            copy = pltpu.make_async_copy(
+                refs[g].at[i], out.at[jnp.maximum(slot, 0)], sems.at[g * len(places) + i]
+            )
+            found.append((slot >= 0, copy))
     for condition, copy in found:
         pl.when(condition)(copy.start)
-    if which == 0:
+    if fill:
         zero[...] = jnp.zeros(zero.shape, jnp.float32)
         slot_count = out.shape[0]
         first = jnp.clip(counts[0], 0, slot_count)
 
         @pl.loop(first, slot_count)
         def _(s):
-            pltpu.make_async_copy(zero, out.at[s], zero_sem).start()
-            pltpu.make_async_copy(zero, out.at[s], zero_sem).wait()
+            pltpu.make_async_copy(zero, out.at[s], zero_sems.at[s]).start()
+
+        @pl.loop(first, slot_count)
+        def _(s):
+            pltpu.make_async_copy(zero, out.at[s], zero_sems.at[s]).wait()
 
     for condition, copy in found:
         pl.when(condition)(copy.wait)
@@ -274,45 +284,61 @@
     got_2 = back(jnp.stack([near_2, handed[1]]), NEAR_2)
     got_1 = back(jnp.stack([near_1, handed[0]]), NEAR_1)
 
-    tiles = pl.pallas_call(
-        functools.partial(update_kernel, samples),
-        name="update",
-        out_shape=tiles_shape,
-        in_specs=[SMEM] + [VMEM] * 10,
-        out_specs=VMEM,
-        compiler_params=PARAMS,
-        cost_estimate=cost(0, 4 * PLACES * tile_bytes),
-    )(own_side, old, near_1, near_2, side, far_1, far_2, got_1, got_2, got_far_1, got_far_2)
-
-    across = permute(tiles, lambda b, t: (b, t ^ 2))
-    mate = permute(tiles, lambda b, t: (b, t ^ 1))
-    last = permute(across, lambda b, t: (b, t ^ 1))
-    out_shape = jax.ShapeDtypeStruct((slot_count, block_size, block_size), f32)
-    new_omega = pl.pallas_call(
-        functools.partial(place_kernel, 0),
-        name="place_1",
-        out_shape=out_shape,
-        in_specs=[SMEM] * 3 + [VMEM] * 3,
-        out_specs=HBM,
-        scratch_shapes=[
-            pltpu.VMEM((block_size, block_size), f32),
-            pltpu.SemaphoreType.DMA((3 * PLACES,)),
-            pltpu.SemaphoreType.DMA,
-        ],
-        compiler_params=PARAMS,
-        cost_estimate=cost(0, 6 * PLACES * tile_bytes),
-    )(slots, ids, counts, tiles, mate, across)
-    new_omega = pl.pallas_call(
-        functools.partial(place_kernel, 1),
-        name="place_2",
-        out_shape=out_shape,
-        in_specs=[SMEM] * 3 + [VMEM, HBM],
-        out_specs=HBM,
-        input_output_aliases={4: 0},
-        scratch_shapes=[pltpu.SemaphoreType.DMA((PLACES,))],
-        compiler_params=PARAMS,
-        cost_estimate=cost(0, 2 * PLACES * tile_bytes),
-    )(slots, ids, counts, last, new_omega)
+    def kernel(function, out_shape, in_specs, nbytes):
+        return pl.pallas_call(
+            function,
+            out_shape=out_shape,
+            in_specs=in_specs,
+            out_specs=VMEM,
+            compiler_params=PARAMS,
+            cost_estimate=cost(0, nbytes),
+        )
+
+    def tiles_of(count):
+        return jax.ShapeDtypeStruct((count, block_size, block_size), f32)
+
+    far_tiles = kernel(
+        functools.partial(update_far_kernel, samples), tiles_of(2), [VMEM] * 5, 8 * tile_bytes
+    )(old, far_1, far_2, got_far_1, got_far_2)
+    near_tiles = kernel(
+        functools.partial(update_near_kernel, samples), tiles_of(4), [SMEM] + [VMEM] * 6, 16 * tile_bytes
+    )(own_side, old, near_1, near_2, side, got_1, got_2)
+
+    def chip(b, t):
+        return b, t ^ 2
+
+    def core(b, t):
+        return b, t ^ 1
+
+    far_across = permute(far_tiles, chip)
+    far_mate = permute(far_tiles, core)
+    near_across = permute(near_tiles, chip)
+    near_mate = permute(near_tiles, core)
+    far_last = permute(far_across, core)
+    near_last = permute(near_across, core)
+
+    def place(groups, places, tiles, into):
+        fill = into is None
+        n = len(groups)
+        sems = [pltpu.SemaphoreType.DMA((n * len(places),))]
+        if fill:
+            scratch = [pltpu.VMEM((block_size, block_size), f32)] + sems + [pltpu.SemaphoreType.DMA((slot_count,))]
+        else:
+            scratch = sems
+        return pl.pallas_call(
+            functools.partial(place_kernel, groups, places, fill),
+            out_shape=tiles_of(slot_count),
+            in_specs=[SMEM] * 3 + [VMEM] * n + ([] if fill else [HBM]),
+            out_specs=HBM,
+            input_output_aliases={} if fill else {3 + n: 0},
+            scratch_shapes=scratch,
+            compiler_params=PARAMS,
+            cost_estimate=cost(0, 2 * n * len(places) * tile_bytes),
+        )(slots, ids, counts, *tiles, *([] if fill else [into]))
+
+    new_omega = place((0, 1, 2, 3), FAR_PLACES, (far_tiles, far_mate, far_across, far_last), None)
+    new_omega = place((0, 1, 2), NEAR_PLACES, (near_tiles, near_mate, near_across), new_omega)
+    new_omega = place((3,), NEAR_PLACES, (near_last,), new_omega)
     return (new_omega[None], y_product[None])
 
 

time: 130 us -> 137 us (1.054)
  the two profiles are of different devices: /device:TPU:1 before, /device:TPU:15 now
where the time goes in v1:
time: 137 us; the launch traced here: 136 us
  starting transfers between devices  91.4 us (67%)
  waiting for transfers between devices  24 us (18%)
  Pallas kernels  8.81 us (6%)
  blocking collectives  7.64 us (6%)
  local copies, waits for them, and re-layouts  2.75 us (2%)
  between operations  1.61 us (1%)
    ppermute x19, starting transfers between devices, permute(): return lax.ppermute(x, AXES, pairs)  91.4 us
    ppermute x19, waiting for transfers between devices, permute(): return lax.ppermute(x, AXES, pairs)  24 us
    all_gather x1, blocking collectives, step(): full = lax.all_gather(own_dosage, 'team', axis=0, tiled=True)  7.64 us
    pallas_call x3, Pallas kernels, place(): pl.pallas_call(functools.partial(place_kernel, groups, places, fill), out...  4.45 us
    unnamed x6, local copies, waits for them, and re-layouts  2.74 us
  transfers between devices with their start and end apart: 19, of which 7 were waited for; matrix products, arithmetic and copies ran while one was open for 0% of the time, Pallas kernels for 4%

profile of v1, /device:TPU:15, one launch (start us, length us, event | category | flops | bytes accessed | tf_op | source)
XLA Modules:
  0.0 136.3 jit_solution(15096291234091391933)
XLA Ops:
  0.6 7.6 %all-gather = f32[1,256,128]{2,1,0:T(8,128)S(1)} all-gather(f32[1,64,128]{2,1,0:T(8,128)} %param.6), channel_id=2, replica_groups=mesh['blk'=128,'team'=4] {'team'}, dimensions={1}, use_global_device_ids=true | all-gather | bytes 163840 | tf_op jit(solution)/shard_map/all_gather | solution.py:239
  8.3 11.9 %collective-permute-start = (f32[256,128]{1,0:T(8,128)S(1)}, f32[256,128]{1,0:T(8,128)S(1)}, u32[]{:S(2)}, u32[]{:S(2)}) collective-permute-start(f32[256,128]{1,0:T(8,128)S(1)} %bitcast.10), channel_id=1, source_target_pairs={{0,9},{1,504},{2,27},{3,490},{4,13},{5,508},{6,31},{7,494},{8,17},... | collective-permute-start | bytes 393224 | tf_op jit(solution)/shard_map/ppermute | solution.py:199
  20.2 4.2 %collective-permute-start.1 = (f32[256,128]{1,0:T(8,128)S(1)}, f32[256,128]{1,0:T(8,128)S(1)}, u32[]{:S(2)}, u32[]{:S(2)}) collective-permute-start(f32[256,128]{1,0:T(8,128)S(1)} %bitcast.11), channel_id=1, source_target_pairs={{0,17},{1,496},{2,35},{3,482},{4,21},{5,500},{6,39},{7,486},{8,25}... | collective-permute-start | bytes 393224 | tf_op jit(solution)/shard_map/ppermute | solution.py:199
  24.5 3.8 %collective-permute-start.4 = (f32[256,128]{1,0:T(8,128)S(1)}, f32[256,128]{1,0:T(8,128)S(1)}, u32[]{:S(2)}, u32[]{:S(2)}) collective-permute-start(f32[256,128]{1,0:T(8,128)S(1)} %bitcast.12), channel_id=1, source_target_pairs={{0,153},{1,360},{2,103},{3,414},{4,157},{5,364},{6,107},{7,418},{8... | collective-permute-start | bytes 393224 | tf_op jit(solution)/shard_map/ppermute | solution.py:199
  28.3 4.9 %collective-permute-start.5 = (f32[256,128]{1,0:T(8,128)S(1)}, f32[256,128]{1,0:T(8,128)S(1)}, u32[]{:S(2)}, u32[]{:S(2)}) collective-permute-start(f32[256,128]{1,0:T(8,128)S(1)} %bitcast.13), channel_id=1, source_target_pairs={{0,205},{1,308},{2,7},{3,259},{4,209},{5,312},{6,262},{7,2},{8,213... | collective-permute-start | bytes 393224 | tf_op jit(solution)/shard_map/ppermute | solution.py:199
  33.1 1.9 %collective-permute-start.2 = (f32[256,128]{1,0:T(8,128)S(1)}, f32[256,128]{1,0:T(8,128)S(1)}, u32[]{:S(2)}, u32[]{:S(2)}) collective-permute-start(f32[256,128]{1,0:T(8,128)S(1)} %collective-permute-done.refs_0_), channel_id=1, source_target_pairs={{0,4},{1,5},{2,6},{3,7},{4,0},{5,1},{6,2},{7,3},{8,12},{9,13},{10,... | collective-permute-start | bytes 393224 | tf_op jit(solution)/shard_map/ppermute | solution.py:199
  35.1 3.7 %collective-permute-done.1.refs_1_ = f32[256,128]{1,0:T(8,128)S(1)} collective-permute-done((f32[256,128]{1,0:T(8,128)S(1)}, f32[256,128]{1,0:T(8,128)S(1)}, u32[]{:S(2)}, u32[]{:S(2)}) %collective-permute-start.1) | collective-permute-done | bytes 131104 | tf_op jit(solution)/shard_map/ppermute | solution.py:199
  38.8 1.9 %collective-permute-start.3 = (f32[256,128]{1,0:T(8,128)S(1)}, f32[256,128]{1,0:T(8,128)S(1)}, u32[]{:S(2)}, u32[]{:S(2)}) collective-permute-start(f32[256,128]{1,0:T(8,128)S(1)} %collective-permute-done.1.refs_1_), channel_id=1, source_target_pairs={{0,4},{1,5},{2,6},{3,7},{4,0},{5,1},{6,2},{7,3},{8,12},{9,13},{10,... | collective-permute-start | bytes 393224 | tf_op jit(solution)/shard_map/ppermute | solution.py:199
  41.5 1.4 %copy-done = f32[1,24,128,128]{3,2,1,0:T(8,128)S(1)} copy-done((f32[1,24,128,128]{3,2,1,0:T(8,128)S(1)}, f32[1,24,128,128]{3,2,1,0:T(8,128)}, u32[]{:S(2)}) %copy-start) | copy-done | bytes 1572888
  44.2 2.0 %pick.1 = (s32[24]{0:T(128)S(1)}, f32[6,128,128]{2,1,0:T(8,128)S(1)}) custom-call(s32[2,24]{1,0:T(2,128)S(1)} %copy-done.1, s32[2]{0:T(128)S(1)} %pad_add_fusion.ids, s32[1,24]{1,0:T(1,128)S(1)} %copy-done.2, s32[1]{0:T(128)S(6)} %copy.11.counts, f32[24,128,128]{2,1,0:T(8,128)S(1)} %bitcast.9), custom_call_target="tpu_custom_call" | custom-call | bytes 786432 | tf_op jit(solution)/shard_map/pick/pallas_call | solution.py:228
  46.7 1.9 %collective-permute-start.6 = (f32[256,128]{1,0:T(8,128)S(1)}, f32[256,128]{1,0:T(8,128)S(1)}, u32[]{:S(2)}, u32[]{:S(2)}) collective-permute-start(f32[256,128]{1,0:T(8,128)S(1)} %partial.1), channel_id=1, source_target_pairs={{0,1},{1,0},{2,3},{3,2},{4,5},{5,4},{6,7},{7,6},{8,9},{9,8},{10,11... | collective-permute-start | bytes 393224 | tf_op jit(solution)/shard_map/ppermute | solution.py:199
  48.7 1.3 collective-permute-done.6
  50.0 4.2 %collective-permute-start.7 = (f32[256,128]{1,0:T(8,128)S(1)}, f32[256,128]{1,0:T(8,128)S(1)}, u32[]{:S(2)}, u32[]{:S(2)}) collective-permute-start(f32[256,128]{1,0:T(8,128)S(1)} %add.9.half), channel_id=1, source_target_pairs={{0,2},{1,3},{2,0},{3,1},{4,6},{5,7},{6,4},{7,5},{8,10},{9,11},{10,... | collective-permute-start | bytes 393224 | tf_op jit(solution)/shard_map/ppermute | solution.py:199
  54.2 4.1 %collective-permute-done.7.other = f32[256,128]{1,0:T(8,128)S(1)} collective-permute-done((f32[256,128]{1,0:T(8,128)S(1)}, f32[256,128]{1,0:T(8,128)S(1)}, u32[]{:S(2)}, u32[]{:S(2)}) %collective-permute-start.7) | collective-permute-done | bytes 131104 | tf_op jit(solution)/shard_map/ppermute | solution.py:199
  58.3 1.6 %tiles.1 = (f32[128,128]{1,0:T(8,128)S(1)}, f32[128,128]{1,0:T(8,128)S(1)}, f32[2,128,128]{2,1,0:T(8,128)S(1)}, f32[128,128]{1,0:T(8,128)S(1)}, f32[128,128]{1,0:T(8,128)S(1)}, /*index=5*/f32[64,128]{1,0:T(8,128)}) custom-call(s32[1]{0:T(128)} %bitcast.3.own_side, s32[2]{0:T(128)S(1)} %pad_add_fusion.ids, f32[256,128]{1,0:T(8,128)S(1)} %add.9.half, ...), custom_call_target="tpu_custom_call" | custom-call | flops 50331648 | bytes 1835008 | tf_op jit(solution)/shard_map/tiles/pallas_call | solution.py:260
  59.9 3.2 %collective-permute-start.8 = (f32[2,128,128]{2,1,0:T(8,128)S(1)}, f32[2,128,128]{2,1,0:T(8,128)S(1)}, u32[]{:S(2)}, u32[]{:S(2)}) collective-permute-start(f32[2,128,128]{2,1,0:T(8,128)S(1)} %get-tuple-element.14.side), channel_id=1, source_target_pairs={{0,4},{1,5},{2,6},{3,7},{4,0},{5,1},{6,2},{7,3},{8,12},{9,13},{10,... | collective-permute-start | bytes 393224 | tf_op jit(solution)/shard_map/ppermute | solution.py:199
  63.1 2.5 %collective-permute-done.8 = f32[2,128,128]{2,1,0:T(8,128)S(1)} collective-permute-done((f32[2,128,128]{2,1,0:T(8,128)S(1)}, f32[2,128,128]{2,1,0:T(8,128)S(1)}, u32[]{:S(2)}, u32[]{:S(2)}) %collective-permute-start.8) | collective-permute-done | bytes 131104 | tf_op jit(solution)/shard_map/ppermute | solution.py:199
  65.7 7.5 %collective-permute-start.10 = (f32[2,128,128]{2,1,0:T(8,128)S(1)}, f32[2,128,128]{2,1,0:T(8,128)S(1)}, u32[]{:S(2)}, u32[]{:S(2)}) collective-permute-start(f32[2,128,128]{2,1,0:T(8,128)S(1)} %pad_maximum_fusion.1), channel_id=1, source_target_pairs={{0,17},{1,496},{2,35},{3,482},{4,21},{5,500},{6,39},{7,486},{8,25}... | collective-permute-start | bytes 393224 | tf_op jit(solution)/shard_map/ppermute | solution.py:199
  73.2 6.3 %collective-permute-start.9 = (f32[2,128,128]{2,1,0:T(8,128)S(1)}, f32[2,128,128]{2,1,0:T(8,128)S(1)}, u32[]{:S(2)}, u32[]{:S(2)}) collective-permute-start(f32[2,128,128]{2,1,0:T(8,128)S(1)} %pad_maximum_fusion), channel_id=1, source_target_pairs={{0,9},{1,504},{2,27},{3,490},{4,13},{5,508},{6,31},{7,494},{8,17},... | collective-permute-start | bytes 393224 | tf_op jit(solution)/shard_map/ppermute | solution.py:199
  79.5 7.4 %collective-permute-done.9.got_1 = f32[2,128,128]{2,1,0:T(8,128)S(1)} collective-permute-done((f32[2,128,128]{2,1,0:T(8,128)S(1)}, f32[2,128,128]{2,1,0:T(8,128)S(1)}, u32[]{:S(2)}, u32[]{:S(2)}) %collective-permute-start.9) | collective-permute-done | bytes 131104 | tf_op jit(solution)/shard_map/ppermute | solution.py:199
  87.0 1.9 %collective-permute-start.11 = (f32[4,128,128]{2,1,0:T(8,128)S(1)}, f32[4,128,128]{2,1,0:T(8,128)S(1)}, u32[]{:S(2)}, u32[]{:S(2)}) collective-permute-start(f32[4,128,128]{2,1,0:T(8,128)S(1)} %shard_map.68.refs_0_), channel_id=1, source_target_pairs={{0,2},{1,3},{2,0},{3,1},{4,6},{5,7},{6,4},{7,5},{8,10},{9,11},{10,... | collective-permute-start | bytes 786440 | tf_op jit(solution)/shard_map/ppermute | solution.py:199
  88.9 2.9 %collective-permute-start.14 = (f32[128,128]{1,0:T(8,128)S(1)}, f32[128,128]{1,0:T(8,128)S(1)}, u32[]{:S(2)}, u32[]{:S(2)}) collective-permute-start(f32[128,128]{1,0:T(8,128)S(1)} %get-tuple-element.15.far_1), channel_id=1, source_target_pairs={{0,153},{1,360},{2,103},{3,414},{4,157},{5,364},{6,107},{7,418},{8... | collective-permute-start | bytes 196616 | tf_op jit(solution)/shard_map/ppermute | solution.py:199
  91.8 4.5 %collective-permute-start.15 = (f32[128,128]{1,0:T(8,128)S(1)}, f32[128,128]{1,0:T(8,128)S(1)}, u32[]{:S(2)}, u32[]{:S(2)}) collective-permute-start(f32[128,128]{1,0:T(8,128)S(1)} %get-tuple-element.16.far_2), channel_id=1, source_target_pairs={{0,205},{1,308},{2,7},{3,259},{4,209},{5,312},{6,262},{7,2},{8,213... | collective-permute-start | bytes 196616 | tf_op jit(solution)/shard_map/ppermute | solution.py:199
  96.4 4.0 %collective-permute-done.14.got_1 = f32[128,128]{1,0:T(8,128)S(1)} collective-permute-done((f32[128,128]{1,0:T(8,128)S(1)}, f32[128,128]{1,0:T(8,128)S(1)}, u32[]{:S(2)}, u32[]{:S(2)}) %collective-permute-start.14) | collective-permute-done | bytes 65568 | tf_op jit(solution)/shard_map/ppermute | solution.py:199
  100.5 21.6 %collective-permute-start.17 = (f32[2,128,128]{2,1,0:T(8,128)S(1)}, f32[2,128,128]{2,1,0:T(8,128)S(1)}, u32[]{:S(2)}, u32[]{:S(2)}) collective-permute-start(f32[2,128,128]{2,1,0:T(8,128)S(1)} %shard_map.69.refs_0_), channel_id=1, source_target_pairs={{0,2},{1,3},{2,0},{3,1},{4,6},{5,7},{6,4},{7,5},{8,10},{9,11},{10,... | collective-permute-start | bytes 393224 | tf_op jit(solution)/shard_map/ppermute | solution.py:199
  122.2 1.9 %collective-permute-start.13 = (f32[4,128,128]{2,1,0:T(8,128)S(1)}, f32[4,128,128]{2,1,0:T(8,128)S(1)}, u32[]{:S(2)}, u32[]{:S(2)}) collective-permute-start(f32[4,128,128]{2,1,0:T(8,128)S(1)} %shard_map.68.refs_0_), channel_id=1, source_target_pairs={{0,1},{1,0},{2,3},{3,2},{4,5},{5,4},{6,7},{7,6},{8,9},{9,8},{10,11... | collective-permute-start | bytes 786440 | tf_op jit(solution)/shard_map/ppermute | solution.py:199
  124.1 2.4 %collective-permute-start.12 = (f32[4,128,128]{2,1,0:T(8,128)S(1)}, f32[4,128,128]{2,1,0:T(8,128)S(1)}, u32[]{:S(2)}, u32[]{:S(2)}) collective-permute-start(f32[4,128,128]{2,1,0:T(8,128)S(1)} %collective-permute-done.11.refs_2_), channel_id=1, source_target_pairs={{0,1},{1,0},{2,3},{3,2},{4,5},{5,4},{6,7},{7,6},{8,9},{9,8},{10,11... | collective-permute-start | bytes 786440 | tf_op jit(solution)/shard_map/ppermute | solution.py:199
  126.5 1.9 %collective-permute-start.16 = (f32[2,128,128]{2,1,0:T(8,128)S(1)}, f32[2,128,128]{2,1,0:T(8,128)S(1)}, u32[]{:S(2)}, u32[]{:S(2)}) collective-permute-start(f32[2,128,128]{2,1,0:T(8,128)S(1)} %shard_map.69.refs_0_), channel_id=1, source_target_pairs={{0,1},{1,0},{2,3},{3,2},{4,5},{5,4},{6,7},{7,6},{8,9},{9,8},{10,11... | collective-permute-start | bytes 393224 | tf_op jit(solution)/shard_map/ppermute | solution.py:199
  128.4 2.4 %collective-permute-start.18 = (f32[2,128,128]{2,1,0:T(8,128)S(1)}, f32[2,128,128]{2,1,0:T(8,128)S(1)}, u32[]{:S(2)}, u32[]{:S(2)}) collective-permute-start(f32[2,128,128]{2,1,0:T(8,128)S(1)} %collective-permute-done.17.refs_2_), channel_id=1, source_target_pairs={{0,1},{1,0},{2,3},{3,2},{4,5},{5,4},{6,7},{7,6},{8,9},{9,8},{10,11... | collective-permute-start | bytes 393224 | tf_op jit(solution)/shard_map/ppermute | solution.py:199
  131.8 1.9 %shard_map.70.refs_3_ = f32[24,128,128]{2,1,0:T(8,128)} custom-call(s32[24]{0:T(128)S(1)} %get-tuple-element.10.slots, s32[2]{0:T(128)S(1)} %pad_add_fusion.ids, s32[1]{0:T(128)S(6)} %copy.11.counts, f32[2,128,128]{2,1,0:T(8,128)S(1)} %shard_map.69.refs_0_, f32[2,128,128]{2,1,0:T(8,128)S(1)} %collective-permute-done.16.refs_1_, ...), custom_call_target="tpu_custom_call" | custom-call | bytes 1048576 | tf_op jit(solution)/shard_map/pallas_call | solution.py:328
  133.7 1.3 shard_map.71.refs_1_
  135.1 1.2 shard_map.72
  (26 shorter events, 3.2 us)
Async XLA Ops:
  8.3 24.9 %collective-permute-start = (f32[256,128]{1,0:T(8,128)S(1)}, f32[256,128]{1,0:T(8,128)S(1)}, u32[]{:S(2)}, u32[]{:S(2)}) collective-permute-start(f32[256,128]{1,0:T(8,128)S(1)} %bitcast.10), channel_id=1, source_target_pairs={{0,9},{1,504},{2,27},{3,490},{4,13},{5,508},{6,31},{7,494},{8,17},... | collective-permute-start | bytes 393224 | tf_op jit(solution)/shard_map/ppermute | solution.py:199
  20.2 18.6 %collective-permute-start.1 = (f32[256,128]{1,0:T(8,128)S(1)}, f32[256,128]{1,0:T(8,128)S(1)}, u32[]{:S(2)}, u32[]{:S(2)}) collective-permute-start(f32[256,128]{1,0:T(8,128)S(1)} %bitcast.11), channel_id=1, source_target_pairs={{0,17},{1,496},{2,35},{3,482},{4,21},{5,500},{6,39},{7,486},{8,25}... | collective-permute-start | bytes 393224 | tf_op jit(solution)/shard_map/ppermute | solution.py:199
  24.5 21.8 %collective-permute-start.4 = (f32[256,128]{1,0:T(8,128)S(1)}, f32[256,128]{1,0:T(8,128)S(1)}, u32[]{:S(2)}, u32[]{:S(2)}) collective-permute-start(f32[256,128]{1,0:T(8,128)S(1)} %bitcast.12), channel_id=1, source_target_pairs={{0,153},{1,360},{2,103},{3,414},{4,157},{5,364},{6,107},{7,418},{8... | collective-permute-start | bytes 393224 | tf_op jit(solution)/shard_map/ppermute | solution.py:199
  28.3 18.0 %collective-permute-start.5 = (f32[256,128]{1,0:T(8,128)S(1)}, f32[256,128]{1,0:T(8,128)S(1)}, u32[]{:S(2)}, u32[]{:S(2)}) collective-permute-start(f32[256,128]{1,0:T(8,128)S(1)} %bitcast.13), channel_id=1, source_target_pairs={{0,205},{1,308},{2,7},{3,259},{4,209},{5,312},{6,262},{7,2},{8,213... | collective-permute-start | bytes 393224 | tf_op jit(solution)/shard_map/ppermute | solution.py:199
  33.1 13.1 %collective-permute-start.2 = (f32[256,128]{1,0:T(8,128)S(1)}, f32[256,128]{1,0:T(8,128)S(1)}, u32[]{:S(2)}, u32[]{:S(2)}) collective-permute-start(f32[256,128]{1,0:T(8,128)S(1)} %collective-permute-done.refs_0_), channel_id=1, source_target_pairs={{0,4},{1,5},{2,6},{3,7},{4,0},{5,1},{6,2},{7,3},{8,12},{9,13},{10,... | collective-permute-start | bytes 393224 | tf_op jit(solution)/shard_map/ppermute | solution.py:199
  38.8 7.4 %collective-permute-start.3 = (f32[256,128]{1,0:T(8,128)S(1)}, f32[256,128]{1,0:T(8,128)S(1)}, u32[]{:S(2)}, u32[]{:S(2)}) collective-permute-start(f32[256,128]{1,0:T(8,128)S(1)} %collective-permute-done.1.refs_1_), channel_id=1, source_target_pairs={{0,4},{1,5},{2,6},{3,7},{4,0},{5,1},{6,2},{7,3},{8,12},{9,13},{10,... | collective-permute-start | bytes 393224 | tf_op jit(solution)/shard_map/ppermute | solution.py:199
  41.5 1.4 %copy-start = (f32[1,24,128,128]{3,2,1,0:T(8,128)S(1)}, f32[1,24,128,128]{3,2,1,0:T(8,128)}, u32[]{:S(2)}) copy-start(f32[1,24,128,128]{3,2,1,0:T(8,128)} %param.5) | copy-start | bytes 4718596
  42.9 0.7 copy-start.1
  43.6 0.7 copy-start.2
  46.7 3.2 %collective-permute-start.6 = (f32[256,128]{1,0:T(8,128)S(1)}, f32[256,128]{1,0:T(8,128)S(1)}, u32[]{:S(2)}, u32[]{:S(2)}) collective-permute-start(f32[256,128]{1,0:T(8,128)S(1)} %partial.1), channel_id=1, source_target_pairs={{0,1},{1,0},{2,3},{3,2},{4,5},{5,4},{6,7},{7,6},{8,9},{9,8},{10,11... | collective-permute-start | bytes 393224 | tf_op jit(solution)/shard_map/ppermute | solution.py:199
  50.0 8.3 %collective-permute-start.7 = (f32[256,128]{1,0:T(8,128)S(1)}, f32[256,128]{1,0:T(8,128)S(1)}, u32[]{:S(2)}, u32[]{:S(2)}) collective-permute-start(f32[256,128]{1,0:T(8,128)S(1)} %add.9.half), channel_id=1, source_target_pairs={{0,2},{1,3},{2,0},{3,1},{4,6},{5,7},{6,4},{7,5},{8,10},{9,11},{10,... | collective-permute-start | bytes 393224 | tf_op jit(solution)/shard_map/ppermute | solution.py:199
  59.9 5.7 %collective-permute-start.8 = (f32[2,128,128]{2,1,0:T(8,128)S(1)}, f32[2,128,128]{2,1,0:T(8,128)S(1)}, u32[]{:S(2)}, u32[]{:S(2)}) collective-permute-start(f32[2,128,128]{2,1,0:T(8,128)S(1)} %get-tuple-element.14.side), channel_id=1, source_target_pairs={{0,4},{1,5},{2,6},{3,7},{4,0},{5,1},{6,2},{7,3},{8,12},{9,13},{10,... | collective-permute-start | bytes 393224 | tf_op jit(solution)/shard_map/ppermute | solution.py:199
  65.7 13.8 %collective-permute-start.10 = (f32[2,128,128]{2,1,0:T(8,128)S(1)}, f32[2,128,128]{2,1,0:T(8,128)S(1)}, u32[]{:S(2)}, u32[]{:S(2)}) collective-permute-start(f32[2,128,128]{2,1,0:T(8,128)S(1)} %pad_maximum_fusion.1), channel_id=1, source_target_pairs={{0,17},{1,496},{2,35},{3,482},{4,21},{5,500},{6,39},{7,486},{8,25}... | collective-permute-start | bytes 393224 | tf_op jit(solution)/shard_map/ppermute | solution.py:199
  73.2 13.6 %collective-permute-start.9 = (f32[2,128,128]{2,1,0:T(8,128)S(1)}, f32[2,128,128]{2,1,0:T(8,128)S(1)}, u32[]{:S(2)}, u32[]{:S(2)}) collective-permute-start(f32[2,128,128]{2,1,0:T(8,128)S(1)} %pad_maximum_fusion), channel_id=1, source_target_pairs={{0,9},{1,504},{2,27},{3,490},{4,13},{5,508},{6,31},{7,494},{8,17},... | collective-permute-start | bytes 393224 | tf_op jit(solution)/shard_map/ppermute | solution.py:199
  87.0 37.1 %collective-permute-start.11 = (f32[4,128,128]{2,1,0:T(8,128)S(1)}, f32[4,128,128]{2,1,0:T(8,128)S(1)}, u32[]{:S(2)}, u32[]{:S(2)}) collective-permute-start(f32[4,128,128]{2,1,0:T(8,128)S(1)} %shard_map.68.refs_0_), channel_id=1, source_target_pairs={{0,2},{1,3},{2,0},{3,1},{4,6},{5,7},{6,4},{7,5},{8,10},{9,11},{10,... | collective-permute-start | bytes 786440 | tf_op jit(solution)/shard_map/ppermute | solution.py:199
  88.9 11.4 %collective-permute-start.14 = (f32[128,128]{1,0:T(8,128)S(1)}, f32[128,128]{1,0:T(8,128)S(1)}, u32[]{:S(2)}, u32[]{:S(2)}) collective-permute-start(f32[128,128]{1,0:T(8,128)S(1)} %get-tuple-element.15.far_1), channel_id=1, source_target_pairs={{0,153},{1,360},{2,103},{3,414},{4,157},{5,364},{6,107},{7,418},{8... | collective-permute-start | bytes 196616 | tf_op jit(solution)/shard_map/ppermute | solution.py:199
  91.8 8.5 %collective-permute-start.15 = (f32[128,128]{1,0:T(8,128)S(1)}, f32[128,128]{1,0:T(8,128)S(1)}, u32[]{:S(2)}, u32[]{:S(2)}) collective-permute-start(f32[128,128]{1,0:T(8,128)S(1)} %get-tuple-element.16.far_2), channel_id=1, source_target_pairs={{0,205},{1,308},{2,7},{3,259},{4,209},{5,312},{6,262},{7,2},{8,213... | collective-permute-start | bytes 196616 | tf_op jit(solution)/shard_map/ppermute | solution.py:199
  100.5 27.9 %collective-permute-start.17 = (f32[2,128,128]{2,1,0:T(8,128)S(1)}, f32[2,128,128]{2,1,0:T(8,128)S(1)}, u32[]{:S(2)}, u32[]{:S(2)}) collective-permute-start(f32[2,128,128]{2,1,0:T(8,128)S(1)} %shard_map.69.refs_0_), channel_id=1, source_target_pairs={{0,2},{1,3},{2,0},{3,1},{4,6},{5,7},{6,4},{7,5},{8,10},{9,11},{10,... | collective-permute-start | bytes 393224 | tf_op jit(solution)/shard_map/ppermute | solution.py:199
  122.2 11.6 %collective-permute-start.13 = (f32[4,128,128]{2,1,0:T(8,128)S(1)}, f32[4,128,128]{2,1,0:T(8,128)S(1)}, u32[]{:S(2)}, u32[]{:S(2)}) collective-permute-start(f32[4,128,128]{2,1,0:T(8,128)S(1)} %shard_map.68.refs_0_), channel_id=1, source_target_pairs={{0,1},{1,0},{2,3},{3,2},{4,5},{5,4},{6,7},{7,6},{8,9},{9,8},{10,11... | collective-permute-start | bytes 786440 | tf_op jit(solution)/shard_map/ppermute | solution.py:199
  124.1 11.0 %collective-permute-start.12 = (f32[4,128,128]{2,1,0:T(8,128)S(1)}, f32[4,128,128]{2,1,0:T(8,128)S(1)}, u32[]{:S(2)}, u32[]{:S(2)}) collective-permute-start(f32[4,128,128]{2,1,0:T(8,128)S(1)} %collective-permute-done.11.refs_2_), channel_id=1, source_target_pairs={{0,1},{1,0},{2,3},{3,2},{4,5},{5,4},{6,7},{7,6},{8,9},{9,8},{10,11... | collective-permute-start | bytes 786440 | tf_op jit(solution)/shard_map/ppermute | solution.py:199
  126.5 4.4 %collective-permute-start.16 = (f32[2,128,128]{2,1,0:T(8,128)S(1)}, f32[2,128,128]{2,1,0:T(8,128)S(1)}, u32[]{:S(2)}, u32[]{:S(2)}) collective-permute-start(f32[2,128,128]{2,1,0:T(8,128)S(1)} %shard_map.69.refs_0_), channel_id=1, source_target_pairs={{0,1},{1,0},{2,3},{3,2},{4,5},{5,4},{6,7},{7,6},{8,9},{9,8},{10,11... | collective-permute-start | bytes 393224 | tf_op jit(solution)/shard_map/ppermute | solution.py:199
  128.4 3.4 %collective-permute-start.18 = (f32[2,128,128]{2,1,0:T(8,128)S(1)}, f32[2,128,128]{2,1,0:T(8,128)S(1)}, u32[]{:S(2)}, u32[]{:S(2)}) collective-permute-start(f32[2,128,128]{2,1,0:T(8,128)S(1)} %collective-permute-done.17.refs_2_), channel_id=1, source_target_pairs={{0,1},{1,0},{2,3},{3,2},{4,5},{5,4},{6,7},{7,6},{8,9},{9,8},{10,11... | collective-permute-start | bytes 393224 | tf_op jit(solution)/shard_map/ppermute | solution.py:199

commit v2 on v1

--- a/solution.py
+++ b/solution.py
@@ -18,8 +18,8 @@
 PLACES = 6
 OFFSETS = np.array(
     [
-        [[2, 4, 3, 5, 38, 51], [-2, -4, -1, -3, -38, -51], [6, 8, 7, 0, 25, 1], [-6, -8, -5, -7, -25, 64]],
-        [[2, 4, 1, 3, 38, 51], [-2, -4, -3, -5, -38, -51], [6, 8, 5, 7, 25, 64], [-6, -8, -7, 0, -25, -1]],
+        [[2, 8, 3, 0, 51, 1], [-2, -8, -1, -7, -51, 64], [4, 6, 5, 7, 38, 25], [-4, -6, -3, -5, -38, -25]],
+        [[2, 8, 1, 7, 51, 64], [-2, -8, -3, 0, -51, -1], [4, 6, 3, 5, 38, 25], [-4, -6, -5, -7, -38, -25]],
     ]
 )
 VMEM = pl.BlockSpec(memory_space=pltpu.VMEM)
@@ -39,20 +39,22 @@
     return one(a[0], b[0]) + (one(a[0], b[1]) + one(a[1], b[0]))
 
 
-def pick_kernel(table, ids, columns, counts, omega, slots, old, sems):
+def pick_kernel(rows, ids, columns, counts, omega, slots, old, sems):
     owner, member = ids[0], ids[1]
     count = counts[0]
     parity = lax.rem(owner, 2)
-    total = table.shape[1]
+    choices = np.mod(OFFSETS, rows).reshape(2, -1)
+    total = choices.shape[1]
     slot_count = columns.shape[1]
+    wanted = [jnp.where(parity == 0, int(choices[0, i]), int(choices[1, i])) for i in range(total)]
     for i in range(total):
         slots[i] = -1
 
     def match(s, carry):
-        offset = lax.rem(columns[0, s] - owner + 128, 128)
+        offset = lax.rem(columns[0, s] - owner + rows, rows)
         for i in range(total):
 
-            @pl.when(table[parity, i] == offset)
+            @pl.when(wanted[i] == offset)
             def _():
                 slots[i] = s
 
@@ -218,23 +220,22 @@
 
     ids = jnp.stack([owner, member]).astype(jnp.int32)
     own_side = jnp.logical_or(
-        jnp.logical_and(owner % 2 == 0, member == 2), jnp.logical_and(owner % 2 == 1, member == 3)
+        jnp.logical_and(owner % 2 == 0, member == 0), jnp.logical_and(owner % 2 == 1, member == 1)
     ).astype(jnp.int32)[None]
-    table = jnp.asarray(np.mod(OFFSETS, rows).astype(np.int32).reshape(2, team * PLACES))
     tile_shape = jax.ShapeDtypeStruct((block_size, block_size), f32)
     tiles_shape = jax.ShapeDtypeStruct((PLACES, block_size, block_size), f32)
     tile_bytes = block_size * block_size * 4
 
     slots, old = pl.pallas_call(
-        pick_kernel,
+        functools.partial(pick_kernel, rows),
         name="pick",
         out_shape=(jax.ShapeDtypeStruct((team * PLACES,), jnp.int32), tiles_shape),
-        in_specs=[SMEM, SMEM, SMEM, SMEM, HBM],
+        in_specs=[SMEM, SMEM, SMEM, HBM],
         out_specs=(SMEM, VMEM),
         scratch_shapes=[pltpu.SemaphoreType.DMA((PLACES,))],
         compiler_params=PARAMS,
         cost_estimate=cost(0, 2 * PLACES * tile_bytes),
-    )(table, ids, columns, counts, weights)
+    )(ids, columns, counts, pltpu.with_memory_space_constraint(weights, pltpu.MemorySpace.HBM))
 
     full = lax.all_gather(own_dosage, "team", axis=0, tiled=True)
     column = [None] * PLACES

time: 137 us -> 126 us (0.920)
  the two profiles are of different devices: /device:TPU:15 before, /device:TPU:1 now
where the time goes in v2:
time: 126 us; the launch traced here: 123 us
  starting transfers between devices  62.6 us (50%)
  waiting for transfers between devices  36.1 us (29%)
  blocking collectives  13.8 us (11%)
  Pallas kernels  8.56 us (7%)
  between operations  1.6 us (1%)
    ppermute x19, starting transfers between devices, permute(): return lax.ppermute(x, AXES, pairs)  62.6 us
    ppermute x19, waiting for transfers between devices, permute(): return lax.ppermute(x, AXES, pairs)  36.1 us
    all_gather x1, blocking collectives, step(): full = lax.all_gather(own_dosage, 'team', axis=0, tiled=True)  13.8 us
    pallas_call x3, Pallas kernels, place(): pl.pallas_call(functools.partial(place_kernel, groups, places, fill), out...  3.85 us
  transfers between devices with their start and end apart: 19, of which 8 were waited for; matrix products, arithmetic and copies ran while one was open for 0% of the time, Pallas kernels for 5%

profile of v2, /device:TPU:1, one launch (start us, length us, event | category | flops | bytes accessed | tf_op | source)
XLA Modules:
  0.0 123.4 jit_solution(2396849855725789571)
XLA Ops:
  0.6 13.8 %all-gather = f32[1,256,128]{2,1,0:T(8,128)S(1)} all-gather(f32[1,64,128]{2,1,0:T(8,128)} %param.5), channel_id=2, replica_groups=mesh['blk'=128,'team'=4] {'team'}, dimensions={1}, use_global_device_ids=true | all-gather | bytes 163840 | tf_op jit(solution)/shard_map/all_gather | solution.py:240
  14.4 8.3 %collective-permute-start = (f32[256,128]{1,0:T(8,128)S(1)}, f32[256,128]{1,0:T(8,128)S(1)}, u32[]{:S(2)}, u32[]{:S(2)}) collective-permute-start(f32[256,128]{1,0:T(8,128)S(1)} %bitcast.9), channel_id=1, source_target_pairs={{0,9},{1,504},{2,19},{3,498},{4,13},{5,508},{6,23},{7,502},{8,17},... | collective-permute-start | bytes 393224 | tf_op jit(solution)/shard_map/ppermute | solution.py:201
  22.7 4.2 %collective-permute-start.1 = (f32[256,128]{1,0:T(8,128)S(1)}, f32[256,128]{1,0:T(8,128)S(1)}, u32[]{:S(2)}, u32[]{:S(2)}) collective-permute-start(f32[256,128]{1,0:T(8,128)S(1)} %bitcast.10), channel_id=1, source_target_pairs={{0,33},{1,480},{2,27},{3,490},{4,37},{5,484},{6,31},{7,494},{8,41}... | collective-permute-start | bytes 393224 | tf_op jit(solution)/shard_map/ppermute | solution.py:201
  26.9 7.2 %collective-permute-start.4 = (f32[256,128]{1,0:T(8,128)S(1)}, f32[256,128]{1,0:T(8,128)S(1)}, u32[]{:S(2)}, u32[]{:S(2)}) collective-permute-start(f32[256,128]{1,0:T(8,128)S(1)} %bitcast.11), channel_id=1, source_target_pairs={{0,205},{1,308},{2,155},{3,362},{4,209},{5,312},{6,159},{7,366},{8... | collective-permute-start | bytes 393224 | tf_op jit(solution)/shard_map/ppermute | solution.py:201
  34.2 2.0 %collective-permute-start.5 = (f32[256,128]{1,0:T(8,128)S(1)}, f32[256,128]{1,0:T(8,128)S(1)}, u32[]{:S(2)}, u32[]{:S(2)}) collective-permute-start(f32[256,128]{1,0:T(8,128)S(1)} %bitcast.12), channel_id=1, source_target_pairs={{0,5},{1,257},{2,103},{3,414},{4,260},{5,0},{6,107},{7,418},{8,13}... | collective-permute-start | bytes 393224 | tf_op jit(solution)/shard_map/ppermute | solution.py:201
  36.2 2.6 %collective-permute-start.2 = (f32[256,128]{1,0:T(8,128)S(1)}, f32[256,128]{1,0:T(8,128)S(1)}, u32[]{:S(2)}, u32[]{:S(2)}) collective-permute-start(f32[256,128]{1,0:T(8,128)S(1)} %collective-permute-done.refs_0_), channel_id=1, source_target_pairs={{0,4},{1,5},{2,6},{3,7},{4,0},{5,1},{6,2},{7,3},{8,12},{9,13},{10,... | collective-permute-start | bytes 393224 | tf_op jit(solution)/shard_map/ppermute | solution.py:201
  38.7 6.5 %collective-permute-done.1.refs_1_ = f32[256,128]{1,0:T(8,128)S(1)} collective-permute-done((f32[256,128]{1,0:T(8,128)S(1)}, f32[256,128]{1,0:T(8,128)S(1)}, u32[]{:S(2)}, u32[]{:S(2)}) %collective-permute-start.1) | collective-permute-done | bytes 131104 | tf_op jit(solution)/shard_map/ppermute | solution.py:201
  45.2 2.9 %collective-permute-start.3 = (f32[256,128]{1,0:T(8,128)S(1)}, f32[256,128]{1,0:T(8,128)S(1)}, u32[]{:S(2)}, u32[]{:S(2)}) collective-permute-start(f32[256,128]{1,0:T(8,128)S(1)} %collective-permute-done.1.refs_1_), channel_id=1, source_target_pairs={{0,4},{1,5},{2,6},{3,7},{4,0},{5,1},{6,2},{7,3},{8,12},{9,13},{10,... | collective-permute-start | bytes 393224 | tf_op jit(solution)/shard_map/ppermute | solution.py:201
  48.9 0.7 copy-done
  49.5 2.3 %pick.1 = (s32[24]{0:T(128)S(1)}, f32[6,128,128]{2,1,0:T(8,128)S(1)}) custom-call(s32[2]{0:T(128)S(1)} %pad_add_fusion.ids, s32[1,24]{1,0:T(1,128)S(1)} %copy-done, s32[1]{0:T(128)S(6)} %copy.10.counts, f32[24,128,128]{2,1,0:T(8,128)} %bitcast.18), custom_call_target="tpu_custom_call" | custom-call | bytes 786432 | tf_op jit(solution)/shard_map/pick/pallas_call | solution.py:229
  52.4 1.9 %collective-permute-start.6 = (f32[256,128]{1,0:T(8,128)S(1)}, f32[256,128]{1,0:T(8,128)S(1)}, u32[]{:S(2)}, u32[]{:S(2)}) collective-permute-start(f32[256,128]{1,0:T(8,128)S(1)} %partial.1), channel_id=1, source_target_pairs={{0,1},{1,0},{2,3},{3,2},{4,5},{5,4},{6,7},{7,6},{8,9},{9,8},{10,11... | collective-permute-start | bytes 393224 | tf_op jit(solution)/shard_map/ppermute | solution.py:201
  54.3 1.3 %collective-permute-done.6 = f32[256,128]{1,0:T(8,128)S(1)} collective-permute-done((f32[256,128]{1,0:T(8,128)S(1)}, f32[256,128]{1,0:T(8,128)S(1)}, u32[]{:S(2)}, u32[]{:S(2)}) %collective-permute-start.6) | collective-permute-done | bytes 131104 | tf_op jit(solution)/shard_map/ppermute | solution.py:201
  55.7 1.9 %collective-permute-start.7 = (f32[256,128]{1,0:T(8,128)S(1)}, f32[256,128]{1,0:T(8,128)S(1)}, u32[]{:S(2)}, u32[]{:S(2)}) collective-permute-start(f32[256,128]{1,0:T(8,128)S(1)} %add.9.half), channel_id=1, source_target_pairs={{0,2},{1,3},{2,0},{3,1},{4,6},{5,7},{6,4},{7,5},{8,10},{9,11},{10,... | collective-permute-start | bytes 393224 | tf_op jit(solution)/shard_map/ppermute | solution.py:201
  57.6 6.4 %collective-permute-done.7.other = f32[256,128]{1,0:T(8,128)S(1)} collective-permute-done((f32[256,128]{1,0:T(8,128)S(1)}, f32[256,128]{1,0:T(8,128)S(1)}, u32[]{:S(2)}, u32[]{:S(2)}) %collective-permute-start.7) | collective-permute-done | bytes 131104 | tf_op jit(solution)/shard_map/ppermute | solution.py:201
  64.0 1.6 %tiles.1 = (f32[128,128]{1,0:T(8,128)S(1)}, f32[128,128]{1,0:T(8,128)S(1)}, f32[2,128,128]{2,1,0:T(8,128)S(1)}, f32[128,128]{1,0:T(8,128)S(1)}, f32[128,128]{1,0:T(8,128)S(1)}, /*index=5*/f32[64,128]{1,0:T(8,128)}) custom-call(s32[1]{0:T(128)} %bitcast.3.own_side, s32[2]{0:T(128)S(1)} %pad_add_fusion.ids, f32[256,128]{1,0:T(8,128)S(1)} %add.9.half, ...), custom_call_target="tpu_custom_call" | custom-call | flops 50331648 | bytes 1835008 | tf_op jit(solution)/shard_map/tiles/pallas_call | solution.py:261
  65.6 2.3 %collective-permute-start.8 = (f32[2,128,128]{2,1,0:T(8,128)S(1)}, f32[2,128,128]{2,1,0:T(8,128)S(1)}, u32[]{:S(2)}, u32[]{:S(2)}) collective-permute-start(f32[2,128,128]{2,1,0:T(8,128)S(1)} %get-tuple-element.14.side), channel_id=1, source_target_pairs={{0,4},{1,5},{2,6},{3,7},{4,0},{5,1},{6,2},{7,3},{8,12},{9,13},{10,... | collective-permute-start | bytes 393224 | tf_op jit(solution)/shard_map/ppermute | solution.py:201
  67.9 3.4 %collective-permute-done.8 = f32[2,128,128]{2,1,0:T(8,128)S(1)} collective-permute-done((f32[2,128,128]{2,1,0:T(8,128)S(1)}, f32[2,128,128]{2,1,0:T(8,128)S(1)}, u32[]{:S(2)}, u32[]{:S(2)}) %collective-permute-start.8) | collective-permute-done | bytes 131104 | tf_op jit(solution)/shard_map/ppermute | solution.py:201
  71.3 5.8 %collective-permute-start.10 = (f32[2,128,128]{2,1,0:T(8,128)S(1)}, f32[2,128,128]{2,1,0:T(8,128)S(1)}, u32[]{:S(2)}, u32[]{:S(2)}) collective-permute-start(f32[2,128,128]{2,1,0:T(8,128)S(1)} %pad_maximum_fusion.1), channel_id=1, source_target_pairs={{0,33},{1,480},{2,27},{3,490},{4,37},{5,484},{6,31},{7,494},{8,41}... | collective-permute-start | bytes 393224 | tf_op jit(solution)/shard_map/ppermute | solution.py:201
  77.2 1.9 %collective-permute-start.9 = (f32[2,128,128]{2,1,0:T(8,128)S(1)}, f32[2,128,128]{2,1,0:T(8,128)S(1)}, u32[]{:S(2)}, u32[]{:S(2)}) collective-permute-start(f32[2,128,128]{2,1,0:T(8,128)S(1)} %pad_maximum_fusion), channel_id=1, source_target_pairs={{0,9},{1,504},{2,19},{3,498},{4,13},{5,508},{6,23},{7,502},{8,17},... | collective-permute-start | bytes 393224 | tf_op jit(solution)/shard_map/ppermute | solution.py:201
  79.1 7.4 %collective-permute-done.10.got_2 = f32[2,128,128]{2,1,0:T(8,128)S(1)} collective-permute-done((f32[2,128,128]{2,1,0:T(8,128)S(1)}, f32[2,128,128]{2,1,0:T(8,128)S(1)}, u32[]{:S(2)}, u32[]{:S(2)}) %collective-permute-start.10) | collective-permute-done | bytes 131104 | tf_op jit(solution)/shard_map/ppermute | solution.py:201
  87.4 3.1 %collective-permute-start.11 = (f32[4,128,128]{2,1,0:T(8,128)S(1)}, f32[4,128,128]{2,1,0:T(8,128)S(1)}, u32[]{:S(2)}, u32[]{:S(2)}) collective-permute-start(f32[4,128,128]{2,1,0:T(8,128)S(1)} %shard_map.59.refs_0_), channel_id=1, source_target_pairs={{0,2},{1,3},{2,0},{3,1},{4,6},{5,7},{6,4},{7,5},{8,10},{9,11},{10,... | collective-permute-start | bytes 786440 | tf_op jit(solution)/shard_map/ppermute | solution.py:201
  90.5 5.5 %collective-permute-start.14 = (f32[128,128]{1,0:T(8,128)S(1)}, f32[128,128]{1,0:T(8,128)S(1)}, u32[]{:S(2)}, u32[]{:S(2)}) collective-permute-start(f32[128,128]{1,0:T(8,128)S(1)} %get-tuple-element.15.far_1), channel_id=1, source_target_pairs={{0,205},{1,308},{2,155},{3,362},{4,209},{5,312},{6,159},{7,366},{8... | collective-permute-start | bytes 196616 | tf_op jit(solution)/shard_map/ppermute | solution.py:201
  96.0 2.3 %collective-permute-start.15 = (f32[128,128]{1,0:T(8,128)S(1)}, f32[128,128]{1,0:T(8,128)S(1)}, u32[]{:S(2)}, u32[]{:S(2)}) collective-permute-start(f32[128,128]{1,0:T(8,128)S(1)} %get-tuple-element.16.far_2), channel_id=1, source_target_pairs={{0,5},{1,257},{2,103},{3,414},{4,260},{5,0},{6,107},{7,418},{8,13}... | collective-permute-start | bytes 196616 | tf_op jit(solution)/shard_map/ppermute | solution.py:201
  98.3 9.4 %collective-permute-done.14.got_1 = f32[128,128]{1,0:T(8,128)S(1)} collective-permute-done((f32[128,128]{1,0:T(8,128)S(1)}, f32[128,128]{1,0:T(8,128)S(1)}, u32[]{:S(2)}, u32[]{:S(2)}) %collective-permute-start.14) | collective-permute-done | bytes 65568 | tf_op jit(solution)/shard_map/ppermute | solution.py:201
  107.9 1.9 %collective-permute-start.17 = (f32[2,128,128]{2,1,0:T(8,128)S(1)}, f32[2,128,128]{2,1,0:T(8,128)S(1)}, u32[]{:S(2)}, u32[]{:S(2)}) collective-permute-start(f32[2,128,128]{2,1,0:T(8,128)S(1)} %shard_map.60.refs_0_), channel_id=1, source_target_pairs={{0,2},{1,3},{2,0},{3,1},{4,6},{5,7},{6,4},{7,5},{8,10},{9,11},{10,... | collective-permute-start | bytes 393224 | tf_op jit(solution)/shard_map/ppermute | solution.py:201
  109.8 1.9 %collective-permute-start.13 = (f32[4,128,128]{2,1,0:T(8,128)S(1)}, f32[4,128,128]{2,1,0:T(8,128)S(1)}, u32[]{:S(2)}, u32[]{:S(2)}) collective-permute-start(f32[4,128,128]{2,1,0:T(8,128)S(1)} %shard_map.59.refs_0_), channel_id=1, source_target_pairs={{0,1},{1,0},{2,3},{3,2},{4,5},{5,4},{6,7},{7,6},{8,9},{9,8},{10,11... | collective-permute-start | bytes 786440 | tf_op jit(solution)/shard_map/ppermute | solution.py:201
  111.7 2.4 %collective-permute-start.12 = (f32[4,128,128]{2,1,0:T(8,128)S(1)}, f32[4,128,128]{2,1,0:T(8,128)S(1)}, u32[]{:S(2)}, u32[]{:S(2)}) collective-permute-start(f32[4,128,128]{2,1,0:T(8,128)S(1)} %collective-permute-done.11.refs_2_), channel_id=1, source_target_pairs={{0,1},{1,0},{2,3},{3,2},{4,5},{5,4},{6,7},{7,6},{8,9},{9,8},{10,11... | collective-permute-start | bytes 786440 | tf_op jit(solution)/shard_map/ppermute | solution.py:201
  114.2 1.9 %collective-permute-start.16 = (f32[2,128,128]{2,1,0:T(8,128)S(1)}, f32[2,128,128]{2,1,0:T(8,128)S(1)}, u32[]{:S(2)}, u32[]{:S(2)}) collective-permute-start(f32[2,128,128]{2,1,0:T(8,128)S(1)} %shard_map.60.refs_0_), channel_id=1, source_target_pairs={{0,1},{1,0},{2,3},{3,2},{4,5},{5,4},{6,7},{7,6},{8,9},{9,8},{10,11... | collective-permute-start | bytes 393224 | tf_op jit(solution)/shard_map/ppermute | solution.py:201
  116.1 2.4 %collective-permute-start.18 = (f32[2,128,128]{2,1,0:T(8,128)S(1)}, f32[2,128,128]{2,1,0:T(8,128)S(1)}, u32[]{:S(2)}, u32[]{:S(2)}) collective-permute-start(f32[2,128,128]{2,1,0:T(8,128)S(1)} %collective-permute-done.17.refs_2_), channel_id=1, source_target_pairs={{0,1},{1,0},{2,3},{3,2},{4,5},{5,4},{6,7},{7,6},{8,9},{9,8},{10,11... | collective-permute-start | bytes 393224 | tf_op jit(solution)/shard_map/ppermute | solution.py:201
  118.5 1.0 collective-permute-done.18.refs_3_
  119.5 1.9 %shard_map.61.refs_3_ = f32[24,128,128]{2,1,0:T(8,128)} custom-call(s32[24]{0:T(128)S(1)} %get-tuple-element.10.slots, s32[2]{0:T(128)S(1)} %pad_add_fusion.ids, s32[1]{0:T(128)S(6)} %copy.10.counts, f32[2,128,128]{2,1,0:T(8,128)S(1)} %shard_map.60.refs_0_, f32[2,128,128]{2,1,0:T(8,128)S(1)} %collective-permute-done.16.refs_1_, ...), custom_call_target="tpu_custom_call" | custom-call | bytes 1048576 | tf_op jit(solution)/shard_map/pallas_call | solution.py:329
  121.4 1.3 %shard_map.62.refs_1_ = f32[24,128,128]{2,1,0:T(8,128)} custom-call(s32[24]{0:T(128)S(1)} %get-tuple-element.10.slots, s32[2]{0:T(128)S(1)} %pad_add_fusion.ids, s32[1]{0:T(128)S(6)} %copy.10.counts, f32[4,128,128]{2,1,0:T(8,128)S(1)} %shard_map.59.refs_0_, f32[4,128,128]{2,1,0:T(8,128)S(1)} %collective-permute-done.13.refs_1_, ...), custom_call_target="tpu_custom_call", output_to_operand_aliasing={{}: (6, {})} | custom-call | bytes 1572864 | tf_op jit(solution)/shard_map/pallas_call | solution.py:329
  (22 shorter events, 2.2 us)
Async XLA Ops:
  14.4 21.7 %collective-permute-start = (f32[256,128]{1,0:T(8,128)S(1)}, f32[256,128]{1,0:T(8,128)S(1)}, u32[]{:S(2)}, u32[]{:S(2)}) collective-permute-start(f32[256,128]{1,0:T(8,128)S(1)} %bitcast.9), channel_id=1, source_target_pairs={{0,9},{1,504},{2,19},{3,498},{4,13},{5,508},{6,23},{7,502},{8,17},... | collective-permute-start | bytes 393224 | tf_op jit(solution)/shard_map/ppermute | solution.py:201
  22.7 22.5 %collective-permute-start.1 = (f32[256,128]{1,0:T(8,128)S(1)}, f32[256,128]{1,0:T(8,128)S(1)}, u32[]{:S(2)}, u32[]{:S(2)}) collective-permute-start(f32[256,128]{1,0:T(8,128)S(1)} %bitcast.10), channel_id=1, source_target_pairs={{0,33},{1,480},{2,27},{3,490},{4,37},{5,484},{6,31},{7,494},{8,41}... | collective-permute-start | bytes 393224 | tf_op jit(solution)/shard_map/ppermute | solution.py:201
  26.9 25.0 %collective-permute-start.4 = (f32[256,128]{1,0:T(8,128)S(1)}, f32[256,128]{1,0:T(8,128)S(1)}, u32[]{:S(2)}, u32[]{:S(2)}) collective-permute-start(f32[256,128]{1,0:T(8,128)S(1)} %bitcast.11), channel_id=1, source_target_pairs={{0,205},{1,308},{2,155},{3,362},{4,209},{5,312},{6,159},{7,366},{8... | collective-permute-start | bytes 393224 | tf_op jit(solution)/shard_map/ppermute | solution.py:201
  34.2 17.7 %collective-permute-start.5 = (f32[256,128]{1,0:T(8,128)S(1)}, f32[256,128]{1,0:T(8,128)S(1)}, u32[]{:S(2)}, u32[]{:S(2)}) collective-permute-start(f32[256,128]{1,0:T(8,128)S(1)} %bitcast.12), channel_id=1, source_target_pairs={{0,5},{1,257},{2,103},{3,414},{4,260},{5,0},{6,107},{7,418},{8,13}... | collective-permute-start | bytes 393224 | tf_op jit(solution)/shard_map/ppermute | solution.py:201
  36.2 15.8 %collective-permute-start.2 = (f32[256,128]{1,0:T(8,128)S(1)}, f32[256,128]{1,0:T(8,128)S(1)}, u32[]{:S(2)}, u32[]{:S(2)}) collective-permute-start(f32[256,128]{1,0:T(8,128)S(1)} %collective-permute-done.refs_0_), channel_id=1, source_target_pairs={{0,4},{1,5},{2,6},{3,7},{4,0},{5,1},{6,2},{7,3},{8,12},{9,13},{10,... | collective-permute-start | bytes 393224 | tf_op jit(solution)/shard_map/ppermute | solution.py:201
  45.2 6.7 %collective-permute-start.3 = (f32[256,128]{1,0:T(8,128)S(1)}, f32[256,128]{1,0:T(8,128)S(1)}, u32[]{:S(2)}, u32[]{:S(2)}) collective-permute-start(f32[256,128]{1,0:T(8,128)S(1)} %collective-permute-done.1.refs_1_), channel_id=1, source_target_pairs={{0,4},{1,5},{2,6},{3,7},{4,0},{5,1},{6,2},{7,3},{8,12},{9,13},{10,... | collective-permute-start | bytes 393224 | tf_op jit(solution)/shard_map/ppermute | solution.py:201
  48.9 0.7 copy-start
  52.4 3.2 %collective-permute-start.6 = (f32[256,128]{1,0:T(8,128)S(1)}, f32[256,128]{1,0:T(8,128)S(1)}, u32[]{:S(2)}, u32[]{:S(2)}) collective-permute-start(f32[256,128]{1,0:T(8,128)S(1)} %partial.1), channel_id=1, source_target_pairs={{0,1},{1,0},{2,3},{3,2},{4,5},{5,4},{6,7},{7,6},{8,9},{9,8},{10,11... | collective-permute-start | bytes 393224 | tf_op jit(solution)/shard_map/ppermute | solution.py:201
  55.7 8.3 %collective-permute-start.7 = (f32[256,128]{1,0:T(8,128)S(1)}, f32[256,128]{1,0:T(8,128)S(1)}, u32[]{:S(2)}, u32[]{:S(2)}) collective-permute-start(f32[256,128]{1,0:T(8,128)S(1)} %add.9.half), channel_id=1, source_target_pairs={{0,2},{1,3},{2,0},{3,1},{4,6},{5,7},{6,4},{7,5},{8,10},{9,11},{10,... | collective-permute-start | bytes 393224 | tf_op jit(solution)/shard_map/ppermute | solution.py:201
  65.6 5.7 %collective-permute-start.8 = (f32[2,128,128]{2,1,0:T(8,128)S(1)}, f32[2,128,128]{2,1,0:T(8,128)S(1)}, u32[]{:S(2)}, u32[]{:S(2)}) collective-permute-start(f32[2,128,128]{2,1,0:T(8,128)S(1)} %get-tuple-element.14.side), channel_id=1, source_target_pairs={{0,4},{1,5},{2,6},{3,7},{4,0},{5,1},{6,2},{7,3},{8,12},{9,13},{10,... | collective-permute-start | bytes 393224 | tf_op jit(solution)/shard_map/ppermute | solution.py:201
  71.3 15.2 %collective-permute-start.10 = (f32[2,128,128]{2,1,0:T(8,128)S(1)}, f32[2,128,128]{2,1,0:T(8,128)S(1)}, u32[]{:S(2)}, u32[]{:S(2)}) collective-permute-start(f32[2,128,128]{2,1,0:T(8,128)S(1)} %pad_maximum_fusion.1), channel_id=1, source_target_pairs={{0,33},{1,480},{2,27},{3,490},{4,37},{5,484},{6,31},{7,494},{8,41}... | collective-permute-start | bytes 393224 | tf_op jit(solution)/shard_map/ppermute | solution.py:201
  77.2 10.0 %collective-permute-start.9 = (f32[2,128,128]{2,1,0:T(8,128)S(1)}, f32[2,128,128]{2,1,0:T(8,128)S(1)}, u32[]{:S(2)}, u32[]{:S(2)}) collective-permute-start(f32[2,128,128]{2,1,0:T(8,128)S(1)} %pad_maximum_fusion), channel_id=1, source_target_pairs={{0,9},{1,504},{2,19},{3,498},{4,13},{5,508},{6,23},{7,502},{8,17},... | collective-permute-start | bytes 393224 | tf_op jit(solution)/shard_map/ppermute | solution.py:201
  87.4 24.3 %collective-permute-start.11 = (f32[4,128,128]{2,1,0:T(8,128)S(1)}, f32[4,128,128]{2,1,0:T(8,128)S(1)}, u32[]{:S(2)}, u32[]{:S(2)}) collective-permute-start(f32[4,128,128]{2,1,0:T(8,128)S(1)} %shard_map.59.refs_0_), channel_id=1, source_target_pairs={{0,2},{1,3},{2,0},{3,1},{4,6},{5,7},{6,4},{7,5},{8,10},{9,11},{10,... | collective-permute-start | bytes 786440 | tf_op jit(solution)/shard_map/ppermute | solution.py:201
  90.5 17.3 %collective-permute-start.14 = (f32[128,128]{1,0:T(8,128)S(1)}, f32[128,128]{1,0:T(8,128)S(1)}, u32[]{:S(2)}, u32[]{:S(2)}) collective-permute-start(f32[128,128]{1,0:T(8,128)S(1)} %get-tuple-element.15.far_1), channel_id=1, source_target_pairs={{0,205},{1,308},{2,155},{3,362},{4,209},{5,312},{6,159},{7,366},{8... | collective-permute-start | bytes 196616 | tf_op jit(solution)/shard_map/ppermute | solution.py:201
  96.0 11.8 %collective-permute-start.15 = (f32[128,128]{1,0:T(8,128)S(1)}, f32[128,128]{1,0:T(8,128)S(1)}, u32[]{:S(2)}, u32[]{:S(2)}) collective-permute-start(f32[128,128]{1,0:T(8,128)S(1)} %get-tuple-element.16.far_2), channel_id=1, source_target_pairs={{0,5},{1,257},{2,103},{3,414},{4,260},{5,0},{6,107},{7,418},{8,13}... | collective-permute-start | bytes 196616 | tf_op jit(solution)/shard_map/ppermute | solution.py:201
  107.9 8.2 %collective-permute-start.17 = (f32[2,128,128]{2,1,0:T(8,128)S(1)}, f32[2,128,128]{2,1,0:T(8,128)S(1)}, u32[]{:S(2)}, u32[]{:S(2)}) collective-permute-start(f32[2,128,128]{2,1,0:T(8,128)S(1)} %shard_map.60.refs_0_), channel_id=1, source_target_pairs={{0,2},{1,3},{2,0},{3,1},{4,6},{5,7},{6,4},{7,5},{8,10},{9,11},{10,... | collective-permute-start | bytes 393224 | tf_op jit(solution)/shard_map/ppermute | solution.py:201
  109.8 11.6 %collective-permute-start.13 = (f32[4,128,128]{2,1,0:T(8,128)S(1)}, f32[4,128,128]{2,1,0:T(8,128)S(1)}, u32[]{:S(2)}, u32[]{:S(2)}) collective-permute-start(f32[4,128,128]{2,1,0:T(8,128)S(1)} %shard_map.59.refs_0_), channel_id=1, source_target_pairs={{0,1},{1,0},{2,3},{3,2},{4,5},{5,4},{6,7},{7,6},{8,9},{9,8},{10,11... | collective-permute-start | bytes 786440 | tf_op jit(solution)/shard_map/ppermute | solution.py:201
  111.7 11.0 %collective-permute-start.12 = (f32[4,128,128]{2,1,0:T(8,128)S(1)}, f32[4,128,128]{2,1,0:T(8,128)S(1)}, u32[]{:S(2)}, u32[]{:S(2)}) collective-permute-start(f32[4,128,128]{2,1,0:T(8,128)S(1)} %collective-permute-done.11.refs_2_), channel_id=1, source_target_pairs={{0,1},{1,0},{2,3},{3,2},{4,5},{5,4},{6,7},{7,6},{8,9},{9,8},{10,11... | collective-permute-start | bytes 786440 | tf_op jit(solution)/shard_map/ppermute | solution.py:201
  114.2 4.4 %collective-permute-start.16 = (f32[2,128,128]{2,1,0:T(8,128)S(1)}, f32[2,128,128]{2,1,0:T(8,128)S(1)}, u32[]{:S(2)}, u32[]{:S(2)}) collective-permute-start(f32[2,128,128]{2,1,0:T(8,128)S(1)} %shard_map.60.refs_0_), channel_id=1, source_target_pairs={{0,1},{1,0},{2,3},{3,2},{4,5},{5,4},{6,7},{7,6},{8,9},{9,8},{10,11... | collective-permute-start | bytes 393224 | tf_op jit(solution)/shard_map/ppermute | solution.py:201
  116.1 3.4 %collective-permute-start.18 = (f32[2,128,128]{2,1,0:T(8,128)S(1)}, f32[2,128,128]{2,1,0:T(8,128)S(1)}, u32[]{:S(2)}, u32[]{:S(2)}) collective-permute-start(f32[2,128,128]{2,1,0:T(8,128)S(1)} %collective-permute-done.17.refs_2_), channel_id=1, source_target_pairs={{0,1},{1,0},{2,3},{3,2},{4,5},{5,4},{6,7},{7,6},{8,9},{9,8},{10,11... | collective-permute-start | bytes 393224 | tf_op jit(solution)/shard_map/ppermute | solution.py:201

commit v3 on v2

--- a/solution.py
+++ b/solution.py
@@ -18,10 +18,11 @@
 PLACES = 6
 OFFSETS = np.array(
     [
-        [[2, 8, 3, 0, 51, 1], [-2, -8, -1, -7, -51, 64], [4, 6, 5, 7, 38, 25], [-4, -6, -3, -5, -38, -25]],
-        [[2, 8, 1, 7, 51, 64], [-2, -8, -3, 0, -51, -1], [4, 6, 3, 5, 38, 25], [-4, -6, -5, -7, -38, -25]],
+        [[4, 2, 5, 3, 51, 38], [-4, -2, -3, -1, -51, -38], [8, 6, 0, 7, 1, 25], [-8, -6, -7, -5, 64, -25]],
+        [[4, 2, 3, 1, 51, 38], [-4, -2, -5, -3, -51, -38], [8, 6, 7, 5, 64, 25], [-8, -6, 0, -7, -1, -25]],
     ]
 )
+SELF = int(np.argwhere(OFFSETS == 0)[0, 2])
 VMEM = pl.BlockSpec(memory_space=pltpu.VMEM)
 SMEM = pl.BlockSpec(memory_space=pltpu.SMEM)
 HBM = pl.BlockSpec(memory_space=pltpu.MemorySpace.HBM)
@@ -85,7 +86,7 @@
     total = jnp.zeros(out.shape, jnp.float32)
     for k in range(PLACES):
         x = column[k][...]
-        if k == SIDE_2:
+        if k == SELF:
             x = jnp.where(own_side[0] == 1, full[...], x)
         total = total + dot3(split(x), split(old[k]), ((1,), (1,)))
     out[...] = total
@@ -99,7 +100,7 @@
     turned = split(product.T)
     for k in range(PLACES):
         x = column[k][...]
-        if k == SIDE_2:
+        if k == SELF:
             x = jnp.where(own_side[0] == 1, full[...], x)
         tile = dot3(turned, split(x), ((1,), (0,)))
         if k in (SIDE_1, SIDE_2):
@@ -129,23 +130,37 @@
     on_self = own_side[0] == 1
     shape = out.shape[1:]
     unit = lax.broadcasted_iota(jnp.int32, shape, 0) == lax.broadcasted_iota(jnp.int32, shape, 1)
-    out[NEAR_1] = update(old[NEAR_1], near_1[...], got_1[0], samples)
-    out[NEAR_2] = update(old[NEAR_2], near_2[...], got_2[0], samples)
-    out[SIDE_1] = update(old[SIDE_1], side[0], got_1[1], samples)
-    theirs = jnp.where(on_self, side[1], got_2[1])
-    out[SIDE_2] = update(old[SIDE_2], side[1], theirs, samples, jnp.logical_and(unit, on_self))
+    corner = jnp.logical_and(unit, on_self)
+    ours = [near_1[...], near_2[...], side[0], side[1]]
+    theirs = [got_1[0], got_2[0], got_1[1], got_2[1]]
+    for k in NEAR_PLACES:
+        if k == SELF:
+            given = jnp.where(on_self, ours[k], theirs[k])
+            out[k] = update(old[k], ours[k], given, samples, corner)
+        else:
+            out[k] = update(old[k], ours[k], theirs[k], samples)
 
 
 NEAR_PLACES = (NEAR_1, NEAR_2, SIDE_1, SIDE_2)
 FAR_PLACES = (FAR_1, FAR_2)
 
 
-def place_kernel(groups, places, fill, slots, ids, counts, *refs):
-    n = len(groups)
-    if fill:
-        out, zero, sems, zero_sems = refs[n:]
-    else:
-        out, sems = refs[n + 1 :]
+def blank_kernel(counts, out, zero, sems):
+    zero[...] = jnp.zeros(zero.shape, jnp.float32)
+    slot_count = out.shape[0]
+    first = jnp.clip(counts[0], 0, slot_count)
+
+    @pl.loop(first, slot_count)
+    def _(s):
+        pltpu.make_async_copy(zero, out.at[s], sems.at[s]).start()
+
+    @pl.loop(first, slot_count)
+    def _(s):
+        pltpu.make_async_copy(zero, out.at[s], sems.at[s]).wait()
+
+
+def place_kernel(groups, places, slots, ids, *refs):
+    out, sems = refs[len(groups) + 1 :]
     found = []
     for g, j in enumerate(groups):
         for i, k in enumerate(places):
@@ -156,19 +171,6 @@
             found.append((slot >= 0, copy))
     for condition, copy in found:
         pl.when(condition)(copy.start)
-    if fill:
-        zero[...] = jnp.zeros(zero.shape, jnp.float32)
-        slot_count = out.shape[0]
-        first = jnp.clip(counts[0], 0, slot_count)
-
-        @pl.loop(first, slot_count)
-        def _(s):
-            pltpu.make_async_copy(zero, out.at[s], zero_sems.at[s]).start()
-
-        @pl.loop(first, slot_count)
-        def _(s):
-            pltpu.make_async_copy(zero, out.at[s], zero_sems.at[s]).wait()
-
     for condition, copy in found:
         pl.when(condition)(copy.wait)
 
@@ -220,7 +222,7 @@
 
     ids = jnp.stack([owner, member]).astype(jnp.int32)
     own_side = jnp.logical_or(
-        jnp.logical_and(owner % 2 == 0, member == 0), jnp.logical_and(owner % 2 == 1, member == 1)
+        jnp.logical_and(owner % 2 == 0, member == 2), jnp.logical_and(owner % 2 == 1, member == 3)
     ).astype(jnp.int32)[None]
     tile_shape = jax.ShapeDtypeStruct((block_size, block_size), f32)
     tiles_shape = jax.ShapeDtypeStruct((PLACES, block_size, block_size), f32)
@@ -318,26 +320,34 @@
     far_last = permute(far_across, core)
     near_last = permute(near_across, core)
 
+    new_omega = pl.pallas_call(
+        blank_kernel,
+        name="blank",
+        out_shape=tiles_of(slot_count),
+        in_specs=[SMEM],
+        out_specs=HBM,
+        scratch_shapes=[
+            pltpu.VMEM((block_size, block_size), f32),
+            pltpu.SemaphoreType.DMA((slot_count,)),
+        ],
+        compiler_params=PARAMS,
+        cost_estimate=cost(0, PLACES * tile_bytes),
+    )(counts)
+
     def place(groups, places, tiles, into):
-        fill = into is None
         n = len(groups)
-        sems = [pltpu.SemaphoreType.DMA((n * len(places),))]
-        if fill:
-            scratch = [pltpu.VMEM((block_size, block_size), f32)] + sems + [pltpu.SemaphoreType.DMA((slot_count,))]
-        else:
-            scratch = sems
         return pl.pallas_call(
-            functools.partial(place_kernel, groups, places, fill),
+            functools.partial(place_kernel, groups, places),
             out_shape=tiles_of(slot_count),
-            in_specs=[SMEM] * 3 + [VMEM] * n + ([] if fill else [HBM]),
+            in_specs=[SMEM] * 2 + [VMEM] * n + [HBM],
             out_specs=HBM,
-            input_output_aliases={} if fill else {3 + n: 0},
-            scratch_shapes=scratch,
+            input_output_aliases={2 + n: 0},
+            scratch_shapes=[pltpu.SemaphoreType.DMA((n * len(places),))],
             compiler_params=PARAMS,
             cost_estimate=cost(0, 2 * n * len(places) * tile_bytes),
-        )(slots, ids, counts, *tiles, *([] if fill else [into]))
-
-    new_omega = place((0, 1, 2, 3), FAR_PLACES, (far_tiles, far_mate, far_across, far_last), None)
+        )(slots, ids, *tiles, into)
+
+    new_omega = place((0, 1, 2, 3), FAR_PLACES, (far_tiles, far_mate, far_across, far_last), new_omega)
     new_omega = place((0, 1, 2), NEAR_PLACES, (near_tiles, near_mate, near_across), new_omega)
     new_omega = place((3,), NEAR_PLACES, (near_last,), new_omega)
     return (new_omega[None], y_product[None])

time: 126 us -> 130 us (1.032); the launches traced: 123 us -> 129 us
  starting transfers between devices: 62.6 us -> 74 us
  waiting for transfers between devices: 36.1 us -> 28.9 us
    ppermute x19, starting transfers between devices: 62.6 us -> 74 us  [permute(): return lax.ppermute(x, AXES, pairs)]
    ppermute x19, waiting for transfers between devices: 36.1 us -> 28.9 us  [permute(): return lax.ppermute(x, AXES, pairs)]
    pallas_call x3 -> x4, Pallas kernels: 3.85 us -> 5.06 us  [the longest x3 3.91 us: place(): pl.pallas_call(functools.partial(place_kernel, groups, places), out_shape...]
where the time goes in v3:
time: 130 us; the launch traced here: 129 us
  starting transfers between devices  74 us (57%)
  waiting for transfers between devices  28.9 us (22%)
  blocking collectives  13.8 us (11%)
  Pallas kernels  9.77 us (8%)
  between operations  1.62 us (1%)
    ppermute x19, starting transfers between devices, permute(): return lax.ppermute(x, AXES, pairs)  74 us
    ppermute x19, waiting for transfers between devices, permute(): return lax.ppermute(x, AXES, pairs)  28.9 us
    all_gather x1, blocking collectives, step(): full = lax.all_gather(own_dosage, 'team', axis=0, tiled=True)  13.8 us
    pallas_call x3, Pallas kernels, place(): pl.pallas_call(functools.partial(place_kernel, groups, places), out_shape...  3.91 us
  transfers between devices with their start and end apart: 19, of which 8 were waited for; matrix products, arithmetic and copies ran while one was open for 0% of the time, Pallas kernels for 5%

profile of v3, /device:TPU:1, one launch (start us, length us, event | category | flops | bytes accessed | tf_op | source)
XLA Modules:
  0.0 128.9 jit_solution(17990953471392395092)
XLA Ops:
  0.6 13.8 %all-gather = f32[1,256,128]{2,1,0:T(8,128)S(1)} all-gather(f32[1,64,128]{2,1,0:T(8,128)} %param.5), channel_id=2, replica_groups=mesh['blk'=128,'team'=4] {'team'}, dimensions={1}, use_global_device_ids=true | all-gather | bytes 163840 | tf_op jit(solution)/shard_map/all_gather | solution.py:242
  14.4 8.7 %collective-permute-start = (f32[256,128]{1,0:T(8,128)S(1)}, f32[256,128]{1,0:T(8,128)S(1)}, u32[]{:S(2)}, u32[]{:S(2)}) collective-permute-start(f32[256,128]{1,0:T(8,128)S(1)} %bitcast.9), channel_id=1, source_target_pairs={{0,17},{1,496},{2,35},{3,482},{4,21},{5,500},{6,39},{7,486},{8,25}... | collective-permute-start | bytes 393224 | tf_op jit(solution)/shard_map/ppermute | solution.py:203
  23.2 1.9 %collective-permute-start.1 = (f32[256,128]{1,0:T(8,128)S(1)}, f32[256,128]{1,0:T(8,128)S(1)}, u32[]{:S(2)}, u32[]{:S(2)}) collective-permute-start(f32[256,128]{1,0:T(8,128)S(1)} %bitcast.10), channel_id=1, source_target_pairs={{0,9},{1,504},{2,27},{3,490},{4,13},{5,508},{6,31},{7,494},{8,17},... | collective-permute-start | bytes 393224 | tf_op jit(solution)/shard_map/ppermute | solution.py:203
  25.1 7.4 %collective-permute-start.4 = (f32[256,128]{1,0:T(8,128)S(1)}, f32[256,128]{1,0:T(8,128)S(1)}, u32[]{:S(2)}, u32[]{:S(2)}) collective-permute-start(f32[256,128]{1,0:T(8,128)S(1)} %bitcast.11), channel_id=1, source_target_pairs={{0,205},{1,308},{2,7},{3,259},{4,209},{5,312},{6,262},{7,2},{8,213... | collective-permute-start | bytes 393224 | tf_op jit(solution)/shard_map/ppermute | solution.py:203
  32.5 3.9 %collective-permute-start.5 = (f32[256,128]{1,0:T(8,128)S(1)}, f32[256,128]{1,0:T(8,128)S(1)}, u32[]{:S(2)}, u32[]{:S(2)}) collective-permute-start(f32[256,128]{1,0:T(8,128)S(1)} %bitcast.12), channel_id=1, source_target_pairs={{0,153},{1,360},{2,103},{3,414},{4,157},{5,364},{6,107},{7,418},{8... | collective-permute-start | bytes 393224 | tf_op jit(solution)/shard_map/ppermute | solution.py:203
  36.4 3.8 %collective-permute-start.2 = (f32[256,128]{1,0:T(8,128)S(1)}, f32[256,128]{1,0:T(8,128)S(1)}, u32[]{:S(2)}, u32[]{:S(2)}) collective-permute-start(f32[256,128]{1,0:T(8,128)S(1)} %collective-permute-done.refs_0_), channel_id=1, source_target_pairs={{0,4},{1,5},{2,6},{3,7},{4,0},{5,1},{6,2},{7,3},{8,12},{9,13},{10,... | collective-permute-start | bytes 393224 | tf_op jit(solution)/shard_map/ppermute | solution.py:203
  40.2 4.7 %collective-permute-start.3 = (f32[256,128]{1,0:T(8,128)S(1)}, f32[256,128]{1,0:T(8,128)S(1)}, u32[]{:S(2)}, u32[]{:S(2)}) collective-permute-start(f32[256,128]{1,0:T(8,128)S(1)} %collective-permute-done.1.refs_1_), channel_id=1, source_target_pairs={{0,4},{1,5},{2,6},{3,7},{4,0},{5,1},{6,2},{7,3},{8,12},{9,13},{10,... | collective-permute-start | bytes 393224 | tf_op jit(solution)/shard_map/ppermute | solution.py:203
  46.3 2.3 %pick.1 = (s32[24]{0:T(128)S(1)}, f32[6,128,128]{2,1,0:T(8,128)S(1)}) custom-call(s32[2]{0:T(128)S(1)} %pad_add_fusion.ids, s32[1,24]{1,0:T(1,128)S(1)} %copy-done, s32[1]{0:T(128)S(6)} %copy.12.counts, f32[24,128,128]{2,1,0:T(8,128)} %bitcast.18), custom_call_target="tpu_custom_call" | custom-call | bytes 786432 | tf_op jit(solution)/shard_map/pick/pallas_call | solution.py:231
  49.4 3.9 %collective-permute-start.6 = (f32[256,128]{1,0:T(8,128)S(1)}, f32[256,128]{1,0:T(8,128)S(1)}, u32[]{:S(2)}, u32[]{:S(2)}) collective-permute-start(f32[256,128]{1,0:T(8,128)S(1)} %partial.1), channel_id=1, source_target_pairs={{0,1},{1,0},{2,3},{3,2},{4,5},{5,4},{6,7},{7,6},{8,9},{9,8},{10,11... | collective-permute-start | bytes 393224 | tf_op jit(solution)/shard_map/ppermute | solution.py:203
  53.3 1.0 collective-permute-done.6
  54.3 1.9 %collective-permute-start.7 = (f32[256,128]{1,0:T(8,128)S(1)}, f32[256,128]{1,0:T(8,128)S(1)}, u32[]{:S(2)}, u32[]{:S(2)}) collective-permute-start(f32[256,128]{1,0:T(8,128)S(1)} %add.9.half), channel_id=1, source_target_pairs={{0,2},{1,3},{2,0},{3,1},{4,6},{5,7},{6,4},{7,5},{8,10},{9,11},{10,... | collective-permute-start | bytes 393224 | tf_op jit(solution)/shard_map/ppermute | solution.py:203
  56.3 6.2 %collective-permute-done.7.other = f32[256,128]{1,0:T(8,128)S(1)} collective-permute-done((f32[256,128]{1,0:T(8,128)S(1)}, f32[256,128]{1,0:T(8,128)S(1)}, u32[]{:S(2)}, u32[]{:S(2)}) %collective-permute-start.7) | collective-permute-done | bytes 131104 | tf_op jit(solution)/shard_map/ppermute | solution.py:203
  62.4 1.6 %tiles.1 = (f32[128,128]{1,0:T(8,128)S(1)}, f32[128,128]{1,0:T(8,128)S(1)}, f32[2,128,128]{2,1,0:T(8,128)S(1)}, f32[128,128]{1,0:T(8,128)S(1)}, f32[128,128]{1,0:T(8,128)S(1)}, /*index=5*/f32[64,128]{1,0:T(8,128)}) custom-call(s32[1]{0:T(128)} %bitcast.3.own_side, s32[2]{0:T(128)S(1)} %pad_add_fusion.ids, f32[256,128]{1,0:T(8,128)S(1)} %add.9.half, ...), custom_call_target="tpu_custom_call" | custom-call | flops 50331648 | bytes 1835008 | tf_op jit(solution)/shard_map/tiles/pallas_call | solution.py:263
  64.0 2.5 %collective-permute-start.8 = (f32[2,128,128]{2,1,0:T(8,128)S(1)}, f32[2,128,128]{2,1,0:T(8,128)S(1)}, u32[]{:S(2)}, u32[]{:S(2)}) collective-permute-start(f32[2,128,128]{2,1,0:T(8,128)S(1)} %get-tuple-element.14.side), channel_id=1, source_target_pairs={{0,4},{1,5},{2,6},{3,7},{4,0},{5,1},{6,2},{7,3},{8,12},{9,13},{10,... | collective-permute-start | bytes 393224 | tf_op jit(solution)/shard_map/ppermute | solution.py:203
  66.6 3.2 %collective-permute-done.8 = f32[2,128,128]{2,1,0:T(8,128)S(1)} collective-permute-done((f32[2,128,128]{2,1,0:T(8,128)S(1)}, f32[2,128,128]{2,1,0:T(8,128)S(1)}, u32[]{:S(2)}, u32[]{:S(2)}) %collective-permute-start.8) | collective-permute-done | bytes 131104 | tf_op jit(solution)/shard_map/ppermute | solution.py:203
  69.8 8.0 %collective-permute-start.10 = (f32[2,128,128]{2,1,0:T(8,128)S(1)}, f32[2,128,128]{2,1,0:T(8,128)S(1)}, u32[]{:S(2)}, u32[]{:S(2)}) collective-permute-start(f32[2,128,128]{2,1,0:T(8,128)S(1)} %pad_maximum_fusion.1), channel_id=1, source_target_pairs={{0,9},{1,504},{2,27},{3,490},{4,13},{5,508},{6,31},{7,494},{8,17},... | collective-permute-start | bytes 393224 | tf_op jit(solution)/shard_map/ppermute | solution.py:203
  77.8 1.9 %collective-permute-start.9 = (f32[2,128,128]{2,1,0:T(8,128)S(1)}, f32[2,128,128]{2,1,0:T(8,128)S(1)}, u32[]{:S(2)}, u32[]{:S(2)}) collective-permute-start(f32[2,128,128]{2,1,0:T(8,128)S(1)} %pad_maximum_fusion), channel_id=1, source_target_pairs={{0,17},{1,496},{2,35},{3,482},{4,21},{5,500},{6,39},{7,486},{8,25}... | collective-permute-start | bytes 393224 | tf_op jit(solution)/shard_map/ppermute | solution.py:203
  80.4 7.9 %collective-permute-done.9.got_1 = f32[2,128,128]{2,1,0:T(8,128)S(1)} collective-permute-done((f32[2,128,128]{2,1,0:T(8,128)S(1)}, f32[2,128,128]{2,1,0:T(8,128)S(1)}, u32[]{:S(2)}, u32[]{:S(2)}) %collective-permute-start.9) | collective-permute-done | bytes 131104 | tf_op jit(solution)/shard_map/ppermute | solution.py:203
  88.5 5.9 %collective-permute-start.11 = (f32[4,128,128]{2,1,0:T(8,128)S(1)}, f32[4,128,128]{2,1,0:T(8,128)S(1)}, u32[]{:S(2)}, u32[]{:S(2)}) collective-permute-start(f32[4,128,128]{2,1,0:T(8,128)S(1)} %shard_map.59.refs_0_), channel_id=1, source_target_pairs={{0,2},{1,3},{2,0},{3,1},{4,6},{5,7},{6,4},{7,5},{8,10},{9,11},{10,... | collective-permute-start | bytes 786440 | tf_op jit(solution)/shard_map/ppermute | solution.py:203
  94.4 6.2 %collective-permute-start.14 = (f32[128,128]{1,0:T(8,128)S(1)}, f32[128,128]{1,0:T(8,128)S(1)}, u32[]{:S(2)}, u32[]{:S(2)}) collective-permute-start(f32[128,128]{1,0:T(8,128)S(1)} %get-tuple-element.15.far_1), channel_id=1, source_target_pairs={{0,205},{1,308},{2,7},{3,259},{4,209},{5,312},{6,262},{7,2},{8,213... | collective-permute-start | bytes 196616 | tf_op jit(solution)/shard_map/ppermute | solution.py:203
  100.6 2.7 %collective-permute-start.15 = (f32[128,128]{1,0:T(8,128)S(1)}, f32[128,128]{1,0:T(8,128)S(1)}, u32[]{:S(2)}, u32[]{:S(2)}) collective-permute-start(f32[128,128]{1,0:T(8,128)S(1)} %get-tuple-element.16.far_2), channel_id=1, source_target_pairs={{0,153},{1,360},{2,103},{3,414},{4,157},{5,364},{6,107},{7,418},{8... | collective-permute-start | bytes 196616 | tf_op jit(solution)/shard_map/ppermute | solution.py:203
  103.2 6.0 %collective-permute-done.14.got_1 = f32[128,128]{1,0:T(8,128)S(1)} collective-permute-done((f32[128,128]{1,0:T(8,128)S(1)}, f32[128,128]{1,0:T(8,128)S(1)}, u32[]{:S(2)}, u32[]{:S(2)}) %collective-permute-start.14) | collective-permute-done | bytes 65568 | tf_op jit(solution)/shard_map/ppermute | solution.py:203
  109.2 3.8 %collective-permute-done.15.got_2 = f32[128,128]{1,0:T(8,128)S(1)} collective-permute-done((f32[128,128]{1,0:T(8,128)S(1)}, f32[128,128]{1,0:T(8,128)S(1)}, u32[]{:S(2)}, u32[]{:S(2)}) %collective-permute-start.15) | collective-permute-done | bytes 65568 | tf_op jit(solution)/shard_map/ppermute | solution.py:203
  113.1 1.9 %collective-permute-start.17 = (f32[2,128,128]{2,1,0:T(8,128)S(1)}, f32[2,128,128]{2,1,0:T(8,128)S(1)}, u32[]{:S(2)}, u32[]{:S(2)}) collective-permute-start(f32[2,128,128]{2,1,0:T(8,128)S(1)} %shard_map.60.refs_0_), channel_id=1, source_target_pairs={{0,2},{1,3},{2,0},{3,1},{4,6},{5,7},{6,4},{7,5},{8,10},{9,11},{10,... | collective-permute-start | bytes 393224 | tf_op jit(solution)/shard_map/ppermute | solution.py:203
  115.0 1.9 %collective-permute-start.13 = (f32[4,128,128]{2,1,0:T(8,128)S(1)}, f32[4,128,128]{2,1,0:T(8,128)S(1)}, u32[]{:S(2)}, u32[]{:S(2)}) collective-permute-start(f32[4,128,128]{2,1,0:T(8,128)S(1)} %shard_map.59.refs_0_), channel_id=1, source_target_pairs={{0,1},{1,0},{2,3},{3,2},{4,5},{5,4},{6,7},{7,6},{8,9},{9,8},{10,11... | collective-permute-start | bytes 786440 | tf_op jit(solution)/shard_map/ppermute | solution.py:203
  117.0 2.4 %collective-permute-start.12 = (f32[4,128,128]{2,1,0:T(8,128)S(1)}, f32[4,128,128]{2,1,0:T(8,128)S(1)}, u32[]{:S(2)}, u32[]{:S(2)}) collective-permute-start(f32[4,128,128]{2,1,0:T(8,128)S(1)} %collective-permute-done.11.refs_2_), channel_id=1, source_target_pairs={{0,1},{1,0},{2,3},{3,2},{4,5},{5,4},{6,7},{7,6},{8,9},{9,8},{10,11... | collective-permute-start | bytes 786440 | tf_op jit(solution)/shard_map/ppermute | solution.py:203
  119.4 1.9 %collective-permute-start.16 = (f32[2,128,128]{2,1,0:T(8,128)S(1)}, f32[2,128,128]{2,1,0:T(8,128)S(1)}, u32[]{:S(2)}, u32[]{:S(2)}) collective-permute-start(f32[2,128,128]{2,1,0:T(8,128)S(1)} %shard_map.60.refs_0_), channel_id=1, source_target_pairs={{0,1},{1,0},{2,3},{3,2},{4,5},{5,4},{6,7},{7,6},{8,9},{9,8},{10,11... | collective-permute-start | bytes 393224 | tf_op jit(solution)/shard_map/ppermute | solution.py:203
  121.3 2.4 %collective-permute-start.18 = (f32[2,128,128]{2,1,0:T(8,128)S(1)}, f32[2,128,128]{2,1,0:T(8,128)S(1)}, u32[]{:S(2)}, u32[]{:S(2)}) collective-permute-start(f32[2,128,128]{2,1,0:T(8,128)S(1)} %collective-permute-done.17.refs_2_), channel_id=1, source_target_pairs={{0,1},{1,0},{2,3},{3,2},{4,5},{5,4},{6,7},{7,6},{8,9},{9,8},{10,11... | collective-permute-start | bytes 393224 | tf_op jit(solution)/shard_map/ppermute | solution.py:203
  123.7 1.1 blank.1.refs_4_
  124.9 1.4 %shard_map.61.refs_3_ = f32[24,128,128]{2,1,0:T(8,128)} custom-call(s32[24]{0:T(128)S(1)} %get-tuple-element.10.slots, s32[2]{0:T(128)S(1)} %pad_add_fusion.ids, f32[2,128,128]{2,1,0:T(8,128)S(1)} %shard_map.60.refs_0_, f32[2,128,128]{2,1,0:T(8,128)S(1)} %collective-permute-done.16.refs_1_, ...), custom_call_target="tpu_custom_call", output_to_operand_aliasing={{}: (6, {})} | custom-call | bytes 1048576 | tf_op jit(solution)/shard_map/pallas_call | solution.py:339
  126.3 1.3 %shard_map.62.refs_1_ = f32[24,128,128]{2,1,0:T(8,128)} custom-call(s32[24]{0:T(128)S(1)} %get-tuple-element.10.slots, s32[2]{0:T(128)S(1)} %pad_add_fusion.ids, f32[4,128,128]{2,1,0:T(8,128)S(1)} %shard_map.59.refs_0_, f32[4,128,128]{2,1,0:T(8,128)S(1)} %collective-permute-done.13.refs_1_, ...), custom_call_target="tpu_custom_call", output_to_operand_aliasing={{}: (5, {})} | custom-call | bytes 1572864 | tf_op jit(solution)/shard_map/pallas_call | solution.py:339
  127.6 1.2 shard_map.63
  (23 shorter events, 2.5 us)
Async XLA Ops:
  14.4 21.9 %collective-permute-start = (f32[256,128]{1,0:T(8,128)S(1)}, f32[256,128]{1,0:T(8,128)S(1)}, u32[]{:S(2)}, u32[]{:S(2)}) collective-permute-start(f32[256,128]{1,0:T(8,128)S(1)} %bitcast.9), channel_id=1, source_target_pairs={{0,17},{1,496},{2,35},{3,482},{4,21},{5,500},{6,39},{7,486},{8,25}... | collective-permute-start | bytes 393224 | tf_op jit(solution)/shard_map/ppermute | solution.py:203
  23.2 17.1 %collective-permute-start.1 = (f32[256,128]{1,0:T(8,128)S(1)}, f32[256,128]{1,0:T(8,128)S(1)}, u32[]{:S(2)}, u32[]{:S(2)}) collective-permute-start(f32[256,128]{1,0:T(8,128)S(1)} %bitcast.10), channel_id=1, source_target_pairs={{0,9},{1,504},{2,27},{3,490},{4,13},{5,508},{6,31},{7,494},{8,17},... | collective-permute-start | bytes 393224 | tf_op jit(solution)/shard_map/ppermute | solution.py:203
  25.1 23.6 %collective-permute-start.4 = (f32[256,128]{1,0:T(8,128)S(1)}, f32[256,128]{1,0:T(8,128)S(1)}, u32[]{:S(2)}, u32[]{:S(2)}) collective-permute-start(f32[256,128]{1,0:T(8,128)S(1)} %bitcast.11), channel_id=1, source_target_pairs={{0,205},{1,308},{2,7},{3,259},{4,209},{5,312},{6,262},{7,2},{8,213... | collective-permute-start | bytes 393224 | tf_op jit(solution)/shard_map/ppermute | solution.py:203
  32.5 16.2 %collective-permute-start.5 = (f32[256,128]{1,0:T(8,128)S(1)}, f32[256,128]{1,0:T(8,128)S(1)}, u32[]{:S(2)}, u32[]{:S(2)}) collective-permute-start(f32[256,128]{1,0:T(8,128)S(1)} %bitcast.12), channel_id=1, source_target_pairs={{0,153},{1,360},{2,103},{3,414},{4,157},{5,364},{6,107},{7,418},{8... | collective-permute-start | bytes 393224 | tf_op jit(solution)/shard_map/ppermute | solution.py:203
  36.4 12.3 %collective-permute-start.2 = (f32[256,128]{1,0:T(8,128)S(1)}, f32[256,128]{1,0:T(8,128)S(1)}, u32[]{:S(2)}, u32[]{:S(2)}) collective-permute-start(f32[256,128]{1,0:T(8,128)S(1)} %collective-permute-done.refs_0_), channel_id=1, source_target_pairs={{0,4},{1,5},{2,6},{3,7},{4,0},{5,1},{6,2},{7,3},{8,12},{9,13},{10,... | collective-permute-start | bytes 393224 | tf_op jit(solution)/shard_map/ppermute | solution.py:203
  40.2 8.7 %collective-permute-start.3 = (f32[256,128]{1,0:T(8,128)S(1)}, f32[256,128]{1,0:T(8,128)S(1)}, u32[]{:S(2)}, u32[]{:S(2)}) collective-permute-start(f32[256,128]{1,0:T(8,128)S(1)} %collective-permute-done.1.refs_1_), channel_id=1, source_target_pairs={{0,4},{1,5},{2,6},{3,7},{4,0},{5,1},{6,2},{7,3},{8,12},{9,13},{10,... | collective-permute-start | bytes 393224 | tf_op jit(solution)/shard_map/ppermute | solution.py:203
  45.6 0.7 copy-start
  49.4 4.9 %collective-permute-start.6 = (f32[256,128]{1,0:T(8,128)S(1)}, f32[256,128]{1,0:T(8,128)S(1)}, u32[]{:S(2)}, u32[]{:S(2)}) collective-permute-start(f32[256,128]{1,0:T(8,128)S(1)} %partial.1), channel_id=1, source_target_pairs={{0,1},{1,0},{2,3},{3,2},{4,5},{5,4},{6,7},{7,6},{8,9},{9,8},{10,11... | collective-permute-start | bytes 393224 | tf_op jit(solution)/shard_map/ppermute | solution.py:203
  54.3 8.1 %collective-permute-start.7 = (f32[256,128]{1,0:T(8,128)S(1)}, f32[256,128]{1,0:T(8,128)S(1)}, u32[]{:S(2)}, u32[]{:S(2)}) collective-permute-start(f32[256,128]{1,0:T(8,128)S(1)} %add.9.half), channel_id=1, source_target_pairs={{0,2},{1,3},{2,0},{3,1},{4,6},{5,7},{6,4},{7,5},{8,10},{9,11},{10,... | collective-permute-start | bytes 393224 | tf_op jit(solution)/shard_map/ppermute | solution.py:203
  64.0 5.7 %collective-permute-start.8 = (f32[2,128,128]{2,1,0:T(8,128)S(1)}, f32[2,128,128]{2,1,0:T(8,128)S(1)}, u32[]{:S(2)}, u32[]{:S(2)}) collective-permute-start(f32[2,128,128]{2,1,0:T(8,128)S(1)} %get-tuple-element.14.side), channel_id=1, source_target_pairs={{0,4},{1,5},{2,6},{3,7},{4,0},{5,1},{6,2},{7,3},{8,12},{9,13},{10,... | collective-permute-start | bytes 393224 | tf_op jit(solution)/shard_map/ppermute | solution.py:203
  69.8 10.7 %collective-permute-start.10 = (f32[2,128,128]{2,1,0:T(8,128)S(1)}, f32[2,128,128]{2,1,0:T(8,128)S(1)}, u32[]{:S(2)}, u32[]{:S(2)}) collective-permute-start(f32[2,128,128]{2,1,0:T(8,128)S(1)} %pad_maximum_fusion.1), channel_id=1, source_target_pairs={{0,9},{1,504},{2,27},{3,490},{4,13},{5,508},{6,31},{7,494},{8,17},... | collective-permute-start | bytes 393224 | tf_op jit(solution)/shard_map/ppermute | solution.py:203
  77.8 10.5 %collective-permute-start.9 = (f32[2,128,128]{2,1,0:T(8,128)S(1)}, f32[2,128,128]{2,1,0:T(8,128)S(1)}, u32[]{:S(2)}, u32[]{:S(2)}) collective-permute-start(f32[2,128,128]{2,1,0:T(8,128)S(1)} %pad_maximum_fusion), channel_id=1, source_target_pairs={{0,17},{1,496},{2,35},{3,482},{4,21},{5,500},{6,39},{7,486},{8,25}... | collective-permute-start | bytes 393224 | tf_op jit(solution)/shard_map/ppermute | solution.py:203
  88.5 28.5 %collective-permute-start.11 = (f32[4,128,128]{2,1,0:T(8,128)S(1)}, f32[4,128,128]{2,1,0:T(8,128)S(1)}, u32[]{:S(2)}, u32[]{:S(2)}) collective-permute-start(f32[4,128,128]{2,1,0:T(8,128)S(1)} %shard_map.59.refs_0_), channel_id=1, source_target_pairs={{0,2},{1,3},{2,0},{3,1},{4,6},{5,7},{6,4},{7,5},{8,10},{9,11},{10,... | collective-permute-start | bytes 786440 | tf_op jit(solution)/shard_map/ppermute | solution.py:203
  94.4 14.8 %collective-permute-start.14 = (f32[128,128]{1,0:T(8,128)S(1)}, f32[128,128]{1,0:T(8,128)S(1)}, u32[]{:S(2)}, u32[]{:S(2)}) collective-permute-start(f32[128,128]{1,0:T(8,128)S(1)} %get-tuple-element.15.far_1), channel_id=1, source_target_pairs={{0,205},{1,308},{2,7},{3,259},{4,209},{5,312},{6,262},{7,2},{8,213... | collective-permute-start | bytes 196616 | tf_op jit(solution)/shard_map/ppermute | solution.py:203
  100.6 12.4 %collective-permute-start.15 = (f32[128,128]{1,0:T(8,128)S(1)}, f32[128,128]{1,0:T(8,128)S(1)}, u32[]{:S(2)}, u32[]{:S(2)}) collective-permute-start(f32[128,128]{1,0:T(8,128)S(1)} %get-tuple-element.16.far_2), channel_id=1, source_target_pairs={{0,153},{1,360},{2,103},{3,414},{4,157},{5,364},{6,107},{7,418},{8... | collective-permute-start | bytes 196616 | tf_op jit(solution)/shard_map/ppermute | solution.py:203
  113.1 8.2 %collective-permute-start.17 = (f32[2,128,128]{2,1,0:T(8,128)S(1)}, f32[2,128,128]{2,1,0:T(8,128)S(1)}, u32[]{:S(2)}, u32[]{:S(2)}) collective-permute-start(f32[2,128,128]{2,1,0:T(8,128)S(1)} %shard_map.60.refs_0_), channel_id=1, source_target_pairs={{0,2},{1,3},{2,0},{3,1},{4,6},{5,7},{6,4},{7,5},{8,10},{9,11},{10,... | collective-permute-start | bytes 393224 | tf_op jit(solution)/shard_map/ppermute | solution.py:203
  115.0 11.3 %collective-permute-start.13 = (f32[4,128,128]{2,1,0:T(8,128)S(1)}, f32[4,128,128]{2,1,0:T(8,128)S(1)}, u32[]{:S(2)}, u32[]{:S(2)}) collective-permute-start(f32[4,128,128]{2,1,0:T(8,128)S(1)} %shard_map.59.refs_0_), channel_id=1, source_target_pairs={{0,1},{1,0},{2,3},{3,2},{4,5},{5,4},{6,7},{7,6},{8,9},{9,8},{10,11... | collective-permute-start | bytes 786440 | tf_op jit(solution)/shard_map/ppermute | solution.py:203
  117.0 10.7 %collective-permute-start.12 = (f32[4,128,128]{2,1,0:T(8,128)S(1)}, f32[4,128,128]{2,1,0:T(8,128)S(1)}, u32[]{:S(2)}, u32[]{:S(2)}) collective-permute-start(f32[4,128,128]{2,1,0:T(8,128)S(1)} %collective-permute-done.11.refs_2_), channel_id=1, source_target_pairs={{0,1},{1,0},{2,3},{3,2},{4,5},{5,4},{6,7},{7,6},{8,9},{9,8},{10,11... | collective-permute-start | bytes 786440 | tf_op jit(solution)/shard_map/ppermute | solution.py:203
  119.4 5.5 %collective-permute-start.16 = (f32[2,128,128]{2,1,0:T(8,128)S(1)}, f32[2,128,128]{2,1,0:T(8,128)S(1)}, u32[]{:S(2)}, u32[]{:S(2)}) collective-permute-start(f32[2,128,128]{2,1,0:T(8,128)S(1)} %shard_map.60.refs_0_), channel_id=1, source_target_pairs={{0,1},{1,0},{2,3},{3,2},{4,5},{5,4},{6,7},{7,6},{8,9},{9,8},{10,11... | collective-permute-start | bytes 393224 | tf_op jit(solution)/shard_map/ppermute | solution.py:203
  121.3 3.6 %collective-permute-start.18 = (f32[2,128,128]{2,1,0:T(8,128)S(1)}, f32[2,128,128]{2,1,0:T(8,128)S(1)}, u32[]{:S(2)}, u32[]{:S(2)}) collective-permute-start(f32[2,128,128]{2,1,0:T(8,128)S(1)} %collective-permute-done.17.refs_2_), channel_id=1, source_target_pairs={{0,1},{1,0},{2,3},{3,2},{4,5},{5,4},{6,7},{7,6},{8,9},{9,8},{10,11... | collective-permute-start | bytes 393224 | tf_op jit(solution)/shard_map/ppermute | solution.py:203

commit v4 on v3

--- a/solution.py
+++ b/solution.py
@@ -16,13 +16,28 @@
 AXES = ("blk", "team")
 NEAR_1, NEAR_2, SIDE_1, SIDE_2, FAR_1, FAR_2 = range(6)
 PLACES = 6
-OFFSETS = np.array(
-    [
-        [[4, 2, 5, 3, 51, 38], [-4, -2, -3, -1, -51, -38], [8, 6, 0, 7, 1, 25], [-8, -6, -7, -5, 64, -25]],
-        [[4, 2, 3, 1, 51, 38], [-4, -2, -5, -3, -51, -38], [8, 6, 7, 5, 64, 25], [-8, -6, 0, -7, -1, -25]],
-    ]
-)
-SELF = int(np.argwhere(OFFSETS == 0)[0, 2])
+NEAR = ((4, 2), (8, 6))
+FAR = ((51, 38), (0, 25))
+
+
+def offsets(near, far):
+    table = np.zeros((2, 4, PLACES), int)
+    for parity in range(2):
+        for t in range(4):
+            sign = 1 - 2 * (t % 2)
+            for i in range(2):
+                near_by = sign * near[t // 2][i]
+                side = near_by + 1 - 2 * parity
+                distant = sign * far[t // 2][i]
+                if distant == 0:
+                    distant = 1 - 2 * parity if parity == t % 2 else 64
+                table[parity, t, i] = near_by
+                table[parity, t, 2 + i] = 0 if abs(side) == 9 else side
+                table[parity, t, 4 + i] = distant
+    return table
+
+
+OFFSETS = offsets(NEAR, FAR)
 VMEM = pl.BlockSpec(memory_space=pltpu.VMEM)
 SMEM = pl.BlockSpec(memory_space=pltpu.SMEM)
 HBM = pl.BlockSpec(memory_space=pltpu.MemorySpace.HBM)
@@ -40,11 +55,11 @@
     return one(a[0], b[0]) + (one(a[0], b[1]) + one(a[1], b[0]))
 
 
-def pick_kernel(rows, ids, columns, counts, omega, slots, old, sems):
+def pick_kernel(rows, offset_table, ids, columns, counts, omega, slots, old, sems):
     owner, member = ids[0], ids[1]
     count = counts[0]
     parity = lax.rem(owner, 2)
-    choices = np.mod(OFFSETS, rows).reshape(2, -1)
+    choices = np.mod(np.array(offset_table), rows).reshape(2, -1)
     total = choices.shape[1]
     slot_count = columns.shape[1]
     wanted = [jnp.where(parity == 0, int(choices[0, i]), int(choices[1, i])) for i in range(total)]
@@ -81,28 +96,41 @@
             pltpu.make_async_copy(omega.at[slot], old.at[k], sems.at[k]).wait()
 
 
-def partial_kernel(own_side, old, full, *refs):
+def partial_kernel(self_place, own_side, old, full, *refs):
     column, out = refs[:PLACES], refs[PLACES]
     total = jnp.zeros(out.shape, jnp.float32)
     for k in range(PLACES):
         x = column[k][...]
-        if k == SELF:
+        if k == self_place:
             x = jnp.where(own_side[0] == 1, full[...], x)
         total = total + dot3(split(x), split(old[k]), ((1,), (1,)))
     out[...] = total
 
 
-def tile_kernel(own_side, ids, half, other, full, *refs):
-    column = refs[:PLACES]
-    near_1, near_2, side, far_1, far_2, y_out = refs[PLACES:]
-    product = half[...] + other[...]
-    samples_here = y_out.shape[0]
-    turned = split(product.T)
+def turn_kernel(self_place, own_side, full, *refs):
+    column, (high, low) = refs[:PLACES], refs[PLACES:]
+    block_size = full.shape[1]
     for k in range(PLACES):
         x = column[k][...]
-        if k == SELF:
+        if k == self_place:
             x = jnp.where(own_side[0] == 1, full[...], x)
-        tile = dot3(turned, split(x), ((1,), (0,)))
+        here = pl.ds(k * block_size, block_size)
+        high[here, :], low[here, :] = split(x.T)
+
+
+def tile_kernel(ids, half, other, high, low, *outs):
+    near_1, near_2, side, far_1, far_2, y_out = outs
+    samples_here, block_size = y_out.shape
+    product_high, product_low = split(half[...] + other[...])
+
+    def one(x, y):
+        return jnp.dot(x, y, preferred_element_type=jnp.float32)
+
+    both = one(high[...], jnp.concatenate([product_high, product_low], axis=1))
+    rest = one(low[...], product_high)
+    tiles = both[:, :block_size] + (both[:, block_size:] + rest)
+    for k in range(PLACES):
+        tile = tiles[k * block_size : (k + 1) * block_size]
         if k in (SIDE_1, SIDE_2):
             side[k - SIDE_1] = tile
         else:
@@ -112,7 +140,7 @@
 
 
 def update(before, ours, theirs, samples, corner=None):
-    grad = (ours + theirs.T) / (2.0 * samples)
+    grad = (ours.T + theirs) / (2.0 * samples)
     if corner is not None:
         grad = grad - jnp.where(corner, 1.0 / jnp.where(corner, before, 1.0), 0.0)
     moved = before - step_size * grad
@@ -126,7 +154,7 @@
     out[1] = update(old[FAR_2], far_2[...], got_2[...], samples)
 
 
-def update_near_kernel(samples, own_side, old, near_1, near_2, side, got_1, got_2, out):
+def update_near_kernel(self_place, samples, own_side, old, near_1, near_2, side, got_1, got_2, out):
     on_self = own_side[0] == 1
     shape = out.shape[1:]
     unit = lax.broadcasted_iota(jnp.int32, shape, 0) == lax.broadcasted_iota(jnp.int32, shape, 1)
@@ -134,7 +162,7 @@
     ours = [near_1[...], near_2[...], side[0], side[1]]
     theirs = [got_1[0], got_2[0], got_1[1], got_2[1]]
     for k in NEAR_PLACES:
-        if k == SELF:
+        if k == self_place:
             given = jnp.where(on_self, ours[k], theirs[k])
             out[k] = update(old[k], ours[k], given, samples, corner)
         else:
@@ -221,15 +249,16 @@
         return b ^ 1, t
 
     ids = jnp.stack([owner, member]).astype(jnp.int32)
-    own_side = jnp.logical_or(
-        jnp.logical_and(owner % 2 == 0, member == 2), jnp.logical_and(owner % 2 == 1, member == 3)
-    ).astype(jnp.int32)[None]
+    table = tuple(tuple(map(tuple, half.tolist())) for half in OFFSETS)
+    self_even, self_odd = np.argwhere(OFFSETS == 0).tolist()
+    self_place = self_even[2]
+    own_side = (member == jnp.where(owner % 2 == 0, self_even[1], self_odd[1])).astype(jnp.int32)[None]
     tile_shape = jax.ShapeDtypeStruct((block_size, block_size), f32)
     tiles_shape = jax.ShapeDtypeStruct((PLACES, block_size, block_size), f32)
     tile_bytes = block_size * block_size * 4
 
     slots, old = pl.pallas_call(
-        functools.partial(pick_kernel, rows),
+        functools.partial(pick_kernel, rows, table),
         name="pick",
         out_shape=(jax.ShapeDtypeStruct((team * PLACES,), jnp.int32), tiles_shape),
         in_specs=[SMEM, SMEM, SMEM, HBM],
@@ -249,7 +278,7 @@
     column[SIDE_1] = permute(column[NEAR_1], beside)
 
     partial = pl.pallas_call(
-        partial_kernel,
+        functools.partial(partial_kernel, self_place),
         name="partial",
         out_shape=jax.ShapeDtypeStruct((samples, block_size), f32),
         in_specs=[SMEM] + [VMEM] * (2 + PLACES),
@@ -260,6 +289,16 @@
     half = partial + permute(partial, lambda b, t: (b, t ^ 1))
     other = permute(half, lambda b, t: (b, t ^ 2))
 
+    turned = jax.ShapeDtypeStruct((PLACES * block_size, samples), jnp.bfloat16)
+    high, low = pl.pallas_call(
+        functools.partial(turn_kernel, self_place),
+        name="turn",
+        out_shape=(turned, turned),
+        in_specs=[SMEM] + [VMEM] * (1 + PLACES),
+        out_specs=(VMEM, VMEM),
+        compiler_params=PARAMS,
+        cost_estimate=cost(0, 14 * samples * block_size * 4),
+    )(own_side, full, *column)
     near_1, near_2, side, far_1, far_2, y_product = pl.pallas_call(
         tile_kernel,
         name="tiles",
@@ -271,11 +310,11 @@
             tile_shape,
             jax.ShapeDtypeStruct((samples_here, block_size), f32),
         ),
-        in_specs=[SMEM, SMEM] + [VMEM] * (3 + PLACES),
+        in_specs=[SMEM] + [VMEM] * 4,
         out_specs=(VMEM,) * 6,
         compiler_params=PARAMS,
         cost_estimate=cost(2 * PLACES * samples * block_size**2, 14 * samples * block_size * 4),
-    )(own_side, ids, half, other, full, *column)
+    )(ids, half, other, high, low)
 
     handed = permute(side, beside)
 
@@ -304,7 +343,7 @@
         functools.partial(update_far_kernel, samples), tiles_of(2), [VMEM] * 5, 8 * tile_bytes
     )(old, far_1, far_2, got_far_1, got_far_2)
     near_tiles = kernel(
-        functools.partial(update_near_kernel, samples), tiles_of(4), [SMEM] + [VMEM] * 6, 16 * tile_bytes
+        functools.partial(update_near_kernel, self_place, samples), tiles_of(4), [SMEM] + [VMEM] * 6, 16 * tile_bytes
     )(own_side, old, near_1, near_2, side, got_1, got_2)
 
     def chip(b, t):

time: 130 us -> 130 us (level)
    pallas_call x3 -> x4, Pallas kernels: 2.99 us -> 3.27 us  [the longest x1 2.35 us: step(): pl.pallas_call(functools.partial(pick_kernel, rows, table), name='pick',...]
where the time goes in v4:
time: 130 us; the launch traced here: 129 us
  starting transfers between devices  74 us (57%)
  waiting for transfers between devices  28.6 us (22%)
  blocking collectives  13.8 us (11%)
  Pallas kernels  9.9 us (8%)
  between operations  1.62 us (1%)
    ppermute x19, starting transfers between devices, permute(): return lax.ppermute(x, AXES, pairs)  74 us
    ppermute x19, waiting for transfers between devices, permute(): return lax.ppermute(x, AXES, pairs)  28.6 us
    all_gather x1, blocking collectives, step(): full = lax.all_gather(own_dosage, 'team', axis=0, tiled=True)  13.8 us
    pallas_call x3, Pallas kernels, place(): pl.pallas_call(functools.partial(place_kernel, groups, places), out_shape...  3.91 us
  transfers between devices with their start and end apart: 19, of which 8 were waited for; matrix products, arithmetic and copies ran while one was open for 0% of the time, Pallas kernels for 5%

profile of v4, /device:TPU:1, one launch (start us, length us, event | category | flops | bytes accessed | tf_op | source)
XLA Modules:
  0.0 128.7 jit_solution(17591316889057428465)
XLA Ops:
  0.6 13.8 %all-gather = f32[1,256,128]{2,1,0:T(8,128)S(1)} all-gather(f32[1,64,128]{2,1,0:T(8,128)} %param.5), channel_id=2, replica_groups=mesh['blk'=128,'team'=4] {'team'}, dimensions={1}, use_global_device_ids=true | all-gather | bytes 163840 | tf_op jit(solution)/shard_map/all_gather | solution.py:271
  14.4 8.7 %collective-permute-start = (f32[256,128]{1,0:T(8,128)S(1)}, f32[256,128]{1,0:T(8,128)S(1)}, u32[]{:S(2)}, u32[]{:S(2)}) collective-permute-start(f32[256,128]{1,0:T(8,128)S(1)} %bitcast.9), channel_id=1, source_target_pairs={{0,17},{1,496},{2,35},{3,482},{4,21},{5,500},{6,39},{7,486},{8,25}... | collective-permute-start | bytes 393224 | tf_op jit(solution)/shard_map/ppermute | solution.py:231
  23.2 1.9 %collective-permute-start.1 = (f32[256,128]{1,0:T(8,128)S(1)}, f32[256,128]{1,0:T(8,128)S(1)}, u32[]{:S(2)}, u32[]{:S(2)}) collective-permute-start(f32[256,128]{1,0:T(8,128)S(1)} %bitcast.10), channel_id=1, source_target_pairs={{0,9},{1,504},{2,27},{3,490},{4,13},{5,508},{6,31},{7,494},{8,17},... | collective-permute-start | bytes 393224 | tf_op jit(solution)/shard_map/ppermute | solution.py:231
  25.1 7.4 %collective-permute-start.4 = (f32[256,128]{1,0:T(8,128)S(1)}, f32[256,128]{1,0:T(8,128)S(1)}, u32[]{:S(2)}, u32[]{:S(2)}) collective-permute-start(f32[256,128]{1,0:T(8,128)S(1)} %bitcast.11), channel_id=1, source_target_pairs={{0,205},{1,308},{2,7},{3,259},{4,209},{5,312},{6,262},{7,2},{8,213... | collective-permute-start | bytes 393224 | tf_op jit(solution)/shard_map/ppermute | solution.py:231
  32.5 3.9 %collective-permute-start.5 = (f32[256,128]{1,0:T(8,128)S(1)}, f32[256,128]{1,0:T(8,128)S(1)}, u32[]{:S(2)}, u32[]{:S(2)}) collective-permute-start(f32[256,128]{1,0:T(8,128)S(1)} %bitcast.12), channel_id=1, source_target_pairs={{0,153},{1,360},{2,103},{3,414},{4,157},{5,364},{6,107},{7,418},{8... | collective-permute-start | bytes 393224 | tf_op jit(solution)/shard_map/ppermute | solution.py:231
  36.4 3.8 %collective-permute-start.2 = (f32[256,128]{1,0:T(8,128)S(1)}, f32[256,128]{1,0:T(8,128)S(1)}, u32[]{:S(2)}, u32[]{:S(2)}) collective-permute-start(f32[256,128]{1,0:T(8,128)S(1)} %collective-permute-done.refs_0_), channel_id=1, source_target_pairs={{0,4},{1,5},{2,6},{3,7},{4,0},{5,1},{6,2},{7,3},{8,12},{9,13},{10,... | collective-permute-start | bytes 393224 | tf_op jit(solution)/shard_map/ppermute | solution.py:231
  40.2 4.7 %collective-permute-start.3 = (f32[256,128]{1,0:T(8,128)S(1)}, f32[256,128]{1,0:T(8,128)S(1)}, u32[]{:S(2)}, u32[]{:S(2)}) collective-permute-start(f32[256,128]{1,0:T(8,128)S(1)} %collective-permute-done.1.refs_1_), channel_id=1, source_target_pairs={{0,4},{1,5},{2,6},{3,7},{4,0},{5,1},{6,2},{7,3},{8,12},{9,13},{10,... | collective-permute-start | bytes 393224 | tf_op jit(solution)/shard_map/ppermute | solution.py:231
  46.3 2.3 %pick.1 = (s32[24]{0:T(128)S(1)}, f32[6,128,128]{2,1,0:T(8,128)S(1)}) custom-call(s32[2]{0:T(128)S(1)} %pad_add_fusion.ids, s32[1,24]{1,0:T(1,128)S(1)} %copy-done, s32[1]{0:T(128)S(6)} %copy.12.counts, f32[24,128,128]{2,1,0:T(8,128)} %bitcast.18), custom_call_target="tpu_custom_call" | custom-call | bytes 786432 | tf_op jit(solution)/shard_map/pick/pallas_call | solution.py:260
  49.4 3.9 %collective-permute-start.6 = (f32[256,128]{1,0:T(8,128)S(1)}, f32[256,128]{1,0:T(8,128)S(1)}, u32[]{:S(2)}, u32[]{:S(2)}) collective-permute-start(f32[256,128]{1,0:T(8,128)S(1)} %partial.1), channel_id=1, source_target_pairs={{0,1},{1,0},{2,3},{3,2},{4,5},{5,4},{6,7},{7,6},{8,9},{9,8},{10,11... | collective-permute-start | bytes 393224 | tf_op jit(solution)/shard_map/ppermute | solution.py:231
  53.3 1.0 collective-permute-done.6
  54.3 1.9 %collective-permute-start.7 = (f32[256,128]{1,0:T(8,128)S(1)}, f32[256,128]{1,0:T(8,128)S(1)}, u32[]{:S(2)}, u32[]{:S(2)}) collective-permute-start(f32[256,128]{1,0:T(8,128)S(1)} %add.8.half), channel_id=1, source_target_pairs={{0,2},{1,3},{2,0},{3,1},{4,6},{5,7},{6,4},{7,5},{8,10},{9,11},{10,... | collective-permute-start | bytes 393224 | tf_op jit(solution)/shard_map/ppermute | solution.py:231
  56.5 5.9 %collective-permute-done.7.other = f32[256,128]{1,0:T(8,128)S(1)} collective-permute-done((f32[256,128]{1,0:T(8,128)S(1)}, f32[256,128]{1,0:T(8,128)S(1)}, u32[]{:S(2)}, u32[]{:S(2)}) %collective-permute-start.7) | collective-permute-done | bytes 131104 | tf_op jit(solution)/shard_map/ppermute | solution.py:231
  62.4 1.5 %tiles.1 = (f32[128,128]{1,0:T(8,128)S(1)}, f32[128,128]{1,0:T(8,128)S(1)}, f32[2,128,128]{2,1,0:T(8,128)S(1)}, f32[128,128]{1,0:T(8,128)S(1)}, f32[128,128]{1,0:T(8,128)S(1)}, /*index=5*/f32[64,128]{1,0:T(8,128)}) custom-call(s32[2]{0:T(128)S(1)} %pad_add_fusion.ids, f32[256,128]{1,0:T(8,128)S(1)} %add.8.half, f32[256,128]{1,0:T(8,128)S(1)} %collective-permute-done.7.other, ...), custom_call_target="tpu_custom_call" | custom-call | flops 50331648 | bytes 1835008 | tf_op jit(solution)/shard_map/tiles/pallas_call | solution.py:302
  63.9 2.5 %collective-permute-start.8 = (f32[2,128,128]{2,1,0:T(8,128)S(1)}, f32[2,128,128]{2,1,0:T(8,128)S(1)}, u32[]{:S(2)}, u32[]{:S(2)}) collective-permute-start(f32[2,128,128]{2,1,0:T(8,128)S(1)} %get-tuple-element.18.side), channel_id=1, source_target_pairs={{0,4},{1,5},{2,6},{3,7},{4,0},{5,1},{6,2},{7,3},{8,12},{9,13},{10,... | collective-permute-start | bytes 393224 | tf_op jit(solution)/shard_map/ppermute | solution.py:231
  66.4 3.2 %collective-permute-done.8 = f32[2,128,128]{2,1,0:T(8,128)S(1)} collective-permute-done((f32[2,128,128]{2,1,0:T(8,128)S(1)}, f32[2,128,128]{2,1,0:T(8,128)S(1)}, u32[]{:S(2)}, u32[]{:S(2)}) %collective-permute-start.8) | collective-permute-done | bytes 131104 | tf_op jit(solution)/shard_map/ppermute | solution.py:231
  69.6 8.0 %collective-permute-start.10 = (f32[2,128,128]{2,1,0:T(8,128)S(1)}, f32[2,128,128]{2,1,0:T(8,128)S(1)}, u32[]{:S(2)}, u32[]{:S(2)}) collective-permute-start(f32[2,128,128]{2,1,0:T(8,128)S(1)} %pad_maximum_fusion.1), channel_id=1, source_target_pairs={{0,9},{1,504},{2,27},{3,490},{4,13},{5,508},{6,31},{7,494},{8,17},... | collective-permute-start | bytes 393224 | tf_op jit(solution)/shard_map/ppermute | solution.py:231
  77.7 1.9 %collective-permute-start.9 = (f32[2,128,128]{2,1,0:T(8,128)S(1)}, f32[2,128,128]{2,1,0:T(8,128)S(1)}, u32[]{:S(2)}, u32[]{:S(2)}) collective-permute-start(f32[2,128,128]{2,1,0:T(8,128)S(1)} %pad_maximum_fusion), channel_id=1, source_target_pairs={{0,17},{1,496},{2,35},{3,482},{4,21},{5,500},{6,39},{7,486},{8,25}... | collective-permute-start | bytes 393224 | tf_op jit(solution)/shard_map/ppermute | solution.py:231
  80.3 7.9 %collective-permute-done.9.got_1 = f32[2,128,128]{2,1,0:T(8,128)S(1)} collective-permute-done((f32[2,128,128]{2,1,0:T(8,128)S(1)}, f32[2,128,128]{2,1,0:T(8,128)S(1)}, u32[]{:S(2)}, u32[]{:S(2)}) %collective-permute-start.9) | collective-permute-done | bytes 131104 | tf_op jit(solution)/shard_map/ppermute | solution.py:231
  88.3 5.9 %collective-permute-start.11 = (f32[4,128,128]{2,1,0:T(8,128)S(1)}, f32[4,128,128]{2,1,0:T(8,128)S(1)}, u32[]{:S(2)}, u32[]{:S(2)}) collective-permute-start(f32[4,128,128]{2,1,0:T(8,128)S(1)} %shard_map.59.refs_0_), channel_id=1, source_target_pairs={{0,2},{1,3},{2,0},{3,1},{4,6},{5,7},{6,4},{7,5},{8,10},{9,11},{10,... | collective-permute-start | bytes 786440 | tf_op jit(solution)/shard_map/ppermute | solution.py:231
  94.3 6.2 %collective-permute-start.14 = (f32[128,128]{1,0:T(8,128)S(1)}, f32[128,128]{1,0:T(8,128)S(1)}, u32[]{:S(2)}, u32[]{:S(2)}) collective-permute-start(f32[128,128]{1,0:T(8,128)S(1)} %get-tuple-element.19.far_1), channel_id=1, source_target_pairs={{0,205},{1,308},{2,7},{3,259},{4,209},{5,312},{6,262},{7,2},{8,213... | collective-permute-start | bytes 196616 | tf_op jit(solution)/shard_map/ppermute | solution.py:231
  100.4 2.7 %collective-permute-start.15 = (f32[128,128]{1,0:T(8,128)S(1)}, f32[128,128]{1,0:T(8,128)S(1)}, u32[]{:S(2)}, u32[]{:S(2)}) collective-permute-start(f32[128,128]{1,0:T(8,128)S(1)} %get-tuple-element.20.far_2), channel_id=1, source_target_pairs={{0,153},{1,360},{2,103},{3,414},{4,157},{5,364},{6,107},{7,418},{8... | collective-permute-start | bytes 196616 | tf_op jit(solution)/shard_map/ppermute | solution.py:231
  103.1 6.0 %collective-permute-done.14.got_1 = f32[128,128]{1,0:T(8,128)S(1)} collective-permute-done((f32[128,128]{1,0:T(8,128)S(1)}, f32[128,128]{1,0:T(8,128)S(1)}, u32[]{:S(2)}, u32[]{:S(2)}) %collective-permute-start.14) | collective-permute-done | bytes 65568 | tf_op jit(solution)/shard_map/ppermute | solution.py:231
  109.1 3.7 %collective-permute-done.15.got_2 = f32[128,128]{1,0:T(8,128)S(1)} collective-permute-done((f32[128,128]{1,0:T(8,128)S(1)}, f32[128,128]{1,0:T(8,128)S(1)}, u32[]{:S(2)}, u32[]{:S(2)}) %collective-permute-start.15) | collective-permute-done | bytes 65568 | tf_op jit(solution)/shard_map/ppermute | solution.py:231
  112.9 1.9 %collective-permute-start.17 = (f32[2,128,128]{2,1,0:T(8,128)S(1)}, f32[2,128,128]{2,1,0:T(8,128)S(1)}, u32[]{:S(2)}, u32[]{:S(2)}) collective-permute-start(f32[2,128,128]{2,1,0:T(8,128)S(1)} %shard_map.60.refs_0_), channel_id=1, source_target_pairs={{0,2},{1,3},{2,0},{3,1},{4,6},{5,7},{6,4},{7,5},{8,10},{9,11},{10,... | collective-permute-start | bytes 393224 | tf_op jit(solution)/shard_map/ppermute | solution.py:231
  114.9 1.9 %collective-permute-start.13 = (f32[4,128,128]{2,1,0:T(8,128)S(1)}, f32[4,128,128]{2,1,0:T(8,128)S(1)}, u32[]{:S(2)}, u32[]{:S(2)}) collective-permute-start(f32[4,128,128]{2,1,0:T(8,128)S(1)} %shard_map.59.refs_0_), channel_id=1, source_target_pairs={{0,1},{1,0},{2,3},{3,2},{4,5},{5,4},{6,7},{7,6},{8,9},{9,8},{10,11... | collective-permute-start | bytes 786440 | tf_op jit(solution)/shard_map/ppermute | solution.py:231
  116.8 2.4 %collective-permute-start.12 = (f32[4,128,128]{2,1,0:T(8,128)S(1)}, f32[4,128,128]{2,1,0:T(8,128)S(1)}, u32[]{:S(2)}, u32[]{:S(2)}) collective-permute-start(f32[4,128,128]{2,1,0:T(8,128)S(1)} %collective-permute-done.11.refs_2_), channel_id=1, source_target_pairs={{0,1},{1,0},{2,3},{3,2},{4,5},{5,4},{6,7},{7,6},{8,9},{9,8},{10,11... | collective-permute-start | bytes 786440 | tf_op jit(solution)/shard_map/ppermute | solution.py:231
  119.2 1.9 %collective-permute-start.16 = (f32[2,128,128]{2,1,0:T(8,128)S(1)}, f32[2,128,128]{2,1,0:T(8,128)S(1)}, u32[]{:S(2)}, u32[]{:S(2)}) collective-permute-start(f32[2,128,128]{2,1,0:T(8,128)S(1)} %shard_map.60.refs_0_), channel_id=1, source_target_pairs={{0,1},{1,0},{2,3},{3,2},{4,5},{5,4},{6,7},{7,6},{8,9},{9,8},{10,11... | collective-permute-start | bytes 393224 | tf_op jit(solution)/shard_map/ppermute | solution.py:231
  121.2 2.4 %collective-permute-start.18 = (f32[2,128,128]{2,1,0:T(8,128)S(1)}, f32[2,128,128]{2,1,0:T(8,128)S(1)}, u32[]{:S(2)}, u32[]{:S(2)}) collective-permute-start(f32[2,128,128]{2,1,0:T(8,128)S(1)} %collective-permute-done.17.refs_2_), channel_id=1, source_target_pairs={{0,1},{1,0},{2,3},{3,2},{4,5},{5,4},{6,7},{7,6},{8,9},{9,8},{10,11... | collective-permute-start | bytes 393224 | tf_op jit(solution)/shard_map/ppermute | solution.py:231
  123.6 1.1 blank.1.refs_4_
  124.8 1.4 %shard_map.61.refs_3_ = f32[24,128,128]{2,1,0:T(8,128)} custom-call(s32[24]{0:T(128)S(1)} %get-tuple-element.12.slots, s32[2]{0:T(128)S(1)} %pad_add_fusion.ids, f32[2,128,128]{2,1,0:T(8,128)S(1)} %shard_map.60.refs_0_, f32[2,128,128]{2,1,0:T(8,128)S(1)} %collective-permute-done.16.refs_1_, ...), custom_call_target="tpu_custom_call", output_to_operand_aliasing={{}: (6, {})} | custom-call | bytes 1048576 | tf_op jit(solution)/shard_map/pallas_call | solution.py:378
  126.2 1.3 %shard_map.62.refs_1_ = f32[24,128,128]{2,1,0:T(8,128)} custom-call(s32[24]{0:T(128)S(1)} %get-tuple-element.12.slots, s32[2]{0:T(128)S(1)} %pad_add_fusion.ids, f32[4,128,128]{2,1,0:T(8,128)S(1)} %shard_map.59.refs_0_, f32[4,128,128]{2,1,0:T(8,128)S(1)} %collective-permute-done.13.refs_1_, ...), custom_call_target="tpu_custom_call", output_to_operand_aliasing={{}: (5, {})} | custom-call | bytes 1572864 | tf_op jit(solution)/shard_map/pallas_call | solution.py:378
  127.5 1.2 shard_map.63
  (24 shorter events, 2.8 us)
Async XLA Ops:
  14.4 21.9 %collective-permute-start = (f32[256,128]{1,0:T(8,128)S(1)}, f32[256,128]{1,0:T(8,128)S(1)}, u32[]{:S(2)}, u32[]{:S(2)}) collective-permute-start(f32[256,128]{1,0:T(8,128)S(1)} %bitcast.9), channel_id=1, source_target_pairs={{0,17},{1,496},{2,35},{3,482},{4,21},{5,500},{6,39},{7,486},{8,25}... | collective-permute-start | bytes 393224 | tf_op jit(solution)/shard_map/ppermute | solution.py:231
  23.2 17.1 %collective-permute-start.1 = (f32[256,128]{1,0:T(8,128)S(1)}, f32[256,128]{1,0:T(8,128)S(1)}, u32[]{:S(2)}, u32[]{:S(2)}) collective-permute-start(f32[256,128]{1,0:T(8,128)S(1)} %bitcast.10), channel_id=1, source_target_pairs={{0,9},{1,504},{2,27},{3,490},{4,13},{5,508},{6,31},{7,494},{8,17},... | collective-permute-start | bytes 393224 | tf_op jit(solution)/shard_map/ppermute | solution.py:231
  25.1 23.6 %collective-permute-start.4 = (f32[256,128]{1,0:T(8,128)S(1)}, f32[256,128]{1,0:T(8,128)S(1)}, u32[]{:S(2)}, u32[]{:S(2)}) collective-permute-start(f32[256,128]{1,0:T(8,128)S(1)} %bitcast.11), channel_id=1, source_target_pairs={{0,205},{1,308},{2,7},{3,259},{4,209},{5,312},{6,262},{7,2},{8,213... | collective-permute-start | bytes 393224 | tf_op jit(solution)/shard_map/ppermute | solution.py:231
  32.5 16.2 %collective-permute-start.5 = (f32[256,128]{1,0:T(8,128)S(1)}, f32[256,128]{1,0:T(8,128)S(1)}, u32[]{:S(2)}, u32[]{:S(2)}) collective-permute-start(f32[256,128]{1,0:T(8,128)S(1)} %bitcast.12), channel_id=1, source_target_pairs={{0,153},{1,360},{2,103},{3,414},{4,157},{5,364},{6,107},{7,418},{8... | collective-permute-start | bytes 393224 | tf_op jit(solution)/shard_map/ppermute | solution.py:231
  36.4 12.3 %collective-permute-start.2 = (f32[256,128]{1,0:T(8,128)S(1)}, f32[256,128]{1,0:T(8,128)S(1)}, u32[]{:S(2)}, u32[]{:S(2)}) collective-permute-start(f32[256,128]{1,0:T(8,128)S(1)} %collective-permute-done.refs_0_), channel_id=1, source_target_pairs={{0,4},{1,5},{2,6},{3,7},{4,0},{5,1},{6,2},{7,3},{8,12},{9,13},{10,... | collective-permute-start | bytes 393224 | tf_op jit(solution)/shard_map/ppermute | solution.py:231
  40.2 8.7 %collective-permute-start.3 = (f32[256,128]{1,0:T(8,128)S(1)}, f32[256,128]{1,0:T(8,128)S(1)}, u32[]{:S(2)}, u32[]{:S(2)}) collective-permute-start(f32[256,128]{1,0:T(8,128)S(1)} %collective-permute-done.1.refs_1_), channel_id=1, source_target_pairs={{0,4},{1,5},{2,6},{3,7},{4,0},{5,1},{6,2},{7,3},{8,12},{9,13},{10,... | collective-permute-start | bytes 393224 | tf_op jit(solution)/shard_map/ppermute | solution.py:231
  45.6 0.7 copy-start
  49.4 4.9 %collective-permute-start.6 = (f32[256,128]{1,0:T(8,128)S(1)}, f32[256,128]{1,0:T(8,128)S(1)}, u32[]{:S(2)}, u32[]{:S(2)}) collective-permute-start(f32[256,128]{1,0:T(8,128)S(1)} %partial.1), channel_id=1, source_target_pairs={{0,1},{1,0},{2,3},{3,2},{4,5},{5,4},{6,7},{7,6},{8,9},{9,8},{10,11... | collective-permute-start | bytes 393224 | tf_op jit(solution)/shard_map/ppermute | solution.py:231
  54.3 8.1 %collective-permute-start.7 = (f32[256,128]{1,0:T(8,128)S(1)}, f32[256,128]{1,0:T(8,128)S(1)}, u32[]{:S(2)}, u32[]{:S(2)}) collective-permute-start(f32[256,128]{1,0:T(8,128)S(1)} %add.8.half), channel_id=1, source_target_pairs={{0,2},{1,3},{2,0},{3,1},{4,6},{5,7},{6,4},{7,5},{8,10},{9,11},{10,... | collective-permute-start | bytes 393224 | tf_op jit(solution)/shard_map/ppermute | solution.py:231
  63.9 5.7 %collective-permute-start.8 = (f32[2,128,128]{2,1,0:T(8,128)S(1)}, f32[2,128,128]{2,1,0:T(8,128)S(1)}, u32[]{:S(2)}, u32[]{:S(2)}) collective-permute-start(f32[2,128,128]{2,1,0:T(8,128)S(1)} %get-tuple-element.18.side), channel_id=1, source_target_pairs={{0,4},{1,5},{2,6},{3,7},{4,0},{5,1},{6,2},{7,3},{8,12},{9,13},{10,... | collective-permute-start | bytes 393224 | tf_op jit(solution)/shard_map/ppermute | solution.py:231
  69.6 10.7 %collective-permute-start.10 = (f32[2,128,128]{2,1,0:T(8,128)S(1)}, f32[2,128,128]{2,1,0:T(8,128)S(1)}, u32[]{:S(2)}, u32[]{:S(2)}) collective-permute-start(f32[2,128,128]{2,1,0:T(8,128)S(1)} %pad_maximum_fusion.1), channel_id=1, source_target_pairs={{0,9},{1,504},{2,27},{3,490},{4,13},{5,508},{6,31},{7,494},{8,17},... | collective-permute-start | bytes 393224 | tf_op jit(solution)/shard_map/ppermute | solution.py:231
  77.7 10.5 %collective-permute-start.9 = (f32[2,128,128]{2,1,0:T(8,128)S(1)}, f32[2,128,128]{2,1,0:T(8,128)S(1)}, u32[]{:S(2)}, u32[]{:S(2)}) collective-permute-start(f32[2,128,128]{2,1,0:T(8,128)S(1)} %pad_maximum_fusion), channel_id=1, source_target_pairs={{0,17},{1,496},{2,35},{3,482},{4,21},{5,500},{6,39},{7,486},{8,25}... | collective-permute-start | bytes 393224 | tf_op jit(solution)/shard_map/ppermute | solution.py:231
  88.3 28.5 %collective-permute-start.11 = (f32[4,128,128]{2,1,0:T(8,128)S(1)}, f32[4,128,128]{2,1,0:T(8,128)S(1)}, u32[]{:S(2)}, u32[]{:S(2)}) collective-permute-start(f32[4,128,128]{2,1,0:T(8,128)S(1)} %shard_map.59.refs_0_), channel_id=1, source_target_pairs={{0,2},{1,3},{2,0},{3,1},{4,6},{5,7},{6,4},{7,5},{8,10},{9,11},{10,... | collective-permute-start | bytes 786440 | tf_op jit(solution)/shard_map/ppermute | solution.py:231
  94.3 14.9 %collective-permute-start.14 = (f32[128,128]{1,0:T(8,128)S(1)}, f32[128,128]{1,0:T(8,128)S(1)}, u32[]{:S(2)}, u32[]{:S(2)}) collective-permute-start(f32[128,128]{1,0:T(8,128)S(1)} %get-tuple-element.19.far_1), channel_id=1, source_target_pairs={{0,205},{1,308},{2,7},{3,259},{4,209},{5,312},{6,262},{7,2},{8,213... | collective-permute-start | bytes 196616 | tf_op jit(solution)/shard_map/ppermute | solution.py:231
  100.4 12.4 %collective-permute-start.15 = (f32[128,128]{1,0:T(8,128)S(1)}, f32[128,128]{1,0:T(8,128)S(1)}, u32[]{:S(2)}, u32[]{:S(2)}) collective-permute-start(f32[128,128]{1,0:T(8,128)S(1)} %get-tuple-element.20.far_2), channel_id=1, source_target_pairs={{0,153},{1,360},{2,103},{3,414},{4,157},{5,364},{6,107},{7,418},{8... | collective-permute-start | bytes 196616 | tf_op jit(solution)/shard_map/ppermute | solution.py:231
  112.9 8.2 %collective-permute-start.17 = (f32[2,128,128]{2,1,0:T(8,128)S(1)}, f32[2,128,128]{2,1,0:T(8,128)S(1)}, u32[]{:S(2)}, u32[]{:S(2)}) collective-permute-start(f32[2,128,128]{2,1,0:T(8,128)S(1)} %shard_map.60.refs_0_), channel_id=1, source_target_pairs={{0,2},{1,3},{2,0},{3,1},{4,6},{5,7},{6,4},{7,5},{8,10},{9,11},{10,... | collective-permute-start | bytes 393224 | tf_op jit(solution)/shard_map/ppermute | solution.py:231
  114.9 11.3 %collective-permute-start.13 = (f32[4,128,128]{2,1,0:T(8,128)S(1)}, f32[4,128,128]{2,1,0:T(8,128)S(1)}, u32[]{:S(2)}, u32[]{:S(2)}) collective-permute-start(f32[4,128,128]{2,1,0:T(8,128)S(1)} %shard_map.59.refs_0_), channel_id=1, source_target_pairs={{0,1},{1,0},{2,3},{3,2},{4,5},{5,4},{6,7},{7,6},{8,9},{9,8},{10,11... | collective-permute-start | bytes 786440 | tf_op jit(solution)/shard_map/ppermute | solution.py:231
  116.8 10.7 %collective-permute-start.12 = (f32[4,128,128]{2,1,0:T(8,128)S(1)}, f32[4,128,128]{2,1,0:T(8,128)S(1)}, u32[]{:S(2)}, u32[]{:S(2)}) collective-permute-start(f32[4,128,128]{2,1,0:T(8,128)S(1)} %collective-permute-done.11.refs_2_), channel_id=1, source_target_pairs={{0,1},{1,0},{2,3},{3,2},{4,5},{5,4},{6,7},{7,6},{8,9},{9,8},{10,11... | collective-permute-start | bytes 786440 | tf_op jit(solution)/shard_map/ppermute | solution.py:231
  119.2 5.5 %collective-permute-start.16 = (f32[2,128,128]{2,1,0:T(8,128)S(1)}, f32[2,128,128]{2,1,0:T(8,128)S(1)}, u32[]{:S(2)}, u32[]{:S(2)}) collective-permute-start(f32[2,128,128]{2,1,0:T(8,128)S(1)} %shard_map.60.refs_0_), channel_id=1, source_target_pairs={{0,1},{1,0},{2,3},{3,2},{4,5},{5,4},{6,7},{7,6},{8,9},{9,8},{10,11... | collective-permute-start | bytes 393224 | tf_op jit(solution)/shard_map/ppermute | solution.py:231
  121.2 3.6 %collective-permute-start.18 = (f32[2,128,128]{2,1,0:T(8,128)S(1)}, f32[2,128,128]{2,1,0:T(8,128)S(1)}, u32[]{:S(2)}, u32[]{:S(2)}) collective-permute-start(f32[2,128,128]{2,1,0:T(8,128)S(1)} %collective-permute-done.17.refs_2_), channel_id=1, source_target_pairs={{0,1},{1,0},{2,3},{3,2},{4,5},{5,4},{6,7},{7,6},{8,9},{9,8},{10,11... | collective-permute-start | bytes 393224 | tf_op jit(solution)/shard_map/ppermute | solution.py:231

commit v5 on v4

--- a/solution.py
+++ b/solution.py
@@ -149,9 +149,13 @@
     return shrunk if corner is None else jnp.where(corner, moved, shrunk)
 
 
-def update_far_kernel(samples, old, far_1, far_2, got_1, got_2, out):
-    out[0] = update(old[FAR_1], far_1[...], got_1[...], samples)
-    out[1] = update(old[FAR_2], far_2[...], got_2[...], samples)
+def update_far_kernel(samples, old, far_1, far_2, got_1, got_2, near, far, every):
+    far[0] = update(old[FAR_1], far_1[...], got_1[...], samples)
+    far[1] = update(old[FAR_2], far_2[...], got_2[...], samples)
+    for k in NEAR_PLACES:
+        every[k] = near[k]
+    for i, k in enumerate(FAR_PLACES):
+        every[k] = far[i]
 
 
 def update_near_kernel(self_place, samples, own_side, old, near_1, near_2, side, got_1, got_2, out):
@@ -187,14 +191,14 @@
         pltpu.make_async_copy(zero, out.at[s], sems.at[s]).wait()
 
 
-def place_kernel(groups, places, slots, ids, *refs):
+def place_kernel(groups, slots, ids, *refs):
     out, sems = refs[len(groups) + 1 :]
     found = []
-    for g, j in enumerate(groups):
+    for (j, places), tiles in zip(groups, refs):
         for i, k in enumerate(places):
             slot = slots[lax.bitwise_xor(ids[1], j) * PLACES + k]
             copy = pltpu.make_async_copy(
-                refs[g].at[i], out.at[jnp.maximum(slot, 0)], sems.at[g * len(places) + i]
+                tiles.at[i], out.at[jnp.maximum(slot, 0)], sems.at[len(found)]
             )
             found.append((slot >= 0, copy))
     for condition, copy in found:
@@ -326,25 +330,27 @@
     got_2 = back(jnp.stack([near_2, handed[1]]), NEAR_2)
     got_1 = back(jnp.stack([near_1, handed[0]]), NEAR_1)
 
-    def kernel(function, out_shape, in_specs, nbytes):
-        return pl.pallas_call(
-            function,
-            out_shape=out_shape,
-            in_specs=in_specs,
-            out_specs=VMEM,
-            compiler_params=PARAMS,
-            cost_estimate=cost(0, nbytes),
-        )
-
     def tiles_of(count):
         return jax.ShapeDtypeStruct((count, block_size, block_size), f32)
 
-    far_tiles = kernel(
-        functools.partial(update_far_kernel, samples), tiles_of(2), [VMEM] * 5, 8 * tile_bytes
-    )(old, far_1, far_2, got_far_1, got_far_2)
-    near_tiles = kernel(
-        functools.partial(update_near_kernel, self_place, samples), tiles_of(4), [SMEM] + [VMEM] * 6, 16 * tile_bytes
+    near_tiles = pl.pallas_call(
+        functools.partial(update_near_kernel, self_place, samples),
+        name="update_near",
+        out_shape=tiles_of(4),
+        in_specs=[SMEM] + [VMEM] * 6,
+        out_specs=VMEM,
+        compiler_params=PARAMS,
+        cost_estimate=cost(0, 16 * tile_bytes),
     )(own_side, old, near_1, near_2, side, got_1, got_2)
+    far_tiles, all_tiles = pl.pallas_call(
+        functools.partial(update_far_kernel, samples),
+        name="update_far",
+        out_shape=(tiles_of(2), tiles_of(PLACES)),
+        in_specs=[VMEM] * 6,
+        out_specs=(VMEM, VMEM),
+        compiler_params=PARAMS,
+        cost_estimate=cost(0, 16 * tile_bytes),
+    )(old, far_1, far_2, got_far_1, got_far_2, near_tiles)
 
     def chip(b, t):
         return b, t ^ 2
@@ -352,12 +358,11 @@
     def core(b, t):
         return b, t ^ 1
 
+    near_across = permute(near_tiles, chip)
     far_across = permute(far_tiles, chip)
-    far_mate = permute(far_tiles, core)
-    near_across = permute(near_tiles, chip)
-    near_mate = permute(near_tiles, core)
+    mate = permute(all_tiles, core)
+    near_last = permute(near_across, core)
     far_last = permute(far_across, core)
-    near_last = permute(near_across, core)
 
     new_omega = pl.pallas_call(
         blank_kernel,
@@ -373,22 +378,25 @@
         cost_estimate=cost(0, PLACES * tile_bytes),
     )(counts)
 
-    def place(groups, places, tiles, into):
+    def place(into, *given):
+        groups = tuple((j, places) for j, places, _ in given)
+        count = sum(len(places) for _, places in groups)
         n = len(groups)
         return pl.pallas_call(
-            functools.partial(place_kernel, groups, places),
+            functools.partial(place_kernel, groups),
             out_shape=tiles_of(slot_count),
             in_specs=[SMEM] * 2 + [VMEM] * n + [HBM],
             out_specs=HBM,
             input_output_aliases={2 + n: 0},
-            scratch_shapes=[pltpu.SemaphoreType.DMA((n * len(places),))],
+            scratch_shapes=[pltpu.SemaphoreType.DMA((count,))],
             compiler_params=PARAMS,
-            cost_estimate=cost(0, 2 * n * len(places) * tile_bytes),
-        )(slots, ids, *tiles, into)
-
-    new_omega = place((0, 1, 2, 3), FAR_PLACES, (far_tiles, far_mate, far_across, far_last), new_omega)
-    new_omega = place((0, 1, 2), NEAR_PLACES, (near_tiles, near_mate, near_across), new_omega)
-    new_omega = place((3,), NEAR_PLACES, (near_last,), new_omega)
+            cost_estimate=cost(0, 2 * count * tile_bytes),
+        )(slots, ids, *(tiles for _, _, tiles in given), into)
+
+    every = tuple(range(PLACES))
+    new_omega = place(new_omega, (0, every, all_tiles), (1, every, mate))
+    new_omega = place(new_omega, (2, NEAR_PLACES, near_across), (2, FAR_PLACES, far_across))
+    new_omega = place(new_omega, (3, NEAR_PLACES, near_last), (3, FAR_PLACES, far_last))
     return (new_omega[None], y_product[None])
 
 

time: 130 us -> 132 us (1.015)
  waiting for transfers between devices: 28.6 us -> 32.2 us
    ppermute x19 -> x18, waiting for transfers between devices: 28.6 us -> 32.2 us  [permute(): return lax.ppermute(x, AXES, pairs)]
    ppermute x19 -> x18, starting transfers between devices: 74 us -> 72.9 us  [permute(): return lax.ppermute(x, AXES, pairs)]
  transfers between devices with their start and end apart: 19 -> 18, of which waited for: 8 -> 9; matrix products, arithmetic and copies ran while one was open for 0% -> 0% of each run, Pallas kernels for 5% -> 5%
where the time goes in v5:
time: 132 us; the launch traced here: 131 us
  starting transfers between devices  72.9 us (55%)
  waiting for transfers between devices  32.2 us (24%)
  blocking collectives  13.8 us (10%)
  Pallas kernels  9.91 us (8%)
  between operations  1.59 us (1%)
    ppermute x18, starting transfers between devices, permute(): return lax.ppermute(x, AXES, pairs)  72.9 us
    ppermute x18, waiting for transfers between devices, permute(): return lax.ppermute(x, AXES, pairs)  32.2 us
    all_gather x1, blocking collectives, step(): full = lax.all_gather(own_dosage, 'team', axis=0, tiled=True)  13.8 us
    pallas_call x3, Pallas kernels, place(): pl.pallas_call(functools.partial(place_kernel, groups), out_shape=tiles_o...  3.92 us
  transfers between devices with their start and end apart: 18, of which 9 were waited for; matrix products, arithmetic and copies ran while one was open for 0% of the time, Pallas kernels for 5%

profile of v5, /device:TPU:1, one launch (start us, length us, event | category | flops | bytes accessed | tf_op | source)
XLA Modules:
  0.0 131.2 jit_solution(8661237710346832695)
XLA Ops:
  0.6 13.8 %all-gather = f32[1,256,128]{2,1,0:T(8,128)S(1)} all-gather(f32[1,64,128]{2,1,0:T(8,128)} %param.5), channel_id=2, replica_groups=mesh['blk'=128,'team'=4] {'team'}, dimensions={1}, use_global_device_ids=true | all-gather | bytes 163840 | tf_op jit(solution)/shard_map/all_gather | solution.py:275
  14.4 8.7 %collective-permute-start = (f32[256,128]{1,0:T(8,128)S(1)}, f32[256,128]{1,0:T(8,128)S(1)}, u32[]{:S(2)}, u32[]{:S(2)}) collective-permute-start(f32[256,128]{1,0:T(8,128)S(1)} %bitcast.9), channel_id=1, source_target_pairs={{0,17},{1,496},{2,35},{3,482},{4,21},{5,500},{6,39},{7,486},{8,25}... | collective-permute-start | bytes 393224 | tf_op jit(solution)/shard_map/ppermute | solution.py:235
  23.2 1.9 %collective-permute-start.1 = (f32[256,128]{1,0:T(8,128)S(1)}, f32[256,128]{1,0:T(8,128)S(1)}, u32[]{:S(2)}, u32[]{:S(2)}) collective-permute-start(f32[256,128]{1,0:T(8,128)S(1)} %bitcast.10), channel_id=1, source_target_pairs={{0,9},{1,504},{2,27},{3,490},{4,13},{5,508},{6,31},{7,494},{8,17},... | collective-permute-start | bytes 393224 | tf_op jit(solution)/shard_map/ppermute | solution.py:235
  25.1 7.4 %collective-permute-start.4 = (f32[256,128]{1,0:T(8,128)S(1)}, f32[256,128]{1,0:T(8,128)S(1)}, u32[]{:S(2)}, u32[]{:S(2)}) collective-permute-start(f32[256,128]{1,0:T(8,128)S(1)} %bitcast.11), channel_id=1, source_target_pairs={{0,205},{1,308},{2,7},{3,259},{4,209},{5,312},{6,262},{7,2},{8,213... | collective-permute-start | bytes 393224 | tf_op jit(solution)/shard_map/ppermute | solution.py:235
  32.5 3.9 %collective-permute-start.5 = (f32[256,128]{1,0:T(8,128)S(1)}, f32[256,128]{1,0:T(8,128)S(1)}, u32[]{:S(2)}, u32[]{:S(2)}) collective-permute-start(f32[256,128]{1,0:T(8,128)S(1)} %bitcast.12), channel_id=1, source_target_pairs={{0,153},{1,360},{2,103},{3,414},{4,157},{5,364},{6,107},{7,418},{8... | collective-permute-start | bytes 393224 | tf_op jit(solution)/shard_map/ppermute | solution.py:235
  36.4 3.8 %collective-permute-start.2 = (f32[256,128]{1,0:T(8,128)S(1)}, f32[256,128]{1,0:T(8,128)S(1)}, u32[]{:S(2)}, u32[]{:S(2)}) collective-permute-start(f32[256,128]{1,0:T(8,128)S(1)} %collective-permute-done.refs_0_), channel_id=1, source_target_pairs={{0,4},{1,5},{2,6},{3,7},{4,0},{5,1},{6,2},{7,3},{8,12},{9,13},{10,... | collective-permute-start | bytes 393224 | tf_op jit(solution)/shard_map/ppermute | solution.py:235
  40.2 4.7 %collective-permute-start.3 = (f32[256,128]{1,0:T(8,128)S(1)}, f32[256,128]{1,0:T(8,128)S(1)}, u32[]{:S(2)}, u32[]{:S(2)}) collective-permute-start(f32[256,128]{1,0:T(8,128)S(1)} %collective-permute-done.1.refs_1_), channel_id=1, source_target_pairs={{0,4},{1,5},{2,6},{3,7},{4,0},{5,1},{6,2},{7,3},{8,12},{9,13},{10,... | collective-permute-start | bytes 393224 | tf_op jit(solution)/shard_map/ppermute | solution.py:235
  46.3 2.3 %pick.1 = (s32[24]{0:T(128)S(1)}, f32[6,128,128]{2,1,0:T(8,128)S(1)}) custom-call(s32[2]{0:T(128)S(1)} %pad_add_fusion.ids, s32[1,24]{1,0:T(1,128)S(1)} %copy-done, s32[1]{0:T(128)S(6)} %copy.12.counts, f32[24,128,128]{2,1,0:T(8,128)} %bitcast.18), custom_call_target="tpu_custom_call" | custom-call | bytes 786432 | tf_op jit(solution)/shard_map/pick/pallas_call | solution.py:264
  49.4 3.9 %collective-permute-start.6 = (f32[256,128]{1,0:T(8,128)S(1)}, f32[256,128]{1,0:T(8,128)S(1)}, u32[]{:S(2)}, u32[]{:S(2)}) collective-permute-start(f32[256,128]{1,0:T(8,128)S(1)} %partial.1), channel_id=1, source_target_pairs={{0,1},{1,0},{2,3},{3,2},{4,5},{5,4},{6,7},{7,6},{8,9},{9,8},{10,11... | collective-permute-start | bytes 393224 | tf_op jit(solution)/shard_map/ppermute | solution.py:235
  53.3 1.0 collective-permute-done.6
  54.3 1.9 %collective-permute-start.7 = (f32[256,128]{1,0:T(8,128)S(1)}, f32[256,128]{1,0:T(8,128)S(1)}, u32[]{:S(2)}, u32[]{:S(2)}) collective-permute-start(f32[256,128]{1,0:T(8,128)S(1)} %add.8.half), channel_id=1, source_target_pairs={{0,2},{1,3},{2,0},{3,1},{4,6},{5,7},{6,4},{7,5},{8,10},{9,11},{10,... | collective-permute-start | bytes 393224 | tf_op jit(solution)/shard_map/ppermute | solution.py:235
  56.5 5.9 %collective-permute-done.7.other = f32[256,128]{1,0:T(8,128)S(1)} collective-permute-done((f32[256,128]{1,0:T(8,128)S(1)}, f32[256,128]{1,0:T(8,128)S(1)}, u32[]{:S(2)}, u32[]{:S(2)}) %collective-permute-start.7) | collective-permute-done | bytes 131104 | tf_op jit(solution)/shard_map/ppermute | solution.py:235
  62.4 1.5 %tiles.1 = (f32[128,128]{1,0:T(8,128)S(1)}, f32[128,128]{1,0:T(8,128)S(1)}, f32[2,128,128]{2,1,0:T(8,128)S(1)}, f32[128,128]{1,0:T(8,128)S(1)}, f32[128,128]{1,0:T(8,128)S(1)}, /*index=5*/f32[64,128]{1,0:T(8,128)}) custom-call(s32[2]{0:T(128)S(1)} %pad_add_fusion.ids, f32[256,128]{1,0:T(8,128)S(1)} %add.8.half, f32[256,128]{1,0:T(8,128)S(1)} %collective-permute-done.7.other, ...), custom_call_target="tpu_custom_call" | custom-call | flops 50331648 | bytes 1835008 | tf_op jit(solution)/shard_map/tiles/pallas_call | solution.py:306
  63.9 2.5 %collective-permute-start.8 = (f32[2,128,128]{2,1,0:T(8,128)S(1)}, f32[2,128,128]{2,1,0:T(8,128)S(1)}, u32[]{:S(2)}, u32[]{:S(2)}) collective-permute-start(f32[2,128,128]{2,1,0:T(8,128)S(1)} %get-tuple-element.20.side), channel_id=1, source_target_pairs={{0,4},{1,5},{2,6},{3,7},{4,0},{5,1},{6,2},{7,3},{8,12},{9,13},{10,... | collective-permute-start | bytes 393224 | tf_op jit(solution)/shard_map/ppermute | solution.py:235
  66.4 3.2 %collective-permute-done.8 = f32[2,128,128]{2,1,0:T(8,128)S(1)} collective-permute-done((f32[2,128,128]{2,1,0:T(8,128)S(1)}, f32[2,128,128]{2,1,0:T(8,128)S(1)}, u32[]{:S(2)}, u32[]{:S(2)}) %collective-permute-start.8) | collective-permute-done | bytes 131104 | tf_op jit(solution)/shard_map/ppermute | solution.py:235
  69.6 8.0 %collective-permute-start.10 = (f32[2,128,128]{2,1,0:T(8,128)S(1)}, f32[2,128,128]{2,1,0:T(8,128)S(1)}, u32[]{:S(2)}, u32[]{:S(2)}) collective-permute-start(f32[2,128,128]{2,1,0:T(8,128)S(1)} %pad_maximum_fusion.1), channel_id=1, source_target_pairs={{0,9},{1,504},{2,27},{3,490},{4,13},{5,508},{6,31},{7,494},{8,17},... | collective-permute-start | bytes 393224 | tf_op jit(solution)/shard_map/ppermute | solution.py:235
  77.7 1.9 %collective-permute-start.9 = (f32[2,128,128]{2,1,0:T(8,128)S(1)}, f32[2,128,128]{2,1,0:T(8,128)S(1)}, u32[]{:S(2)}, u32[]{:S(2)}) collective-permute-start(f32[2,128,128]{2,1,0:T(8,128)S(1)} %pad_maximum_fusion), channel_id=1, source_target_pairs={{0,17},{1,496},{2,35},{3,482},{4,21},{5,500},{6,39},{7,486},{8,25}... | collective-permute-start | bytes 393224 | tf_op jit(solution)/shard_map/ppermute | solution.py:235
  80.3 7.9 %collective-permute-done.9.got_1 = f32[2,128,128]{2,1,0:T(8,128)S(1)} collective-permute-done((f32[2,128,128]{2,1,0:T(8,128)S(1)}, f32[2,128,128]{2,1,0:T(8,128)S(1)}, u32[]{:S(2)}, u32[]{:S(2)}) %collective-permute-start.9) | collective-permute-done | bytes 131104 | tf_op jit(solution)/shard_map/ppermute | solution.py:235
  88.4 5.9 %collective-permute-start.11 = (f32[4,128,128]{2,1,0:T(8,128)S(1)}, f32[4,128,128]{2,1,0:T(8,128)S(1)}, u32[]{:S(2)}, u32[]{:S(2)}) collective-permute-start(f32[4,128,128]{2,1,0:T(8,128)S(1)} %update_near.1.near), channel_id=1, source_target_pairs={{0,2},{1,3},{2,0},{3,1},{4,6},{5,7},{6,4},{7,5},{8,10},{9,11},{10,... | collective-permute-start | bytes 786440 | tf_op jit(solution)/shard_map/ppermute | solution.py:235
  94.3 6.2 %collective-permute-start.13 = (f32[128,128]{1,0:T(8,128)S(1)}, f32[128,128]{1,0:T(8,128)S(1)}, u32[]{:S(2)}, u32[]{:S(2)}) collective-permute-start(f32[128,128]{1,0:T(8,128)S(1)} %get-tuple-element.21.far_1), channel_id=1, source_target_pairs={{0,205},{1,308},{2,7},{3,259},{4,209},{5,312},{6,262},{7,2},{8,213... | collective-permute-start | bytes 196616 | tf_op jit(solution)/shard_map/ppermute | solution.py:235
  100.4 2.7 %collective-permute-start.14 = (f32[128,128]{1,0:T(8,128)S(1)}, f32[128,128]{1,0:T(8,128)S(1)}, u32[]{:S(2)}, u32[]{:S(2)}) collective-permute-start(f32[128,128]{1,0:T(8,128)S(1)} %get-tuple-element.22.far_2), channel_id=1, source_target_pairs={{0,153},{1,360},{2,103},{3,414},{4,157},{5,364},{6,107},{7,418},{8... | collective-permute-start | bytes 196616 | tf_op jit(solution)/shard_map/ppermute | solution.py:235
  103.1 6.0 %collective-permute-done.13.got_1 = f32[128,128]{1,0:T(8,128)S(1)} collective-permute-done((f32[128,128]{1,0:T(8,128)S(1)}, f32[128,128]{1,0:T(8,128)S(1)}, u32[]{:S(2)}, u32[]{:S(2)}) %collective-permute-start.13) | collective-permute-done | bytes 65568 | tf_op jit(solution)/shard_map/ppermute | solution.py:235
  109.1 3.7 %collective-permute-done.14.got_2 = f32[128,128]{1,0:T(8,128)S(1)} collective-permute-done((f32[128,128]{1,0:T(8,128)S(1)}, f32[128,128]{1,0:T(8,128)S(1)}, u32[]{:S(2)}, u32[]{:S(2)}) %collective-permute-start.14) | collective-permute-done | bytes 65568 | tf_op jit(solution)/shard_map/ppermute | solution.py:235
  112.9 1.9 %collective-permute-start.17 = (f32[6,128,128]{2,1,0:T(8,128)S(1)}, f32[6,128,128]{2,1,0:T(8,128)S(1)}, u32[]{:S(2)}, u32[]{:S(2)}) collective-permute-start(f32[6,128,128]{2,1,0:T(8,128)S(1)} %get-tuple-element.24.refs_0_), channel_id=1, source_target_pairs={{0,1},{1,0},{2,3},{3,2},{4,5},{5,4},{6,7},{7,6},{8,9},{9,8},{10,11... | collective-permute-start | bytes 1179656 | tf_op jit(solution)/shard_map/ppermute | solution.py:235
  114.9 1.9 %collective-permute-start.15 = (f32[2,128,128]{2,1,0:T(8,128)S(1)}, f32[2,128,128]{2,1,0:T(8,128)S(1)}, u32[]{:S(2)}, u32[]{:S(2)}) collective-permute-start(f32[2,128,128]{2,1,0:T(8,128)S(1)} %get-tuple-element.23), channel_id=1, source_target_pairs={{0,2},{1,3},{2,0},{3,1},{4,6},{5,7},{6,4},{7,5},{8,10},{9,11},{10,... | collective-permute-start | bytes 393224 | tf_op jit(solution)/shard_map/ppermute | solution.py:235
  116.8 2.4 %collective-permute-start.12 = (f32[4,128,128]{2,1,0:T(8,128)S(1)}, f32[4,128,128]{2,1,0:T(8,128)S(1)}, u32[]{:S(2)}, u32[]{:S(2)}) collective-permute-start(f32[4,128,128]{2,1,0:T(8,128)S(1)} %collective-permute-done.11.refs_0_), channel_id=1, source_target_pairs={{0,1},{1,0},{2,3},{3,2},{4,5},{5,4},{6,7},{7,6},{8,9},{9,8},{10,11... | collective-permute-start | bytes 786440 | tf_op jit(solution)/shard_map/ppermute | solution.py:235
  119.2 3.6 %collective-permute-done.15.refs_1_ = f32[2,128,128]{2,1,0:T(8,128)S(1)} collective-permute-done((f32[2,128,128]{2,1,0:T(8,128)S(1)}, f32[2,128,128]{2,1,0:T(8,128)S(1)}, u32[]{:S(2)}, u32[]{:S(2)}) %collective-permute-start.15) | collective-permute-done | bytes 131104 | tf_op jit(solution)/shard_map/ppermute | solution.py:235
  122.8 3.3 %collective-permute-start.16 = (f32[2,128,128]{2,1,0:T(8,128)S(1)}, f32[2,128,128]{2,1,0:T(8,128)S(1)}, u32[]{:S(2)}, u32[]{:S(2)}) collective-permute-start(f32[2,128,128]{2,1,0:T(8,128)S(1)} %collective-permute-done.15.refs_1_), channel_id=1, source_target_pairs={{0,1},{1,0},{2,3},{3,2},{4,5},{5,4},{6,7},{7,6},{8,9},{9,8},{10,11... | collective-permute-start | bytes 393224 | tf_op jit(solution)/shard_map/ppermute | solution.py:235
  126.1 1.1 blank.1.refs_2_
  127.3 1.4 %shard_map.59.refs_2_ = f32[24,128,128]{2,1,0:T(8,128)} custom-call(s32[24]{0:T(128)S(1)} %get-tuple-element.14.slots, s32[2]{0:T(128)S(1)} %pad_add_fusion.ids, f32[6,128,128]{2,1,0:T(8,128)S(1)} %get-tuple-element.24.refs_0_, f32[6,128,128]{2,1,0:T(8,128)S(1)} %collective-permute-done.17.refs_1_, ...), custom_call_target="tpu_custom_call", output_to_operand_aliasing={{}: (4, {})} | custom-call | bytes 1572864 | tf_op jit(solution)/shard_map/pallas_call | solution.py:385
  128.6 1.3 shard_map.60.refs_2_
  129.9 1.3 shard_map.61
  (22 shorter events, 2.8 us)
Async XLA Ops:
  14.4 21.9 %collective-permute-start = (f32[256,128]{1,0:T(8,128)S(1)}, f32[256,128]{1,0:T(8,128)S(1)}, u32[]{:S(2)}, u32[]{:S(2)}) collective-permute-start(f32[256,128]{1,0:T(8,128)S(1)} %bitcast.9), channel_id=1, source_target_pairs={{0,17},{1,496},{2,35},{3,482},{4,21},{5,500},{6,39},{7,486},{8,25}... | collective-permute-start | bytes 393224 | tf_op jit(solution)/shard_map/ppermute | solution.py:235
  23.2 17.1 %collective-permute-start.1 = (f32[256,128]{1,0:T(8,128)S(1)}, f32[256,128]{1,0:T(8,128)S(1)}, u32[]{:S(2)}, u32[]{:S(2)}) collective-permute-start(f32[256,128]{1,0:T(8,128)S(1)} %bitcast.10), channel_id=1, source_target_pairs={{0,9},{1,504},{2,27},{3,490},{4,13},{5,508},{6,31},{7,494},{8,17},... | collective-permute-start | bytes 393224 | tf_op jit(solution)/shard_map/ppermute | solution.py:235
  25.1 23.6 %collective-permute-start.4 = (f32[256,128]{1,0:T(8,128)S(1)}, f32[256,128]{1,0:T(8,128)S(1)}, u32[]{:S(2)}, u32[]{:S(2)}) collective-permute-start(f32[256,128]{1,0:T(8,128)S(1)} %bitcast.11), channel_id=1, source_target_pairs={{0,205},{1,308},{2,7},{3,259},{4,209},{5,312},{6,262},{7,2},{8,213... | collective-permute-start | bytes 393224 | tf_op jit(solution)/shard_map/ppermute | solution.py:235
  32.5 16.2 %collective-permute-start.5 = (f32[256,128]{1,0:T(8,128)S(1)}, f32[256,128]{1,0:T(8,128)S(1)}, u32[]{:S(2)}, u32[]{:S(2)}) collective-permute-start(f32[256,128]{1,0:T(8,128)S(1)} %bitcast.12), channel_id=1, source_target_pairs={{0,153},{1,360},{2,103},{3,414},{4,157},{5,364},{6,107},{7,418},{8... | collective-permute-start | bytes 393224 | tf_op jit(solution)/shard_map/ppermute | solution.py:235
  36.4 12.3 %collective-permute-start.2 = (f32[256,128]{1,0:T(8,128)S(1)}, f32[256,128]{1,0:T(8,128)S(1)}, u32[]{:S(2)}, u32[]{:S(2)}) collective-permute-start(f32[256,128]{1,0:T(8,128)S(1)} %collective-permute-done.refs_0_), channel_id=1, source_target_pairs={{0,4},{1,5},{2,6},{3,7},{4,0},{5,1},{6,2},{7,3},{8,12},{9,13},{10,... | collective-permute-start | bytes 393224 | tf_op jit(solution)/shard_map/ppermute | solution.py:235
  40.2 8.7 %collective-permute-start.3 = (f32[256,128]{1,0:T(8,128)S(1)}, f32[256,128]{1,0:T(8,128)S(1)}, u32[]{:S(2)}, u32[]{:S(2)}) collective-permute-start(f32[256,128]{1,0:T(8,128)S(1)} %collective-permute-done.1.refs_1_), channel_id=1, source_target_pairs={{0,4},{1,5},{2,6},{3,7},{4,0},{5,1},{6,2},{7,3},{8,12},{9,13},{10,... | collective-permute-start | bytes 393224 | tf_op jit(solution)/shard_map/ppermute | solution.py:235
  45.6 0.7 copy-start
  49.4 4.9 %collective-permute-start.6 = (f32[256,128]{1,0:T(8,128)S(1)}, f32[256,128]{1,0:T(8,128)S(1)}, u32[]{:S(2)}, u32[]{:S(2)}) collective-permute-start(f32[256,128]{1,0:T(8,128)S(1)} %partial.1), channel_id=1, source_target_pairs={{0,1},{1,0},{2,3},{3,2},{4,5},{5,4},{6,7},{7,6},{8,9},{9,8},{10,11... | collective-permute-start | bytes 393224 | tf_op jit(solution)/shard_map/ppermute | solution.py:235
  54.3 8.1 %collective-permute-start.7 = (f32[256,128]{1,0:T(8,128)S(1)}, f32[256,128]{1,0:T(8,128)S(1)}, u32[]{:S(2)}, u32[]{:S(2)}) collective-permute-start(f32[256,128]{1,0:T(8,128)S(1)} %add.8.half), channel_id=1, source_target_pairs={{0,2},{1,3},{2,0},{3,1},{4,6},{5,7},{6,4},{7,5},{8,10},{9,11},{10,... | collective-permute-start | bytes 393224 | tf_op jit(solution)/shard_map/ppermute | solution.py:235
  63.9 5.7 %collective-permute-start.8 = (f32[2,128,128]{2,1,0:T(8,128)S(1)}, f32[2,128,128]{2,1,0:T(8,128)S(1)}, u32[]{:S(2)}, u32[]{:S(2)}) collective-permute-start(f32[2,128,128]{2,1,0:T(8,128)S(1)} %get-tuple-element.20.side), channel_id=1, source_target_pairs={{0,4},{1,5},{2,6},{3,7},{4,0},{5,1},{6,2},{7,3},{8,12},{9,13},{10,... | collective-permute-start | bytes 393224 | tf_op jit(solution)/shard_map/ppermute | solution.py:235
  69.6 10.7 %collective-permute-start.10 = (f32[2,128,128]{2,1,0:T(8,128)S(1)}, f32[2,128,128]{2,1,0:T(8,128)S(1)}, u32[]{:S(2)}, u32[]{:S(2)}) collective-permute-start(f32[2,128,128]{2,1,0:T(8,128)S(1)} %pad_maximum_fusion.1), channel_id=1, source_target_pairs={{0,9},{1,504},{2,27},{3,490},{4,13},{5,508},{6,31},{7,494},{8,17},... | collective-permute-start | bytes 393224 | tf_op jit(solution)/shard_map/ppermute | solution.py:235
  77.7 10.5 %collective-permute-start.9 = (f32[2,128,128]{2,1,0:T(8,128)S(1)}, f32[2,128,128]{2,1,0:T(8,128)S(1)}, u32[]{:S(2)}, u32[]{:S(2)}) collective-permute-start(f32[2,128,128]{2,1,0:T(8,128)S(1)} %pad_maximum_fusion), channel_id=1, source_target_pairs={{0,17},{1,496},{2,35},{3,482},{4,21},{5,500},{6,39},{7,486},{8,25}... | collective-permute-start | bytes 393224 | tf_op jit(solution)/shard_map/ppermute | solution.py:235
  88.4 28.5 %collective-permute-start.11 = (f32[4,128,128]{2,1,0:T(8,128)S(1)}, f32[4,128,128]{2,1,0:T(8,128)S(1)}, u32[]{:S(2)}, u32[]{:S(2)}) collective-permute-start(f32[4,128,128]{2,1,0:T(8,128)S(1)} %update_near.1.near), channel_id=1, source_target_pairs={{0,2},{1,3},{2,0},{3,1},{4,6},{5,7},{6,4},{7,5},{8,10},{9,11},{10,... | collective-permute-start | bytes 786440 | tf_op jit(solution)/shard_map/ppermute | solution.py:235
  94.3 14.9 %collective-permute-start.13 = (f32[128,128]{1,0:T(8,128)S(1)}, f32[128,128]{1,0:T(8,128)S(1)}, u32[]{:S(2)}, u32[]{:S(2)}) collective-permute-start(f32[128,128]{1,0:T(8,128)S(1)} %get-tuple-element.21.far_1), channel_id=1, source_target_pairs={{0,205},{1,308},{2,7},{3,259},{4,209},{5,312},{6,262},{7,2},{8,213... | collective-permute-start | bytes 196616 | tf_op jit(solution)/shard_map/ppermute | solution.py:235
  100.4 12.4 %collective-permute-start.14 = (f32[128,128]{1,0:T(8,128)S(1)}, f32[128,128]{1,0:T(8,128)S(1)}, u32[]{:S(2)}, u32[]{:S(2)}) collective-permute-start(f32[128,128]{1,0:T(8,128)S(1)} %get-tuple-element.22.far_2), channel_id=1, source_target_pairs={{0,153},{1,360},{2,103},{3,414},{4,157},{5,364},{6,107},{7,418},{8... | collective-permute-start | bytes 196616 | tf_op jit(solution)/shard_map/ppermute | solution.py:235
  112.9 14.3 %collective-permute-start.17 = (f32[6,128,128]{2,1,0:T(8,128)S(1)}, f32[6,128,128]{2,1,0:T(8,128)S(1)}, u32[]{:S(2)}, u32[]{:S(2)}) collective-permute-start(f32[6,128,128]{2,1,0:T(8,128)S(1)} %get-tuple-element.24.refs_0_), channel_id=1, source_target_pairs={{0,1},{1,0},{2,3},{3,2},{4,5},{5,4},{6,7},{7,6},{8,9},{9,8},{10,11... | collective-permute-start | bytes 1179656 | tf_op jit(solution)/shard_map/ppermute | solution.py:235
  114.9 8.0 %collective-permute-start.15 = (f32[2,128,128]{2,1,0:T(8,128)S(1)}, f32[2,128,128]{2,1,0:T(8,128)S(1)}, u32[]{:S(2)}, u32[]{:S(2)}) collective-permute-start(f32[2,128,128]{2,1,0:T(8,128)S(1)} %get-tuple-element.23), channel_id=1, source_target_pairs={{0,2},{1,3},{2,0},{3,1},{4,6},{5,7},{6,4},{7,5},{8,10},{9,11},{10,... | collective-permute-start | bytes 393224 | tf_op jit(solution)/shard_map/ppermute | solution.py:235
  116.8 13.1 %collective-permute-start.12 = (f32[4,128,128]{2,1,0:T(8,128)S(1)}, f32[4,128,128]{2,1,0:T(8,128)S(1)}, u32[]{:S(2)}, u32[]{:S(2)}) collective-permute-start(f32[4,128,128]{2,1,0:T(8,128)S(1)} %collective-permute-done.11.refs_0_), channel_id=1, source_target_pairs={{0,1},{1,0},{2,3},{3,2},{4,5},{5,4},{6,7},{7,6},{8,9},{9,8},{10,11... | collective-permute-start | bytes 786440 | tf_op jit(solution)/shard_map/ppermute | solution.py:235
  122.8 7.1 %collective-permute-start.16 = (f32[2,128,128]{2,1,0:T(8,128)S(1)}, f32[2,128,128]{2,1,0:T(8,128)S(1)}, u32[]{:S(2)}, u32[]{:S(2)}) collective-permute-start(f32[2,128,128]{2,1,0:T(8,128)S(1)} %collective-permute-done.15.refs_1_), channel_id=1, source_target_pairs={{0,1},{1,0},{2,3},{3,2},{4,5},{5,4},{6,7},{7,6},{8,9},{9,8},{10,11... | collective-permute-start | bytes 393224 | tf_op jit(solution)/shard_map/ppermute | solution.py:235

commit v6 on v5

--- a/solution.py
+++ b/solution.py
@@ -16,8 +16,8 @@
 AXES = ("blk", "team")
 NEAR_1, NEAR_2, SIDE_1, SIDE_2, FAR_1, FAR_2 = range(6)
 PLACES = 6
-NEAR = ((4, 2), (8, 6))
-FAR = ((51, 38), (0, 25))
+NEAR = ((2, 8), (4, 6))
+FAR = ((51, 0), (25, 38))
 
 
 def offsets(near, far):
@@ -230,8 +230,9 @@
         pairs = []
         for b in range(rows):
             for t in range(team):
-                b2, t2 = target(b, t)
-                pairs.append((b * team + t, (b2 % rows) * team + t2))
+                found = target(b, t)
+                if found is not None:
+                    pairs.append((b * team + t, (found[0] % rows) * team + found[1]))
         return lax.ppermute(x, AXES, pairs)
 
     def partner(b, t, k):
@@ -239,15 +240,18 @@
         found = [
             u for u in range(team) if (OFFSETS[there % 2, u, k] + OFFSETS[b % 2, t, k]) % rows == 0
         ]
+        if k in (NEAR_1, NEAR_2) and not 0 <= there < rows:
+            return None
         return there, found[0]
 
     def fetch(x, k):
         source = {}
         for b in range(rows):
             for t in range(team):
-                b2, t2 = partner(b, t, k)
-                source[b2 % rows, t2] = (b, t)
-        return permute(x, lambda b, t: source[b, t])
+                found = partner(b, t, k)
+                if found is not None:
+                    source[found[0] % rows, found[1]] = (b, t)
+        return permute(x, lambda b, t: source.get((b, t)))
 
     def beside(b, t):
         return b ^ 1, t

time: 132 us -> 124 us (0.939)
  waiting for transfers between devices: 32.2 us -> 11.9 us
  starting transfers between devices: 72.9 us -> 85 us
    ppermute x18, waiting for transfers between devices: 32.2 us -> 11.9 us  [permute(): return lax.ppermute(x, AXES, pairs)]
    ppermute x18, starting transfers between devices: 72.9 us -> 85 us  [permute(): return lax.ppermute(x, AXES, pairs)]
  transfers between devices with their start and end apart: 18 -> 18, of which waited for: 9 -> 6; matrix products, arithmetic and copies ran while one was open for 0% -> 0% of each run, Pallas kernels for 5% -> 5%
where the time goes in v6:
time: 124 us; the launch traced here: 123 us
  starting transfers between devices  85 us (69%)
  blocking collectives  13.8 us (11%)
  waiting for transfers between devices  11.9 us (10%)
  Pallas kernels  9.92 us (8%)
  between operations  1.62 us (1%)
    ppermute x18, starting transfers between devices, permute(): return lax.ppermute(x, AXES, pairs)  85 us
    all_gather x1, blocking collectives, step(): full = lax.all_gather(own_dosage, 'team', axis=0, tiled=True)  13.8 us
    ppermute x18, waiting for transfers between devices, permute(): return lax.ppermute(x, AXES, pairs)  11.9 us
    pallas_call x3, Pallas kernels, place(): pl.pallas_call(functools.partial(place_kernel, groups), out_shape=tiles_o...  3.92 us
  transfers between devices with their start and end apart: 18, of which 6 were waited for; matrix products, arithmetic and copies ran while one was open for 0% of the time, Pallas kernels for 5%

profile of v6, /device:TPU:1, one launch (start us, length us, event | category | flops | bytes accessed | tf_op | source)
XLA Modules:
  0.0 123.0 jit_solution(14974394320017297465)
XLA Ops:
  0.6 13.8 %all-gather = f32[1,256,128]{2,1,0:T(8,128)S(1)} all-gather(f32[1,64,128]{2,1,0:T(8,128)} %param.5), channel_id=2, replica_groups=mesh['blk'=128,'team'=4] {'team'}, dimensions={1}, use_global_device_ids=true | all-gather | bytes 163840 | tf_op jit(solution)/shard_map/all_gather | solution.py:279
  14.4 0.7 collective-permute-start
  15.1 0.7 collective-permute-start.1
  15.8 18.4 %collective-permute-start.4 = (f32[256,128]{1,0:T(8,128)S(1)}, f32[256,128]{1,0:T(8,128)S(1)}, u32[]{:S(2)}, u32[]{:S(2)}) collective-permute-start(f32[256,128]{1,0:T(8,128)S(1)} %bitcast.11), channel_id=1, source_target_pairs={{0,205},{1,308},{2,103},{3,414},{4,209},{5,312},{6,107},{7,418},{8... | collective-permute-start | bytes 393224 | tf_op jit(solution)/shard_map/ppermute | solution.py:236
  34.2 2.0 %collective-permute-start.5 = (f32[256,128]{1,0:T(8,128)S(1)}, f32[256,128]{1,0:T(8,128)S(1)}, u32[]{:S(2)}, u32[]{:S(2)}) collective-permute-start(f32[256,128]{1,0:T(8,128)S(1)} %bitcast.12), channel_id=1, source_target_pairs={{0,5},{1,257},{2,155},{3,362},{4,260},{5,0},{6,159},{7,366},{8,13}... | collective-permute-start | bytes 393224 | tf_op jit(solution)/shard_map/ppermute | solution.py:236
  36.2 2.6 %collective-permute-start.2 = (f32[256,128]{1,0:T(8,128)S(1)}, f32[256,128]{1,0:T(8,128)S(1)}, u32[]{:S(2)}, u32[]{:S(2)}) collective-permute-start(f32[256,128]{1,0:T(8,128)S(1)} %collective-permute-done.refs_0_), channel_id=1, source_target_pairs={{0,4},{1,5},{2,6},{3,7},{4,0},{5,1},{6,2},{7,3},{8,12},{9,13},{10,... | collective-permute-start | bytes 393224 | tf_op jit(solution)/shard_map/ppermute | solution.py:236
  38.7 2.7 %collective-permute-start.3 = (f32[256,128]{1,0:T(8,128)S(1)}, f32[256,128]{1,0:T(8,128)S(1)}, u32[]{:S(2)}, u32[]{:S(2)}) collective-permute-start(f32[256,128]{1,0:T(8,128)S(1)} %collective-permute-done.1.refs_1_), channel_id=1, source_target_pairs={{0,4},{1,5},{2,6},{3,7},{4,0},{5,1},{6,2},{7,3},{8,12},{9,13},{10,... | collective-permute-start | bytes 393224 | tf_op jit(solution)/shard_map/ppermute | solution.py:236
  42.2 0.7 copy-done
  42.9 2.3 %pick.1 = (s32[24]{0:T(128)S(1)}, f32[6,128,128]{2,1,0:T(8,128)S(1)}) custom-call(s32[2]{0:T(128)S(1)} %pad_add_fusion.ids, s32[1,24]{1,0:T(1,128)S(1)} %copy-done, s32[1]{0:T(128)S(6)} %copy.12.counts, f32[24,128,128]{2,1,0:T(8,128)} %bitcast.18), custom_call_target="tpu_custom_call" | custom-call | bytes 786432 | tf_op jit(solution)/shard_map/pick/pallas_call | solution.py:268
  45.2 1.1 collective-permute-done.3.refs_3_
  46.8 2.9 %collective-permute-start.6 = (f32[256,128]{1,0:T(8,128)S(1)}, f32[256,128]{1,0:T(8,128)S(1)}, u32[]{:S(2)}, u32[]{:S(2)}) collective-permute-start(f32[256,128]{1,0:T(8,128)S(1)} %partial.1), channel_id=1, source_target_pairs={{0,1},{1,0},{2,3},{3,2},{4,5},{5,4},{6,7},{7,6},{8,9},{9,8},{10,11... | collective-permute-start | bytes 393224 | tf_op jit(solution)/shard_map/ppermute | solution.py:236
  49.7 1.0 collective-permute-done.6
  50.7 5.5 %collective-permute-start.7 = (f32[256,128]{1,0:T(8,128)S(1)}, f32[256,128]{1,0:T(8,128)S(1)}, u32[]{:S(2)}, u32[]{:S(2)}) collective-permute-start(f32[256,128]{1,0:T(8,128)S(1)} %add.8.half), channel_id=1, source_target_pairs={{0,2},{1,3},{2,0},{3,1},{4,6},{5,7},{6,4},{7,5},{8,10},{9,11},{10,... | collective-permute-start | bytes 393224 | tf_op jit(solution)/shard_map/ppermute | solution.py:236
  56.5 3.4 %collective-permute-done.7.other = f32[256,128]{1,0:T(8,128)S(1)} collective-permute-done((f32[256,128]{1,0:T(8,128)S(1)}, f32[256,128]{1,0:T(8,128)S(1)}, u32[]{:S(2)}, u32[]{:S(2)}) %collective-permute-start.7) | collective-permute-done | bytes 131104 | tf_op jit(solution)/shard_map/ppermute | solution.py:236
  59.9 1.5 %tiles.1 = (f32[128,128]{1,0:T(8,128)S(1)}, f32[128,128]{1,0:T(8,128)S(1)}, f32[2,128,128]{2,1,0:T(8,128)S(1)}, f32[128,128]{1,0:T(8,128)S(1)}, f32[128,128]{1,0:T(8,128)S(1)}, /*index=5*/f32[64,128]{1,0:T(8,128)}) custom-call(s32[2]{0:T(128)S(1)} %pad_add_fusion.ids, f32[256,128]{1,0:T(8,128)S(1)} %add.8.half, f32[256,128]{1,0:T(8,128)S(1)} %collective-permute-done.7.other, ...), custom_call_target="tpu_custom_call" | custom-call | flops 50331648 | bytes 1835008 | tf_op jit(solution)/shard_map/tiles/pallas_call | solution.py:310
  61.4 2.4 %collective-permute-start.8 = (f32[2,128,128]{2,1,0:T(8,128)S(1)}, f32[2,128,128]{2,1,0:T(8,128)S(1)}, u32[]{:S(2)}, u32[]{:S(2)}) collective-permute-start(f32[2,128,128]{2,1,0:T(8,128)S(1)} %get-tuple-element.20.side), channel_id=1, source_target_pairs={{0,4},{1,5},{2,6},{3,7},{4,0},{5,1},{6,2},{7,3},{8,12},{9,13},{10,... | collective-permute-start | bytes 393224 | tf_op jit(solution)/shard_map/ppermute | solution.py:236
  63.7 3.8 %collective-permute-done.8 = f32[2,128,128]{2,1,0:T(8,128)S(1)} collective-permute-done((f32[2,128,128]{2,1,0:T(8,128)S(1)}, f32[2,128,128]{2,1,0:T(8,128)S(1)}, u32[]{:S(2)}, u32[]{:S(2)}) %collective-permute-start.8) | collective-permute-done | bytes 131104 | tf_op jit(solution)/shard_map/ppermute | solution.py:236
  67.6 0.7 collective-permute-start.10
  68.3 0.7 collective-permute-start.9
  69.2 4.1 %collective-permute-start.11 = (f32[4,128,128]{2,1,0:T(8,128)S(1)}, f32[4,128,128]{2,1,0:T(8,128)S(1)}, u32[]{:S(2)}, u32[]{:S(2)}) collective-permute-start(f32[4,128,128]{2,1,0:T(8,128)S(1)} %update_near.1.near), channel_id=1, source_target_pairs={{0,2},{1,3},{2,0},{3,1},{4,6},{5,7},{6,4},{7,5},{8,10},{9,11},{10,... | collective-permute-start | bytes 786440 | tf_op jit(solution)/shard_map/ppermute | solution.py:236
  73.3 19.4 %collective-permute-start.13 = (f32[128,128]{1,0:T(8,128)S(1)}, f32[128,128]{1,0:T(8,128)S(1)}, u32[]{:S(2)}, u32[]{:S(2)}) collective-permute-start(f32[128,128]{1,0:T(8,128)S(1)} %get-tuple-element.21.far_1), channel_id=1, source_target_pairs={{0,205},{1,308},{2,103},{3,414},{4,209},{5,312},{6,107},{7,418},{8... | collective-permute-start | bytes 196616 | tf_op jit(solution)/shard_map/ppermute | solution.py:236
  92.7 5.7 %collective-permute-start.14 = (f32[128,128]{1,0:T(8,128)S(1)}, f32[128,128]{1,0:T(8,128)S(1)}, u32[]{:S(2)}, u32[]{:S(2)}) collective-permute-start(f32[128,128]{1,0:T(8,128)S(1)} %get-tuple-element.22.far_2), channel_id=1, source_target_pairs={{0,5},{1,257},{2,155},{3,362},{4,260},{5,0},{6,159},{7,366},{8,13}... | collective-permute-start | bytes 196616 | tf_op jit(solution)/shard_map/ppermute | solution.py:236
  98.4 1.9 %collective-permute-done.14.got_2 = f32[128,128]{1,0:T(8,128)S(1)} collective-permute-done((f32[128,128]{1,0:T(8,128)S(1)}, f32[128,128]{1,0:T(8,128)S(1)}, u32[]{:S(2)}, u32[]{:S(2)}) %collective-permute-start.14) | collective-permute-done | bytes 65568 | tf_op jit(solution)/shard_map/ppermute | solution.py:236
  100.4 4.2 %collective-permute-start.17 = (f32[6,128,128]{2,1,0:T(8,128)S(1)}, f32[6,128,128]{2,1,0:T(8,128)S(1)}, u32[]{:S(2)}, u32[]{:S(2)}) collective-permute-start(f32[6,128,128]{2,1,0:T(8,128)S(1)} %get-tuple-element.24.refs_0_), channel_id=1, source_target_pairs={{0,1},{1,0},{2,3},{3,2},{4,5},{5,4},{6,7},{7,6},{8,9},{9,8},{10,11... | collective-permute-start | bytes 1179656 | tf_op jit(solution)/shard_map/ppermute | solution.py:236
  104.6 6.9 %collective-permute-start.15 = (f32[2,128,128]{2,1,0:T(8,128)S(1)}, f32[2,128,128]{2,1,0:T(8,128)S(1)}, u32[]{:S(2)}, u32[]{:S(2)}) collective-permute-start(f32[2,128,128]{2,1,0:T(8,128)S(1)} %get-tuple-element.23), channel_id=1, source_target_pairs={{0,2},{1,3},{2,0},{3,1},{4,6},{5,7},{6,4},{7,5},{8,10},{9,11},{10,... | collective-permute-start | bytes 393224 | tf_op jit(solution)/shard_map/ppermute | solution.py:236
  111.5 2.7 %collective-permute-start.12 = (f32[4,128,128]{2,1,0:T(8,128)S(1)}, f32[4,128,128]{2,1,0:T(8,128)S(1)}, u32[]{:S(2)}, u32[]{:S(2)}) collective-permute-start(f32[4,128,128]{2,1,0:T(8,128)S(1)} %collective-permute-done.11.refs_0_), channel_id=1, source_target_pairs={{0,1},{1,0},{2,3},{3,2},{4,5},{5,4},{6,7},{7,6},{8,9},{9,8},{10,11... | collective-permute-start | bytes 786440 | tf_op jit(solution)/shard_map/ppermute | solution.py:236
  114.2 0.7 collective-permute-done.15.refs_1_
  114.9 3.0 %collective-permute-start.16 = (f32[2,128,128]{2,1,0:T(8,128)S(1)}, f32[2,128,128]{2,1,0:T(8,128)S(1)}, u32[]{:S(2)}, u32[]{:S(2)}) collective-permute-start(f32[2,128,128]{2,1,0:T(8,128)S(1)} %collective-permute-done.15.refs_1_), channel_id=1, source_target_pairs={{0,1},{1,0},{2,3},{3,2},{4,5},{5,4},{6,7},{7,6},{8,9},{9,8},{10,11... | collective-permute-start | bytes 393224 | tf_op jit(solution)/shard_map/ppermute | solution.py:236
  117.9 1.1 blank.1.refs_2_
  119.0 1.4 %shard_map.59.refs_2_ = f32[24,128,128]{2,1,0:T(8,128)} custom-call(s32[24]{0:T(128)S(1)} %get-tuple-element.14.slots, s32[2]{0:T(128)S(1)} %pad_add_fusion.ids, f32[6,128,128]{2,1,0:T(8,128)S(1)} %get-tuple-element.24.refs_0_, f32[6,128,128]{2,1,0:T(8,128)S(1)} %collective-permute-done.17.refs_1_, ...), custom_call_target="tpu_custom_call", output_to_operand_aliasing={{}: (4, {})} | custom-call | bytes 1572864 | tf_op jit(solution)/shard_map/pallas_call | solution.py:389
  120.4 1.3 %shard_map.60.refs_2_ = f32[24,128,128]{2,1,0:T(8,128)} custom-call(s32[24]{0:T(128)S(1)} %get-tuple-element.14.slots, s32[2]{0:T(128)S(1)} %pad_add_fusion.ids, f32[4,128,128]{2,1,0:T(8,128)S(1)} %collective-permute-done.11.refs_0_, f32[2,128,128]{2,1,0:T(8,128)S(1)} %collective-permute-done.15.refs_1_, ...), custom_call_target="tpu_custom_call", output_to_operand_aliasing={{}: (4, {})} | custom-call | bytes 786432 | tf_op jit(solution)/shard_map/pallas_call | solution.py:389
  121.7 1.3 %shard_map.61 = f32[24,128,128]{2,1,0:T(8,128)} custom-call(s32[24]{0:T(128)S(1)} %get-tuple-element.14.slots, s32[2]{0:T(128)S(1)} %pad_add_fusion.ids, f32[4,128,128]{2,1,0:T(8,128)S(1)} %collective-permute-done.12.refs_0_, f32[2,128,128]{2,1,0:T(8,128)S(1)} %collective-permute-done.16.refs_1_, ...), custom_call_target="tpu_custom_call", output_to_operand_aliasing={{}: (4, {})} | custom-call | bytes 786432 | tf_op jit(solution)/shard_map/pallas_call | solution.py:389
  (22 shorter events, 1.2 us)
Async XLA Ops:
  14.4 21.7 %collective-permute-start = (f32[256,128]{1,0:T(8,128)S(1)}, f32[256,128]{1,0:T(8,128)S(1)}, u32[]{:S(2)}, u32[]{:S(2)}) collective-permute-start(f32[256,128]{1,0:T(8,128)S(1)} %bitcast.9), channel_id=1, source_target_pairs={{0,9},{2,19},{4,13},{6,23},{8,17},{9,0},{10,27},{12,21},{13,4},{14... | collective-permute-start | bytes 393224 | tf_op jit(solution)/shard_map/ppermute | solution.py:236
  15.1 23.6 %collective-permute-start.1 = (f32[256,128]{1,0:T(8,128)S(1)}, f32[256,128]{1,0:T(8,128)S(1)}, u32[]{:S(2)}, u32[]{:S(2)}) collective-permute-start(f32[256,128]{1,0:T(8,128)S(1)} %bitcast.10), channel_id=1, source_target_pairs={{0,33},{2,27},{4,37},{6,31},{8,41},{10,35},{12,45},{14,39},{16,49}... | collective-permute-start | bytes 393224 | tf_op jit(solution)/shard_map/ppermute | solution.py:236
  15.8 29.4 %collective-permute-start.4 = (f32[256,128]{1,0:T(8,128)S(1)}, f32[256,128]{1,0:T(8,128)S(1)}, u32[]{:S(2)}, u32[]{:S(2)}) collective-permute-start(f32[256,128]{1,0:T(8,128)S(1)} %bitcast.11), channel_id=1, source_target_pairs={{0,205},{1,308},{2,103},{3,414},{4,209},{5,312},{6,107},{7,418},{8... | collective-permute-start | bytes 393224 | tf_op jit(solution)/shard_map/ppermute | solution.py:236
  34.2 11.1 %collective-permute-start.5 = (f32[256,128]{1,0:T(8,128)S(1)}, f32[256,128]{1,0:T(8,128)S(1)}, u32[]{:S(2)}, u32[]{:S(2)}) collective-permute-start(f32[256,128]{1,0:T(8,128)S(1)} %bitcast.12), channel_id=1, source_target_pairs={{0,5},{1,257},{2,155},{3,362},{4,260},{5,0},{6,159},{7,366},{8,13}... | collective-permute-start | bytes 393224 | tf_op jit(solution)/shard_map/ppermute | solution.py:236
  36.2 9.1 %collective-permute-start.2 = (f32[256,128]{1,0:T(8,128)S(1)}, f32[256,128]{1,0:T(8,128)S(1)}, u32[]{:S(2)}, u32[]{:S(2)}) collective-permute-start(f32[256,128]{1,0:T(8,128)S(1)} %collective-permute-done.refs_0_), channel_id=1, source_target_pairs={{0,4},{1,5},{2,6},{3,7},{4,0},{5,1},{6,2},{7,3},{8,12},{9,13},{10,... | collective-permute-start | bytes 393224 | tf_op jit(solution)/shard_map/ppermute | solution.py:236
  38.7 7.6 %collective-permute-start.3 = (f32[256,128]{1,0:T(8,128)S(1)}, f32[256,128]{1,0:T(8,128)S(1)}, u32[]{:S(2)}, u32[]{:S(2)}) collective-permute-start(f32[256,128]{1,0:T(8,128)S(1)} %collective-permute-done.1.refs_1_), channel_id=1, source_target_pairs={{0,4},{1,5},{2,6},{3,7},{4,0},{5,1},{6,2},{7,3},{8,12},{9,13},{10,... | collective-permute-start | bytes 393224 | tf_op jit(solution)/shard_map/ppermute | solution.py:236
  42.2 0.7 copy-start
  46.8 3.8 %collective-permute-start.6 = (f32[256,128]{1,0:T(8,128)S(1)}, f32[256,128]{1,0:T(8,128)S(1)}, u32[]{:S(2)}, u32[]{:S(2)}) collective-permute-start(f32[256,128]{1,0:T(8,128)S(1)} %partial.1), channel_id=1, source_target_pairs={{0,1},{1,0},{2,3},{3,2},{4,5},{5,4},{6,7},{7,6},{8,9},{9,8},{10,11... | collective-permute-start | bytes 393224 | tf_op jit(solution)/shard_map/ppermute | solution.py:236
  50.7 9.3 %collective-permute-start.7 = (f32[256,128]{1,0:T(8,128)S(1)}, f32[256,128]{1,0:T(8,128)S(1)}, u32[]{:S(2)}, u32[]{:S(2)}) collective-permute-start(f32[256,128]{1,0:T(8,128)S(1)} %add.8.half), channel_id=1, source_target_pairs={{0,2},{1,3},{2,0},{3,1},{4,6},{5,7},{6,4},{7,5},{8,10},{9,11},{10,... | collective-permute-start | bytes 393224 | tf_op jit(solution)/shard_map/ppermute | solution.py:236
  61.4 6.2 %collective-permute-start.8 = (f32[2,128,128]{2,1,0:T(8,128)S(1)}, f32[2,128,128]{2,1,0:T(8,128)S(1)}, u32[]{:S(2)}, u32[]{:S(2)}) collective-permute-start(f32[2,128,128]{2,1,0:T(8,128)S(1)} %get-tuple-element.20.side), channel_id=1, source_target_pairs={{0,4},{1,5},{2,6},{3,7},{4,0},{5,1},{6,2},{7,3},{8,12},{9,13},{10,... | collective-permute-start | bytes 393224 | tf_op jit(solution)/shard_map/ppermute | solution.py:236
  67.6 1.4 %collective-permute-start.10 = (f32[2,128,128]{2,1,0:T(8,128)S(1)}, f32[2,128,128]{2,1,0:T(8,128)S(1)}, u32[]{:S(2)}, u32[]{:S(2)}) collective-permute-start(f32[2,128,128]{2,1,0:T(8,128)S(1)} %pad_maximum_fusion.1), channel_id=1, source_target_pairs={{0,33},{2,27},{4,37},{6,31},{8,41},{10,35},{12,45},{14,39},{16,49}... | collective-permute-start | bytes 393224 | tf_op jit(solution)/shard_map/ppermute | solution.py:236
  68.3 0.7 collective-permute-start.9
  69.2 42.3 %collective-permute-start.11 = (f32[4,128,128]{2,1,0:T(8,128)S(1)}, f32[4,128,128]{2,1,0:T(8,128)S(1)}, u32[]{:S(2)}, u32[]{:S(2)}) collective-permute-start(f32[4,128,128]{2,1,0:T(8,128)S(1)} %update_near.1.near), channel_id=1, source_target_pairs={{0,2},{1,3},{2,0},{3,1},{4,6},{5,7},{6,4},{7,5},{8,10},{9,11},{10,... | collective-permute-start | bytes 786440 | tf_op jit(solution)/shard_map/ppermute | solution.py:236
  73.3 25.1 %collective-permute-start.13 = (f32[128,128]{1,0:T(8,128)S(1)}, f32[128,128]{1,0:T(8,128)S(1)}, u32[]{:S(2)}, u32[]{:S(2)}) collective-permute-start(f32[128,128]{1,0:T(8,128)S(1)} %get-tuple-element.21.far_1), channel_id=1, source_target_pairs={{0,205},{1,308},{2,103},{3,414},{4,209},{5,312},{6,107},{7,418},{8... | collective-permute-start | bytes 196616 | tf_op jit(solution)/shard_map/ppermute | solution.py:236
  92.7 7.6 %collective-permute-start.14 = (f32[128,128]{1,0:T(8,128)S(1)}, f32[128,128]{1,0:T(8,128)S(1)}, u32[]{:S(2)}, u32[]{:S(2)}) collective-permute-start(f32[128,128]{1,0:T(8,128)S(1)} %get-tuple-element.22.far_2), channel_id=1, source_target_pairs={{0,5},{1,257},{2,155},{3,362},{4,260},{5,0},{6,159},{7,366},{8,13}... | collective-permute-start | bytes 196616 | tf_op jit(solution)/shard_map/ppermute | solution.py:236
  100.4 18.6 %collective-permute-start.17 = (f32[6,128,128]{2,1,0:T(8,128)S(1)}, f32[6,128,128]{2,1,0:T(8,128)S(1)}, u32[]{:S(2)}, u32[]{:S(2)}) collective-permute-start(f32[6,128,128]{2,1,0:T(8,128)S(1)} %get-tuple-element.24.refs_0_), channel_id=1, source_target_pairs={{0,1},{1,0},{2,3},{3,2},{4,5},{5,4},{6,7},{7,6},{8,9},{9,8},{10,11... | collective-permute-start | bytes 1179656 | tf_op jit(solution)/shard_map/ppermute | solution.py:236
  104.6 10.3 %collective-permute-start.15 = (f32[2,128,128]{2,1,0:T(8,128)S(1)}, f32[2,128,128]{2,1,0:T(8,128)S(1)}, u32[]{:S(2)}, u32[]{:S(2)}) collective-permute-start(f32[2,128,128]{2,1,0:T(8,128)S(1)} %get-tuple-element.23), channel_id=1, source_target_pairs={{0,2},{1,3},{2,0},{3,1},{4,6},{5,7},{6,4},{7,5},{8,10},{9,11},{10,... | collective-permute-start | bytes 393224 | tf_op jit(solution)/shard_map/ppermute | solution.py:236
  111.5 10.2 %collective-permute-start.12 = (f32[4,128,128]{2,1,0:T(8,128)S(1)}, f32[4,128,128]{2,1,0:T(8,128)S(1)}, u32[]{:S(2)}, u32[]{:S(2)}) collective-permute-start(f32[4,128,128]{2,1,0:T(8,128)S(1)} %collective-permute-done.11.refs_0_), channel_id=1, source_target_pairs={{0,1},{1,0},{2,3},{3,2},{4,5},{5,4},{6,7},{7,6},{8,9},{9,8},{10,11... | collective-permute-start | bytes 786440 | tf_op jit(solution)/shard_map/ppermute | solution.py:236
  114.9 6.8 %collective-permute-start.16 = (f32[2,128,128]{2,1,0:T(8,128)S(1)}, f32[2,128,128]{2,1,0:T(8,128)S(1)}, u32[]{:S(2)}, u32[]{:S(2)}) collective-permute-start(f32[2,128,128]{2,1,0:T(8,128)S(1)} %collective-permute-done.15.refs_1_), channel_id=1, source_target_pairs={{0,1},{1,0},{2,3},{3,2},{4,5},{5,4},{6,7},{7,6},{8,9},{9,8},{10,11... | collective-permute-start | bytes 393224 | tf_op jit(solution)/shard_map/ppermute | solution.py:236

commit v7 on v6

--- a/solution.py
+++ b/solution.py
@@ -16,7 +16,7 @@
 AXES = ("blk", "team")
 NEAR_1, NEAR_2, SIDE_1, SIDE_2, FAR_1, FAR_2 = range(6)
 PLACES = 6
-NEAR = ((2, 8), (4, 6))
+NEAR = ((2, 6), (4, 8))
 FAR = ((51, 0), (25, 38))
 
 
@@ -118,10 +118,10 @@
         high[here, :], low[here, :] = split(x.T)
 
 
-def tile_kernel(ids, half, other, high, low, *outs):
+def tile_kernel(ids, own, mate, across, both_ways, high, low, *outs):
     near_1, near_2, side, far_1, far_2, y_out = outs
     samples_here, block_size = y_out.shape
-    product_high, product_low = split(half[...] + other[...])
+    product_high, product_low = split((own[...] + mate[...]) + (across[...] + both_ways[...]))
 
     def one(x, y):
         return jnp.dot(x, y, preferred_element_type=jnp.float32)
@@ -136,7 +136,8 @@
         else:
             {NEAR_1: near_1, NEAR_2: near_2, FAR_1: far_1, FAR_2: far_2}[k][...] = tile
     start = pl.multiple_of(ids[1] * samples_here, samples_here)
-    y_out[...] = half[pl.ds(start, samples_here), :] + other[pl.ds(start, samples_here), :]
+    here = (pl.ds(start, samples_here), slice(None))
+    y_out[...] = (own[here] + mate[here]) + (across[here] + both_ways[here])
 
 
 def update(before, ours, theirs, samples, corner=None):
@@ -191,8 +192,14 @@
         pltpu.make_async_copy(zero, out.at[s], sems.at[s]).wait()
 
 
-def place_kernel(groups, slots, ids, *refs):
-    out, sems = refs[len(groups) + 1 :]
+def place_kernel(groups, extra, slots, ids, *refs):
+    n = len(groups)
+    if extra:
+        rows_in, _, out, rows_out, sems, rows_sem = refs[n:]
+        rows_copy = pltpu.make_async_copy(rows_in, rows_out, rows_sem)
+        rows_copy.start()
+    else:
+        _, out, sems = refs[n:]
     found = []
     for (j, places), tiles in zip(groups, refs):
         for i, k in enumerate(places):
@@ -205,6 +212,8 @@
         pl.when(condition)(copy.start)
     for condition, copy in found:
         pl.when(condition)(copy.wait)
+    if extra:
+        rows_copy.wait()
 
 
 PARAMS = pltpu.CompilerParams(vmem_limit_bytes=8 * 2**20)
@@ -294,8 +303,12 @@
         compiler_params=PARAMS,
         cost_estimate=cost(2 * PLACES * samples * block_size**2, 14 * samples * block_size * 4),
     )(own_side, old, full, *column)
-    half = partial + permute(partial, lambda b, t: (b, t ^ 1))
-    other = permute(half, lambda b, t: (b, t ^ 2))
+    products = [
+        partial,
+        permute(partial, lambda b, t: (b, t ^ 1)),
+        permute(partial, lambda b, t: (b, t ^ 2)),
+        permute(partial, lambda b, t: (b, t ^ 3)),
+    ]
 
     turned = jax.ShapeDtypeStruct((PLACES * block_size, samples), jnp.bfloat16)
     high, low = pl.pallas_call(
@@ -307,7 +320,7 @@
         compiler_params=PARAMS,
         cost_estimate=cost(0, 14 * samples * block_size * 4),
     )(own_side, full, *column)
-    near_1, near_2, side, far_1, far_2, y_product = pl.pallas_call(
+    near_1, near_2, side, far_1, far_2, own_rows = pl.pallas_call(
         tile_kernel,
         name="tiles",
         out_shape=(
@@ -318,11 +331,11 @@
             tile_shape,
             jax.ShapeDtypeStruct((samples_here, block_size), f32),
         ),
-        in_specs=[SMEM] + [VMEM] * 4,
+        in_specs=[SMEM] + [VMEM] * 6,
         out_specs=(VMEM,) * 6,
         compiler_params=PARAMS,
         cost_estimate=cost(2 * PLACES * samples * block_size**2, 14 * samples * block_size * 4),
-    )(ids, half, other, high, low)
+    )(ids, *products, high, low)
 
     handed = permute(side, beside)
 
@@ -382,25 +395,35 @@
         cost_estimate=cost(0, PLACES * tile_bytes),
     )(counts)
 
-    def place(into, *given):
+    def place(into, own_rows, *given):
         groups = tuple((j, places) for j, places, _ in given)
         count = sum(len(places) for _, places in groups)
-        n = len(groups)
+        extra = own_rows is not None
+        operands = [tiles for _, _, tiles in given] + ([own_rows] if extra else [])
+        n = len(operands)
+        rows_shape = jax.ShapeDtypeStruct((samples_here, block_size), f32)
         return pl.pallas_call(
-            functools.partial(place_kernel, groups),
-            out_shape=tiles_of(slot_count),
+            functools.partial(place_kernel, groups, extra),
+            out_shape=(tiles_of(slot_count), rows_shape) if extra else tiles_of(slot_count),
             in_specs=[SMEM] * 2 + [VMEM] * n + [HBM],
-            out_specs=HBM,
+            out_specs=(HBM, HBM) if extra else HBM,
             input_output_aliases={2 + n: 0},
-            scratch_shapes=[pltpu.SemaphoreType.DMA((count,))],
+            scratch_shapes=[pltpu.SemaphoreType.DMA((count,))]
+            + ([pltpu.SemaphoreType.DMA] if extra else []),
             compiler_params=PARAMS,
             cost_estimate=cost(0, 2 * count * tile_bytes),
-        )(slots, ids, *(tiles for _, _, tiles in given), into)
+        )(slots, ids, *operands, into)
 
     every = tuple(range(PLACES))
-    new_omega = place(new_omega, (0, every, all_tiles), (1, every, mate))
-    new_omega = place(new_omega, (2, NEAR_PLACES, near_across), (2, FAR_PLACES, far_across))
-    new_omega = place(new_omega, (3, NEAR_PLACES, near_last), (3, FAR_PLACES, far_last))
+    new_omega, y_product = place(
+        new_omega,
+        own_rows,
+        (0, every, all_tiles),
+        (1, every, mate),
+        (2, NEAR_PLACES, near_across),
+        (2, FAR_PLACES, far_across),
+    )
+    new_omega = place(new_omega, None, (3, NEAR_PLACES, near_last), (3, FAR_PLACES, far_last))
     return (new_omega[None], y_product[None])
 
 

time: 124 us -> 127 us (1.024)
  the two profiles are of different devices: /device:TPU:1 before, /device:TPU:9 now
where the time goes in v7:
time: 127 us
  starting transfers between devices  76 us (60%)
  waiting for transfers between devices  32.3 us (25%)
  Pallas kernels  8.25 us (6%)
  blocking collectives  7.64 us (6%)
  between operations  1.6 us (1%)
    ppermute x19, starting transfers between devices, permute(): return lax.ppermute(x, AXES, pairs)  76 us
    ppermute x19, waiting for transfers between devices, permute(): return lax.ppermute(x, AXES, pairs)  32.3 us
    all_gather x1, blocking collectives, step(): full = lax.all_gather(own_dosage, 'team', axis=0, tiled=True)  7.64 us
    pallas_call x2, Pallas kernels, place(): pl.pallas_call(functools.partial(place_kernel, groups, extra), out_shape=...  2.79 us
  transfers between devices with their start and end apart: 19, of which 8 were waited for; matrix products, arithmetic and copies ran while one was open for 0% of the time, Pallas kernels for 4%

profile of v7, /device:TPU:9, one launch (start us, length us, event | category | flops | bytes accessed | tf_op | source)
XLA Modules:
  0.0 126.6 jit_solution(15910948578919790626)
XLA Ops:
  0.6 7.6 %all-gather = f32[1,256,128]{2,1,0:T(8,128)S(1)} all-gather(f32[1,64,128]{2,1,0:T(8,128)} %param.5), channel_id=2, replica_groups=mesh['blk'=128,'team'=4] {'team'}, dimensions={1}, use_global_device_ids=true | all-gather | bytes 163840 | tf_op jit(solution)/shard_map/all_gather | solution.py:288
  8.3 11.0 %collective-permute-start = (f32[256,128]{1,0:T(8,128)S(1)}, f32[256,128]{1,0:T(8,128)S(1)}, u32[]{:S(2)}, u32[]{:S(2)}) collective-permute-start(f32[256,128]{1,0:T(8,128)S(1)} %bitcast.9), channel_id=1, source_target_pairs={{0,9},{2,19},{4,13},{6,23},{8,17},{9,0},{10,27},{12,21},{13,4},{14... | collective-permute-start | bytes 393224 | tf_op jit(solution)/shard_map/ppermute | solution.py:245
  19.3 3.8 %collective-permute-start.1 = (f32[256,128]{1,0:T(8,128)S(1)}, f32[256,128]{1,0:T(8,128)S(1)}, u32[]{:S(2)}, u32[]{:S(2)}) collective-permute-start(f32[256,128]{1,0:T(8,128)S(1)} %bitcast.10), channel_id=1, source_target_pairs={{0,25},{2,35},{4,29},{6,39},{8,33},{10,43},{12,37},{14,47},{16,41}... | collective-permute-start | bytes 393224 | tf_op jit(solution)/shard_map/ppermute | solution.py:245
  23.1 8.9 %collective-permute-start.4 = (f32[256,128]{1,0:T(8,128)S(1)}, f32[256,128]{1,0:T(8,128)S(1)}, u32[]{:S(2)}, u32[]{:S(2)}) collective-permute-start(f32[256,128]{1,0:T(8,128)S(1)} %bitcast.11), channel_id=1, source_target_pairs={{0,205},{1,308},{2,103},{3,414},{4,209},{5,312},{6,107},{7,418},{8... | collective-permute-start | bytes 393224 | tf_op jit(solution)/shard_map/ppermute | solution.py:245
  32.0 2.9 %collective-permute-start.5 = (f32[256,128]{1,0:T(8,128)S(1)}, f32[256,128]{1,0:T(8,128)S(1)}, u32[]{:S(2)}, u32[]{:S(2)}) collective-permute-start(f32[256,128]{1,0:T(8,128)S(1)} %bitcast.12), channel_id=1, source_target_pairs={{0,5},{1,257},{2,155},{3,362},{4,260},{5,0},{6,159},{7,366},{8,13}... | collective-permute-start | bytes 393224 | tf_op jit(solution)/shard_map/ppermute | solution.py:245
  34.9 1.9 %collective-permute-start.2 = (f32[256,128]{1,0:T(8,128)S(1)}, f32[256,128]{1,0:T(8,128)S(1)}, u32[]{:S(2)}, u32[]{:S(2)}) collective-permute-start(f32[256,128]{1,0:T(8,128)S(1)} %collective-permute-done.refs_0_), channel_id=1, source_target_pairs={{0,4},{1,5},{2,6},{3,7},{4,0},{5,1},{6,2},{7,3},{8,12},{9,13},{10,... | collective-permute-start | bytes 393224 | tf_op jit(solution)/shard_map/ppermute | solution.py:245
  36.8 3.4 %collective-permute-start.3 = (f32[256,128]{1,0:T(8,128)S(1)}, f32[256,128]{1,0:T(8,128)S(1)}, u32[]{:S(2)}, u32[]{:S(2)}) collective-permute-start(f32[256,128]{1,0:T(8,128)S(1)} %collective-permute-done.1.refs_1_), channel_id=1, source_target_pairs={{0,4},{1,5},{2,6},{3,7},{4,0},{5,1},{6,2},{7,3},{8,12},{9,13},{10,... | collective-permute-start | bytes 393224 | tf_op jit(solution)/shard_map/ppermute | solution.py:245
  41.6 2.4 %pick.1 = (s32[24]{0:T(128)S(1)}, f32[6,128,128]{2,1,0:T(8,128)S(1)}) custom-call(s32[2]{0:T(128)S(1)} %pad_add_fusion.ids, s32[1,24]{1,0:T(1,128)S(1)} %copy-done, s32[1]{0:T(128)S(6)} %copy.10.counts, f32[24,128,128]{2,1,0:T(8,128)} %bitcast.18), custom_call_target="tpu_custom_call" | custom-call | bytes 786432 | tf_op jit(solution)/shard_map/pick/pallas_call | solution.py:277
  44.0 2.4 %collective-permute-done.3.refs_3_ = f32[256,128]{1,0:T(8,128)S(1)} collective-permute-done((f32[256,128]{1,0:T(8,128)S(1)}, f32[256,128]{1,0:T(8,128)S(1)}, u32[]{:S(2)}, u32[]{:S(2)}) %collective-permute-start.3) | collective-permute-done | bytes 131104 | tf_op jit(solution)/shard_map/ppermute | solution.py:245
  46.9 2.5 %collective-permute-start.6 = (f32[256,128]{1,0:T(8,128)S(1)}, f32[256,128]{1,0:T(8,128)S(1)}, u32[]{:S(2)}, u32[]{:S(2)}) collective-permute-start(f32[256,128]{1,0:T(8,128)S(1)} %partial.1.own), channel_id=1, source_target_pairs={{0,1},{1,0},{2,3},{3,2},{4,5},{5,4},{6,7},{7,6},{8,9},{9,8},{10,11... | collective-permute-start | bytes 393224 | tf_op jit(solution)/shard_map/ppermute | solution.py:245
  49.5 5.3 %collective-permute-start.7 = (f32[256,128]{1,0:T(8,128)S(1)}, f32[256,128]{1,0:T(8,128)S(1)}, u32[]{:S(2)}, u32[]{:S(2)}) collective-permute-start(f32[256,128]{1,0:T(8,128)S(1)} %partial.1.own), channel_id=1, source_target_pairs={{0,2},{1,3},{2,0},{3,1},{4,6},{5,7},{6,4},{7,5},{8,10},{9,11},{10,... | collective-permute-start | bytes 393224 | tf_op jit(solution)/shard_map/ppermute | solution.py:245
  54.8 2.3 %collective-permute-start.8 = (f32[256,128]{1,0:T(8,128)S(1)}, f32[256,128]{1,0:T(8,128)S(1)}, u32[]{:S(2)}, u32[]{:S(2)}) collective-permute-start(f32[256,128]{1,0:T(8,128)S(1)} %partial.1.own), channel_id=1, source_target_pairs={{0,3},{1,2},{2,1},{3,0},{4,7},{5,6},{6,5},{7,4},{8,11},{9,10},{10,... | collective-permute-start | bytes 393224 | tf_op jit(solution)/shard_map/ppermute | solution.py:245
  58.1 6.0 %collective-permute-done.8.both_ways = f32[256,128]{1,0:T(8,128)S(1)} collective-permute-done((f32[256,128]{1,0:T(8,128)S(1)}, f32[256,128]{1,0:T(8,128)S(1)}, u32[]{:S(2)}, u32[]{:S(2)}) %collective-permute-start.8) | collective-permute-done | bytes 131104 | tf_op jit(solution)/shard_map/ppermute | solution.py:245
  64.2 0.9 tiles.1
  65.1 2.8 %collective-permute-start.9 = (f32[2,128,128]{2,1,0:T(8,128)S(1)}, f32[2,128,128]{2,1,0:T(8,128)S(1)}, u32[]{:S(2)}, u32[]{:S(2)}) collective-permute-start(f32[2,128,128]{2,1,0:T(8,128)S(1)} %get-tuple-element.22.side), channel_id=1, source_target_pairs={{0,4},{1,5},{2,6},{3,7},{4,0},{5,1},{6,2},{7,3},{8,12},{9,13},{10,... | collective-permute-start | bytes 393224 | tf_op jit(solution)/shard_map/ppermute | solution.py:245
  67.9 3.6 %collective-permute-done.9 = f32[2,128,128]{2,1,0:T(8,128)S(1)} collective-permute-done((f32[2,128,128]{2,1,0:T(8,128)S(1)}, f32[2,128,128]{2,1,0:T(8,128)S(1)}, u32[]{:S(2)}, u32[]{:S(2)}) %collective-permute-start.9) | collective-permute-done | bytes 131104 | tf_op jit(solution)/shard_map/ppermute | solution.py:245
  71.6 4.0 %collective-permute-start.11 = (f32[2,128,128]{2,1,0:T(8,128)S(1)}, f32[2,128,128]{2,1,0:T(8,128)S(1)}, u32[]{:S(2)}, u32[]{:S(2)}) collective-permute-start(f32[2,128,128]{2,1,0:T(8,128)S(1)} %pad_maximum_fusion.1), channel_id=1, source_target_pairs={{0,25},{2,35},{4,29},{6,39},{8,33},{10,43},{12,37},{14,47},{16,41}... | collective-permute-start | bytes 393224 | tf_op jit(solution)/shard_map/ppermute | solution.py:245
  75.6 3.2 %collective-permute-start.10 = (f32[2,128,128]{2,1,0:T(8,128)S(1)}, f32[2,128,128]{2,1,0:T(8,128)S(1)}, u32[]{:S(2)}, u32[]{:S(2)}) collective-permute-start(f32[2,128,128]{2,1,0:T(8,128)S(1)} %pad_maximum_fusion), channel_id=1, source_target_pairs={{0,9},{2,19},{4,13},{6,23},{8,17},{9,0},{10,27},{12,21},{13,4},{14... | collective-permute-start | bytes 393224 | tf_op jit(solution)/shard_map/ppermute | solution.py:245
  78.7 4.0 %collective-permute-done.11.got_2 = f32[2,128,128]{2,1,0:T(8,128)S(1)} collective-permute-done((f32[2,128,128]{2,1,0:T(8,128)S(1)}, f32[2,128,128]{2,1,0:T(8,128)S(1)}, u32[]{:S(2)}, u32[]{:S(2)}) %collective-permute-start.11) | collective-permute-done | bytes 131104 | tf_op jit(solution)/shard_map/ppermute | solution.py:245
  82.7 1.4 %collective-permute-done.10.got_1 = f32[2,128,128]{2,1,0:T(8,128)S(1)} collective-permute-done((f32[2,128,128]{2,1,0:T(8,128)S(1)}, f32[2,128,128]{2,1,0:T(8,128)S(1)}, u32[]{:S(2)}, u32[]{:S(2)}) %collective-permute-start.10) | collective-permute-done | bytes 131104 | tf_op jit(solution)/shard_map/ppermute | solution.py:245
  84.3 6.4 %collective-permute-start.12 = (f32[4,128,128]{2,1,0:T(8,128)S(1)}, f32[4,128,128]{2,1,0:T(8,128)S(1)}, u32[]{:S(2)}, u32[]{:S(2)}) collective-permute-start(f32[4,128,128]{2,1,0:T(8,128)S(1)} %update_near.1.near), channel_id=1, source_target_pairs={{0,2},{1,3},{2,0},{3,1},{4,6},{5,7},{6,4},{7,5},{8,10},{9,11},{10,... | collective-permute-start | bytes 786440 | tf_op jit(solution)/shard_map/ppermute | solution.py:245
  90.7 6.7 %collective-permute-start.14 = (f32[128,128]{1,0:T(8,128)S(1)}, f32[128,128]{1,0:T(8,128)S(1)}, u32[]{:S(2)}, u32[]{:S(2)}) collective-permute-start(f32[128,128]{1,0:T(8,128)S(1)} %get-tuple-element.23.far_1), channel_id=1, source_target_pairs={{0,205},{1,308},{2,103},{3,414},{4,209},{5,312},{6,107},{7,418},{8... | collective-permute-start | bytes 196616 | tf_op jit(solution)/shard_map/ppermute | solution.py:245
  97.4 1.9 %collective-permute-start.15 = (f32[128,128]{1,0:T(8,128)S(1)}, f32[128,128]{1,0:T(8,128)S(1)}, u32[]{:S(2)}, u32[]{:S(2)}) collective-permute-start(f32[128,128]{1,0:T(8,128)S(1)} %get-tuple-element.24.far_2), channel_id=1, source_target_pairs={{0,5},{1,257},{2,155},{3,362},{4,260},{5,0},{6,159},{7,366},{8,13}... | collective-permute-start | bytes 196616 | tf_op jit(solution)/shard_map/ppermute | solution.py:245
  99.3 9.7 %collective-permute-done.14.got_1 = f32[128,128]{1,0:T(8,128)S(1)} collective-permute-done((f32[128,128]{1,0:T(8,128)S(1)}, f32[128,128]{1,0:T(8,128)S(1)}, u32[]{:S(2)}, u32[]{:S(2)}) %collective-permute-start.14) | collective-permute-done | bytes 65568 | tf_op jit(solution)/shard_map/ppermute | solution.py:245
  109.1 2.3 %collective-permute-start.18 = (f32[6,128,128]{2,1,0:T(8,128)S(1)}, f32[6,128,128]{2,1,0:T(8,128)S(1)}, u32[]{:S(2)}, u32[]{:S(2)}) collective-permute-start(f32[6,128,128]{2,1,0:T(8,128)S(1)} %get-tuple-element.26.refs_0_), channel_id=1, source_target_pairs={{0,1},{1,0},{2,3},{3,2},{4,5},{5,4},{6,7},{7,6},{8,9},{9,8},{10,11... | collective-permute-start | bytes 1179656 | tf_op jit(solution)/shard_map/ppermute | solution.py:245
  111.4 1.9 %collective-permute-start.16 = (f32[2,128,128]{2,1,0:T(8,128)S(1)}, f32[2,128,128]{2,1,0:T(8,128)S(1)}, u32[]{:S(2)}, u32[]{:S(2)}) collective-permute-start(f32[2,128,128]{2,1,0:T(8,128)S(1)} %get-tuple-element.25), channel_id=1, source_target_pairs={{0,2},{1,3},{2,0},{3,1},{4,6},{5,7},{6,4},{7,5},{8,10},{9,11},{10,... | collective-permute-start | bytes 393224 | tf_op jit(solution)/shard_map/ppermute | solution.py:245
  113.3 2.0 %collective-permute-start.13 = (f32[4,128,128]{2,1,0:T(8,128)S(1)}, f32[4,128,128]{2,1,0:T(8,128)S(1)}, u32[]{:S(2)}, u32[]{:S(2)}) collective-permute-start(f32[4,128,128]{2,1,0:T(8,128)S(1)} %collective-permute-done.12.refs_2_), channel_id=1, source_target_pairs={{0,1},{1,0},{2,3},{3,2},{4,5},{5,4},{6,7},{7,6},{8,9},{9,8},{10,11... | collective-permute-start | bytes 786440 | tf_op jit(solution)/shard_map/ppermute | solution.py:245
  115.4 4.4 %collective-permute-done.16.refs_3_ = f32[2,128,128]{2,1,0:T(8,128)S(1)} collective-permute-done((f32[2,128,128]{2,1,0:T(8,128)S(1)}, f32[2,128,128]{2,1,0:T(8,128)S(1)}, u32[]{:S(2)}, u32[]{:S(2)}) %collective-permute-start.16) | collective-permute-done | bytes 131104 | tf_op jit(solution)/shard_map/ppermute | solution.py:245
  119.7 2.9 %collective-permute-start.17 = (f32[2,128,128]{2,1,0:T(8,128)S(1)}, f32[2,128,128]{2,1,0:T(8,128)S(1)}, u32[]{:S(2)}, u32[]{:S(2)}) collective-permute-start(f32[2,128,128]{2,1,0:T(8,128)S(1)} %collective-permute-done.16.refs_3_), channel_id=1, source_target_pairs={{0,1},{1,0},{2,3},{3,2},{4,5},{5,4},{6,7},{7,6},{8,9},{9,8},{10,11... | collective-permute-start | bytes 393224 | tf_op jit(solution)/shard_map/ppermute | solution.py:245
  122.6 1.1 blank.1.refs_5_
  123.8 1.5 %shard_map.59 = (f32[24,128,128]{2,1,0:T(8,128)}, f32[64,128]{1,0:T(8,128)}) custom-call(s32[24]{0:T(128)S(1)} %get-tuple-element.16.slots, s32[2]{0:T(128)S(1)} %pad_add_fusion.ids, f32[6,128,128]{2,1,0:T(8,128)S(1)} %get-tuple-element.26.refs_0_, f32[6,128,128]{2,1,0:T(8,128)S(1)} %collective-permute-done.18.refs_1_, ...), custom_call_target="tpu_custom_call", output_to_operand_aliasing={{0}: (7, {})} | custom-call | bytes 2359296 | tf_op jit(solution)/shard_map/pallas_call | solution.py:405
  125.3 1.3 %shard_map.60 = f32[24,128,128]{2,1,0:T(8,128)} custom-call(s32[24]{0:T(128)S(1)} %get-tuple-element.16.slots, s32[2]{0:T(128)S(1)} %pad_add_fusion.ids, f32[4,128,128]{2,1,0:T(8,128)S(1)} %collective-permute-done.13.refs_0_, f32[2,128,128]{2,1,0:T(8,128)S(1)} %collective-permute-done.17.refs_1_, ...), custom_call_target="tpu_custom_call", output_to_operand_aliasing={{}: (4, {})} | custom-call | bytes 786432 | tf_op jit(solution)/shard_map/pallas_call | solution.py:405
  (22 shorter events, 2.6 us)
Async XLA Ops:
  8.3 26.6 %collective-permute-start = (f32[256,128]{1,0:T(8,128)S(1)}, f32[256,128]{1,0:T(8,128)S(1)}, u32[]{:S(2)}, u32[]{:S(2)}) collective-permute-start(f32[256,128]{1,0:T(8,128)S(1)} %bitcast.9), channel_id=1, source_target_pairs={{0,9},{2,19},{4,13},{6,23},{8,17},{9,0},{10,27},{12,21},{13,4},{14... | collective-permute-start | bytes 393224 | tf_op jit(solution)/shard_map/ppermute | solution.py:245
  19.3 17.5 %collective-permute-start.1 = (f32[256,128]{1,0:T(8,128)S(1)}, f32[256,128]{1,0:T(8,128)S(1)}, u32[]{:S(2)}, u32[]{:S(2)}) collective-permute-start(f32[256,128]{1,0:T(8,128)S(1)} %bitcast.10), channel_id=1, source_target_pairs={{0,25},{2,35},{4,29},{6,39},{8,33},{10,43},{12,37},{14,47},{16,41}... | collective-permute-start | bytes 393224 | tf_op jit(solution)/shard_map/ppermute | solution.py:245
  23.1 20.9 %collective-permute-start.4 = (f32[256,128]{1,0:T(8,128)S(1)}, f32[256,128]{1,0:T(8,128)S(1)}, u32[]{:S(2)}, u32[]{:S(2)}) collective-permute-start(f32[256,128]{1,0:T(8,128)S(1)} %bitcast.11), channel_id=1, source_target_pairs={{0,205},{1,308},{2,103},{3,414},{4,209},{5,312},{6,107},{7,418},{8... | collective-permute-start | bytes 393224 | tf_op jit(solution)/shard_map/ppermute | solution.py:245
  32.0 12.0 %collective-permute-start.5 = (f32[256,128]{1,0:T(8,128)S(1)}, f32[256,128]{1,0:T(8,128)S(1)}, u32[]{:S(2)}, u32[]{:S(2)}) collective-permute-start(f32[256,128]{1,0:T(8,128)S(1)} %bitcast.12), channel_id=1, source_target_pairs={{0,5},{1,257},{2,155},{3,362},{4,260},{5,0},{6,159},{7,366},{8,13}... | collective-permute-start | bytes 393224 | tf_op jit(solution)/shard_map/ppermute | solution.py:245
  34.9 9.1 %collective-permute-start.2 = (f32[256,128]{1,0:T(8,128)S(1)}, f32[256,128]{1,0:T(8,128)S(1)}, u32[]{:S(2)}, u32[]{:S(2)}) collective-permute-start(f32[256,128]{1,0:T(8,128)S(1)} %collective-permute-done.refs_0_), channel_id=1, source_target_pairs={{0,4},{1,5},{2,6},{3,7},{4,0},{5,1},{6,2},{7,3},{8,12},{9,13},{10,... | collective-permute-start | bytes 393224 | tf_op jit(solution)/shard_map/ppermute | solution.py:245
  36.8 9.6 %collective-permute-start.3 = (f32[256,128]{1,0:T(8,128)S(1)}, f32[256,128]{1,0:T(8,128)S(1)}, u32[]{:S(2)}, u32[]{:S(2)}) collective-permute-start(f32[256,128]{1,0:T(8,128)S(1)} %collective-permute-done.1.refs_1_), channel_id=1, source_target_pairs={{0,4},{1,5},{2,6},{3,7},{4,0},{5,1},{6,2},{7,3},{8,12},{9,13},{10,... | collective-permute-start | bytes 393224 | tf_op jit(solution)/shard_map/ppermute | solution.py:245
  40.9 0.7 copy-start
  46.9 10.4 %collective-permute-start.6 = (f32[256,128]{1,0:T(8,128)S(1)}, f32[256,128]{1,0:T(8,128)S(1)}, u32[]{:S(2)}, u32[]{:S(2)}) collective-permute-start(f32[256,128]{1,0:T(8,128)S(1)} %partial.1.own), channel_id=1, source_target_pairs={{0,1},{1,0},{2,3},{3,2},{4,5},{5,4},{6,7},{7,6},{8,9},{9,8},{10,11... | collective-permute-start | bytes 393224 | tf_op jit(solution)/shard_map/ppermute | solution.py:245
  49.5 8.7 %collective-permute-start.7 = (f32[256,128]{1,0:T(8,128)S(1)}, f32[256,128]{1,0:T(8,128)S(1)}, u32[]{:S(2)}, u32[]{:S(2)}) collective-permute-start(f32[256,128]{1,0:T(8,128)S(1)} %partial.1.own), channel_id=1, source_target_pairs={{0,2},{1,3},{2,0},{3,1},{4,6},{5,7},{6,4},{7,5},{8,10},{9,11},{10,... | collective-permute-start | bytes 393224 | tf_op jit(solution)/shard_map/ppermute | solution.py:245
  54.8 9.4 %collective-permute-start.8 = (f32[256,128]{1,0:T(8,128)S(1)}, f32[256,128]{1,0:T(8,128)S(1)}, u32[]{:S(2)}, u32[]{:S(2)}) collective-permute-start(f32[256,128]{1,0:T(8,128)S(1)} %partial.1.own), channel_id=1, source_target_pairs={{0,3},{1,2},{2,1},{3,0},{4,7},{5,6},{6,5},{7,4},{8,11},{9,10},{10,... | collective-permute-start | bytes 393224 | tf_op jit(solution)/shard_map/ppermute | solution.py:245
  65.1 6.5 %collective-permute-start.9 = (f32[2,128,128]{2,1,0:T(8,128)S(1)}, f32[2,128,128]{2,1,0:T(8,128)S(1)}, u32[]{:S(2)}, u32[]{:S(2)}) collective-permute-start(f32[2,128,128]{2,1,0:T(8,128)S(1)} %get-tuple-element.22.side), channel_id=1, source_target_pairs={{0,4},{1,5},{2,6},{3,7},{4,0},{5,1},{6,2},{7,3},{8,12},{9,13},{10,... | collective-permute-start | bytes 393224 | tf_op jit(solution)/shard_map/ppermute | solution.py:245
  71.6 11.1 %collective-permute-start.11 = (f32[2,128,128]{2,1,0:T(8,128)S(1)}, f32[2,128,128]{2,1,0:T(8,128)S(1)}, u32[]{:S(2)}, u32[]{:S(2)}) collective-permute-start(f32[2,128,128]{2,1,0:T(8,128)S(1)} %pad_maximum_fusion.1), channel_id=1, source_target_pairs={{0,25},{2,35},{4,29},{6,39},{8,33},{10,43},{12,37},{14,47},{16,41}... | collective-permute-start | bytes 393224 | tf_op jit(solution)/shard_map/ppermute | solution.py:245
  75.6 8.5 %collective-permute-start.10 = (f32[2,128,128]{2,1,0:T(8,128)S(1)}, f32[2,128,128]{2,1,0:T(8,128)S(1)}, u32[]{:S(2)}, u32[]{:S(2)}) collective-permute-start(f32[2,128,128]{2,1,0:T(8,128)S(1)} %pad_maximum_fusion), channel_id=1, source_target_pairs={{0,9},{2,19},{4,13},{6,23},{8,17},{9,0},{10,27},{12,21},{13,4},{14... | collective-permute-start | bytes 393224 | tf_op jit(solution)/shard_map/ppermute | solution.py:245
  84.3 29.0 %collective-permute-start.12 = (f32[4,128,128]{2,1,0:T(8,128)S(1)}, f32[4,128,128]{2,1,0:T(8,128)S(1)}, u32[]{:S(2)}, u32[]{:S(2)}) collective-permute-start(f32[4,128,128]{2,1,0:T(8,128)S(1)} %update_near.1.near), channel_id=1, source_target_pairs={{0,2},{1,3},{2,0},{3,1},{4,6},{5,7},{6,4},{7,5},{8,10},{9,11},{10,... | collective-permute-start | bytes 786440 | tf_op jit(solution)/shard_map/ppermute | solution.py:245
  90.7 18.2 %collective-permute-start.14 = (f32[128,128]{1,0:T(8,128)S(1)}, f32[128,128]{1,0:T(8,128)S(1)}, u32[]{:S(2)}, u32[]{:S(2)}) collective-permute-start(f32[128,128]{1,0:T(8,128)S(1)} %get-tuple-element.23.far_1), channel_id=1, source_target_pairs={{0,205},{1,308},{2,103},{3,414},{4,209},{5,312},{6,107},{7,418},{8... | collective-permute-start | bytes 196616 | tf_op jit(solution)/shard_map/ppermute | solution.py:245
  97.4 11.6 %collective-permute-start.15 = (f32[128,128]{1,0:T(8,128)S(1)}, f32[128,128]{1,0:T(8,128)S(1)}, u32[]{:S(2)}, u32[]{:S(2)}) collective-permute-start(f32[128,128]{1,0:T(8,128)S(1)} %get-tuple-element.24.far_2), channel_id=1, source_target_pairs={{0,5},{1,257},{2,155},{3,362},{4,260},{5,0},{6,159},{7,366},{8,13}... | collective-permute-start | bytes 196616 | tf_op jit(solution)/shard_map/ppermute | solution.py:245
  109.1 14.7 %collective-permute-start.18 = (f32[6,128,128]{2,1,0:T(8,128)S(1)}, f32[6,128,128]{2,1,0:T(8,128)S(1)}, u32[]{:S(2)}, u32[]{:S(2)}) collective-permute-start(f32[6,128,128]{2,1,0:T(8,128)S(1)} %get-tuple-element.26.refs_0_), channel_id=1, source_target_pairs={{0,1},{1,0},{2,3},{3,2},{4,5},{5,4},{6,7},{7,6},{8,9},{9,8},{10,11... | collective-permute-start | bytes 1179656 | tf_op jit(solution)/shard_map/ppermute | solution.py:245
  111.4 8.3 %collective-permute-start.16 = (f32[2,128,128]{2,1,0:T(8,128)S(1)}, f32[2,128,128]{2,1,0:T(8,128)S(1)}, u32[]{:S(2)}, u32[]{:S(2)}) collective-permute-start(f32[2,128,128]{2,1,0:T(8,128)S(1)} %get-tuple-element.25), channel_id=1, source_target_pairs={{0,2},{1,3},{2,0},{3,1},{4,6},{5,7},{6,4},{7,5},{8,10},{9,11},{10,... | collective-permute-start | bytes 393224 | tf_op jit(solution)/shard_map/ppermute | solution.py:245
  113.3 11.9 %collective-permute-start.13 = (f32[4,128,128]{2,1,0:T(8,128)S(1)}, f32[4,128,128]{2,1,0:T(8,128)S(1)}, u32[]{:S(2)}, u32[]{:S(2)}) collective-permute-start(f32[4,128,128]{2,1,0:T(8,128)S(1)} %collective-permute-done.12.refs_2_), channel_id=1, source_target_pairs={{0,1},{1,0},{2,3},{3,2},{4,5},{5,4},{6,7},{7,6},{8,9},{9,8},{10,11... | collective-permute-start | bytes 786440 | tf_op jit(solution)/shard_map/ppermute | solution.py:245
  119.7 5.5 %collective-permute-start.17 = (f32[2,128,128]{2,1,0:T(8,128)S(1)}, f32[2,128,128]{2,1,0:T(8,128)S(1)}, u32[]{:S(2)}, u32[]{:S(2)}) collective-permute-start(f32[2,128,128]{2,1,0:T(8,128)S(1)} %collective-permute-done.16.refs_3_), channel_id=1, source_target_pairs={{0,1},{1,0},{2,3},{3,2},{4,5},{5,4},{6,7},{7,6},{8,9},{9,8},{10,11... | collective-permute-start | bytes 393224 | tf_op jit(solution)/shard_map/ppermute | solution.py:245

commit v8 on v7

--- a/solution.py
+++ b/solution.py
@@ -16,7 +16,7 @@
 AXES = ("blk", "team")
 NEAR_1, NEAR_2, SIDE_1, SIDE_2, FAR_1, FAR_2 = range(6)
 PLACES = 6
-NEAR = ((2, 6), (4, 8))
+NEAR = ((2, 6), (-4, -8))
 FAR = ((51, 0), (25, 38))
 
 
@@ -118,10 +118,10 @@
         high[here, :], low[here, :] = split(x.T)
 
 
-def tile_kernel(ids, own, mate, across, both_ways, high, low, *outs):
+def tile_kernel(ids, half, other, high, low, *outs):
     near_1, near_2, side, far_1, far_2, y_out = outs
     samples_here, block_size = y_out.shape
-    product_high, product_low = split((own[...] + mate[...]) + (across[...] + both_ways[...]))
+    product_high, product_low = split(half[...] + other[...])
 
     def one(x, y):
         return jnp.dot(x, y, preferred_element_type=jnp.float32)
@@ -136,8 +136,7 @@
         else:
             {NEAR_1: near_1, NEAR_2: near_2, FAR_1: far_1, FAR_2: far_2}[k][...] = tile
     start = pl.multiple_of(ids[1] * samples_here, samples_here)
-    here = (pl.ds(start, samples_here), slice(None))
-    y_out[...] = (own[here] + mate[here]) + (across[here] + both_ways[here])
+    y_out[...] = half[pl.ds(start, samples_here), :] + other[pl.ds(start, samples_here), :]
 
 
 def update(before, ours, theirs, samples, corner=None):
@@ -303,12 +302,8 @@
         compiler_params=PARAMS,
         cost_estimate=cost(2 * PLACES * samples * block_size**2, 14 * samples * block_size * 4),
     )(own_side, old, full, *column)
-    products = [
-        partial,
-        permute(partial, lambda b, t: (b, t ^ 1)),
-        permute(partial, lambda b, t: (b, t ^ 2)),
-        permute(partial, lambda b, t: (b, t ^ 3)),
-    ]
+    half = partial + permute(partial, lambda b, t: (b, t ^ 1))
+    other = permute(half, lambda b, t: (b, t ^ 2))
 
     turned = jax.ShapeDtypeStruct((PLACES * block_size, samples), jnp.bfloat16)
     high, low = pl.pallas_call(
@@ -331,11 +326,11 @@
             tile_shape,
             jax.ShapeDtypeStruct((samples_here, block_size), f32),
         ),
-        in_specs=[SMEM] + [VMEM] * 6,
+        in_specs=[SMEM] + [VMEM] * 4,
         out_specs=(VMEM,) * 6,
         compiler_params=PARAMS,
         cost_estimate=cost(2 * PLACES * samples * block_size**2, 14 * samples * block_size * 4),
-    )(ids, *products, high, low)
+    )(ids, half, other, high, low)
 
     handed = permute(side, beside)
 

time: 127 us -> 125 us (0.984)
  the two profiles are of different devices: /device:TPU:9 before, /device:TPU:25 now
where the time goes in v8:
time: 125 us
  starting transfers between devices  80.1 us (64%)
  waiting for transfers between devices  26.2 us (21%)
  Pallas kernels  8.26 us (7%)
  blocking collectives  7.64 us (6%)
  between operations  1.59 us (1%)
    ppermute x18, starting transfers between devices, permute(): return lax.ppermute(x, AXES, pairs)  80.1 us
    ppermute x18, waiting for transfers between devices, permute(): return lax.ppermute(x, AXES, pairs)  26.2 us
    all_gather x1, blocking collectives, step(): full = lax.all_gather(own_dosage, 'team', axis=0, tiled=True)  7.64 us
    pallas_call x2, Pallas kernels, place(): pl.pallas_call(functools.partial(place_kernel, groups, extra), out_shape=...  2.79 us
  transfers between devices with their start and end apart: 18, of which 8 were waited for; matrix products, arithmetic and copies ran while one was open for 0% of the time, Pallas kernels for 4%

profile of v8, /device:TPU:25, one launch (start us, length us, event | category | flops | bytes accessed | tf_op | source)
XLA Modules:
  0.0 124.5 jit_solution(3756743868490369605)
XLA Ops:
  0.6 7.6 %all-gather = f32[1,256,128]{2,1,0:T(8,128)S(1)} all-gather(f32[1,64,128]{2,1,0:T(8,128)} %param.5), channel_id=2, replica_groups=mesh['blk'=128,'team'=4] {'team'}, dimensions={1}, use_global_device_ids=true | all-gather | bytes 163840 | tf_op jit(solution)/shard_map/all_gather | solution.py:287
  8.3 11.3 %collective-permute-start = (f32[256,128]{1,0:T(8,128)S(1)}, f32[256,128]{1,0:T(8,128)S(1)}, u32[]{:S(2)}, u32[]{:S(2)}) collective-permute-start(f32[256,128]{1,0:T(8,128)S(1)} %bitcast.9), channel_id=1, source_target_pairs={{0,9},{3,18},{4,13},{7,22},{8,17},{9,0},{11,26},{12,21},{13,4},{15... | collective-permute-start | bytes 393224 | tf_op jit(solution)/shard_map/ppermute | solution.py:244
  19.6 3.8 %collective-permute-start.1 = (f32[256,128]{1,0:T(8,128)S(1)}, f32[256,128]{1,0:T(8,128)S(1)}, u32[]{:S(2)}, u32[]{:S(2)}) collective-permute-start(f32[256,128]{1,0:T(8,128)S(1)} %bitcast.10), channel_id=1, source_target_pairs={{0,25},{3,34},{4,29},{7,38},{8,33},{11,42},{12,37},{15,46},{16,41}... | collective-permute-start | bytes 393224 | tf_op jit(solution)/shard_map/ppermute | solution.py:244
  23.4 7.5 %collective-permute-start.4 = (f32[256,128]{1,0:T(8,128)S(1)}, f32[256,128]{1,0:T(8,128)S(1)}, u32[]{:S(2)}, u32[]{:S(2)}) collective-permute-start(f32[256,128]{1,0:T(8,128)S(1)} %bitcast.11), channel_id=1, source_target_pairs={{0,205},{1,308},{2,103},{3,414},{4,209},{5,312},{6,107},{7,418},{8... | collective-permute-start | bytes 393224 | tf_op jit(solution)/shard_map/ppermute | solution.py:244
  30.9 3.9 %collective-permute-start.5 = (f32[256,128]{1,0:T(8,128)S(1)}, f32[256,128]{1,0:T(8,128)S(1)}, u32[]{:S(2)}, u32[]{:S(2)}) collective-permute-start(f32[256,128]{1,0:T(8,128)S(1)} %bitcast.12), channel_id=1, source_target_pairs={{0,5},{1,257},{2,155},{3,362},{4,260},{5,0},{6,159},{7,366},{8,13}... | collective-permute-start | bytes 393224 | tf_op jit(solution)/shard_map/ppermute | solution.py:244
  34.9 1.9 %collective-permute-start.2 = (f32[256,128]{1,0:T(8,128)S(1)}, f32[256,128]{1,0:T(8,128)S(1)}, u32[]{:S(2)}, u32[]{:S(2)}) collective-permute-start(f32[256,128]{1,0:T(8,128)S(1)} %collective-permute-done.refs_0_), channel_id=1, source_target_pairs={{0,4},{1,5},{2,6},{3,7},{4,0},{5,1},{6,2},{7,3},{8,12},{9,13},{10,... | collective-permute-start | bytes 393224 | tf_op jit(solution)/shard_map/ppermute | solution.py:244
  36.8 0.7 collective-permute-done.1.refs_1_
  37.5 4.6 %collective-permute-start.3 = (f32[256,128]{1,0:T(8,128)S(1)}, f32[256,128]{1,0:T(8,128)S(1)}, u32[]{:S(2)}, u32[]{:S(2)}) collective-permute-start(f32[256,128]{1,0:T(8,128)S(1)} %collective-permute-done.1.refs_1_), channel_id=1, source_target_pairs={{0,4},{1,5},{2,6},{3,7},{4,0},{5,1},{6,2},{7,3},{8,12},{9,13},{10,... | collective-permute-start | bytes 393224 | tf_op jit(solution)/shard_map/ppermute | solution.py:244
  43.5 2.4 %pick.1 = (s32[24]{0:T(128)S(1)}, f32[6,128,128]{2,1,0:T(8,128)S(1)}) custom-call(s32[2]{0:T(128)S(1)} %pad_add_fusion.ids, s32[1,24]{1,0:T(1,128)S(1)} %copy-done, s32[1]{0:T(128)S(6)} %copy.10.counts, f32[24,128,128]{2,1,0:T(8,128)} %bitcast.18), custom_call_target="tpu_custom_call" | custom-call | bytes 786432 | tf_op jit(solution)/shard_map/pick/pallas_call | solution.py:276
  46.4 2.5 %collective-permute-start.6 = (f32[256,128]{1,0:T(8,128)S(1)}, f32[256,128]{1,0:T(8,128)S(1)}, u32[]{:S(2)}, u32[]{:S(2)}) collective-permute-start(f32[256,128]{1,0:T(8,128)S(1)} %partial.1), channel_id=1, source_target_pairs={{0,1},{1,0},{2,3},{3,2},{4,5},{5,4},{6,7},{7,6},{8,9},{9,8},{10,11... | collective-permute-start | bytes 393224 | tf_op jit(solution)/shard_map/ppermute | solution.py:244
  48.9 1.0 collective-permute-done.6
  49.9 4.3 %collective-permute-start.7 = (f32[256,128]{1,0:T(8,128)S(1)}, f32[256,128]{1,0:T(8,128)S(1)}, u32[]{:S(2)}, u32[]{:S(2)}) collective-permute-start(f32[256,128]{1,0:T(8,128)S(1)} %add.8.half), channel_id=1, source_target_pairs={{0,2},{1,3},{2,0},{3,1},{4,6},{5,7},{6,4},{7,5},{8,10},{9,11},{10,... | collective-permute-start | bytes 393224 | tf_op jit(solution)/shard_map/ppermute | solution.py:244
  54.5 3.5 %collective-permute-done.7.other = f32[256,128]{1,0:T(8,128)S(1)} collective-permute-done((f32[256,128]{1,0:T(8,128)S(1)}, f32[256,128]{1,0:T(8,128)S(1)}, u32[]{:S(2)}, u32[]{:S(2)}) %collective-permute-start.7) | collective-permute-done | bytes 131104 | tf_op jit(solution)/shard_map/ppermute | solution.py:244
  58.0 0.9 tiles.1
  58.9 2.0 %collective-permute-start.8 = (f32[2,128,128]{2,1,0:T(8,128)S(1)}, f32[2,128,128]{2,1,0:T(8,128)S(1)}, u32[]{:S(2)}, u32[]{:S(2)}) collective-permute-start(f32[2,128,128]{2,1,0:T(8,128)S(1)} %get-tuple-element.22.side), channel_id=1, source_target_pairs={{0,4},{1,5},{2,6},{3,7},{4,0},{5,1},{6,2},{7,3},{8,12},{9,13},{10,... | collective-permute-start | bytes 393224 | tf_op jit(solution)/shard_map/ppermute | solution.py:244
  60.9 3.7 %collective-permute-done.8 = f32[2,128,128]{2,1,0:T(8,128)S(1)} collective-permute-done((f32[2,128,128]{2,1,0:T(8,128)S(1)}, f32[2,128,128]{2,1,0:T(8,128)S(1)}, u32[]{:S(2)}, u32[]{:S(2)}) %collective-permute-start.8) | collective-permute-done | bytes 131104 | tf_op jit(solution)/shard_map/ppermute | solution.py:244
  64.6 7.4 %collective-permute-start.10 = (f32[2,128,128]{2,1,0:T(8,128)S(1)}, f32[2,128,128]{2,1,0:T(8,128)S(1)}, u32[]{:S(2)}, u32[]{:S(2)}) collective-permute-start(f32[2,128,128]{2,1,0:T(8,128)S(1)} %pad_maximum_fusion.1), channel_id=1, source_target_pairs={{0,25},{3,34},{4,29},{7,38},{8,33},{11,42},{12,37},{15,46},{16,41}... | collective-permute-start | bytes 393224 | tf_op jit(solution)/shard_map/ppermute | solution.py:244
  72.1 2.6 %collective-permute-start.9 = (f32[2,128,128]{2,1,0:T(8,128)S(1)}, f32[2,128,128]{2,1,0:T(8,128)S(1)}, u32[]{:S(2)}, u32[]{:S(2)}) collective-permute-start(f32[2,128,128]{2,1,0:T(8,128)S(1)} %pad_maximum_fusion), channel_id=1, source_target_pairs={{0,9},{3,18},{4,13},{7,22},{8,17},{9,0},{11,26},{12,21},{13,4},{15... | collective-permute-start | bytes 393224 | tf_op jit(solution)/shard_map/ppermute | solution.py:244
  74.6 2.5 %collective-permute-done.10.got_2 = f32[2,128,128]{2,1,0:T(8,128)S(1)} collective-permute-done((f32[2,128,128]{2,1,0:T(8,128)S(1)}, f32[2,128,128]{2,1,0:T(8,128)S(1)}, u32[]{:S(2)}, u32[]{:S(2)}) %collective-permute-start.10) | collective-permute-done | bytes 131104 | tf_op jit(solution)/shard_map/ppermute | solution.py:244
  77.2 3.3 %collective-permute-done.9.got_1 = f32[2,128,128]{2,1,0:T(8,128)S(1)} collective-permute-done((f32[2,128,128]{2,1,0:T(8,128)S(1)}, f32[2,128,128]{2,1,0:T(8,128)S(1)}, u32[]{:S(2)}, u32[]{:S(2)}) %collective-permute-start.9) | collective-permute-done | bytes 131104 | tf_op jit(solution)/shard_map/ppermute | solution.py:244
  80.6 4.9 %collective-permute-start.11 = (f32[4,128,128]{2,1,0:T(8,128)S(1)}, f32[4,128,128]{2,1,0:T(8,128)S(1)}, u32[]{:S(2)}, u32[]{:S(2)}) collective-permute-start(f32[4,128,128]{2,1,0:T(8,128)S(1)} %update_near.1.near), channel_id=1, source_target_pairs={{0,2},{1,3},{2,0},{3,1},{4,6},{5,7},{6,4},{7,5},{8,10},{9,11},{10,... | collective-permute-start | bytes 786440 | tf_op jit(solution)/shard_map/ppermute | solution.py:244
  85.6 5.8 %collective-permute-start.13 = (f32[128,128]{1,0:T(8,128)S(1)}, f32[128,128]{1,0:T(8,128)S(1)}, u32[]{:S(2)}, u32[]{:S(2)}) collective-permute-start(f32[128,128]{1,0:T(8,128)S(1)} %get-tuple-element.23.far_1), channel_id=1, source_target_pairs={{0,205},{1,308},{2,103},{3,414},{4,209},{5,312},{6,107},{7,418},{8... | collective-permute-start | bytes 196616 | tf_op jit(solution)/shard_map/ppermute | solution.py:244
  91.4 3.2 %collective-permute-start.14 = (f32[128,128]{1,0:T(8,128)S(1)}, f32[128,128]{1,0:T(8,128)S(1)}, u32[]{:S(2)}, u32[]{:S(2)}) collective-permute-start(f32[128,128]{1,0:T(8,128)S(1)} %get-tuple-element.24.far_2), channel_id=1, source_target_pairs={{0,5},{1,257},{2,155},{3,362},{4,260},{5,0},{6,159},{7,366},{8,13}... | collective-permute-start | bytes 196616 | tf_op jit(solution)/shard_map/ppermute | solution.py:244
  94.7 7.0 %collective-permute-done.13.got_1 = f32[128,128]{1,0:T(8,128)S(1)} collective-permute-done((f32[128,128]{1,0:T(8,128)S(1)}, f32[128,128]{1,0:T(8,128)S(1)}, u32[]{:S(2)}, u32[]{:S(2)}) %collective-permute-start.13) | collective-permute-done | bytes 65568 | tf_op jit(solution)/shard_map/ppermute | solution.py:244
  101.8 7.6 %collective-permute-start.17 = (f32[6,128,128]{2,1,0:T(8,128)S(1)}, f32[6,128,128]{2,1,0:T(8,128)S(1)}, u32[]{:S(2)}, u32[]{:S(2)}) collective-permute-start(f32[6,128,128]{2,1,0:T(8,128)S(1)} %get-tuple-element.26.refs_0_), channel_id=1, source_target_pairs={{0,1},{1,0},{2,3},{3,2},{4,5},{5,4},{6,7},{7,6},{8,9},{9,8},{10,11... | collective-permute-start | bytes 1179656 | tf_op jit(solution)/shard_map/ppermute | solution.py:244
  109.3 1.9 %collective-permute-start.15 = (f32[2,128,128]{2,1,0:T(8,128)S(1)}, f32[2,128,128]{2,1,0:T(8,128)S(1)}, u32[]{:S(2)}, u32[]{:S(2)}) collective-permute-start(f32[2,128,128]{2,1,0:T(8,128)S(1)} %get-tuple-element.25), channel_id=1, source_target_pairs={{0,2},{1,3},{2,0},{3,1},{4,6},{5,7},{6,4},{7,5},{8,10},{9,11},{10,... | collective-permute-start | bytes 393224 | tf_op jit(solution)/shard_map/ppermute | solution.py:244
  111.3 1.9 %collective-permute-start.12 = (f32[4,128,128]{2,1,0:T(8,128)S(1)}, f32[4,128,128]{2,1,0:T(8,128)S(1)}, u32[]{:S(2)}, u32[]{:S(2)}) collective-permute-start(f32[4,128,128]{2,1,0:T(8,128)S(1)} %collective-permute-done.11.refs_2_), channel_id=1, source_target_pairs={{0,1},{1,0},{2,3},{3,2},{4,5},{5,4},{6,7},{7,6},{8,9},{9,8},{10,11... | collective-permute-start | bytes 786440 | tf_op jit(solution)/shard_map/ppermute | solution.py:244
  113.2 4.6 %collective-permute-done.15.refs_3_ = f32[2,128,128]{2,1,0:T(8,128)S(1)} collective-permute-done((f32[2,128,128]{2,1,0:T(8,128)S(1)}, f32[2,128,128]{2,1,0:T(8,128)S(1)}, u32[]{:S(2)}, u32[]{:S(2)}) %collective-permute-start.15) | collective-permute-done | bytes 131104 | tf_op jit(solution)/shard_map/ppermute | solution.py:244
  117.8 2.8 %collective-permute-start.16 = (f32[2,128,128]{2,1,0:T(8,128)S(1)}, f32[2,128,128]{2,1,0:T(8,128)S(1)}, u32[]{:S(2)}, u32[]{:S(2)}) collective-permute-start(f32[2,128,128]{2,1,0:T(8,128)S(1)} %collective-permute-done.15.refs_3_), channel_id=1, source_target_pairs={{0,1},{1,0},{2,3},{3,2},{4,5},{5,4},{6,7},{7,6},{8,9},{9,8},{10,11... | collective-permute-start | bytes 393224 | tf_op jit(solution)/shard_map/ppermute | solution.py:244
  120.5 1.1 blank.1.refs_5_
  121.7 1.5 %shard_map.59 = (f32[24,128,128]{2,1,0:T(8,128)}, f32[64,128]{1,0:T(8,128)}) custom-call(s32[24]{0:T(128)S(1)} %get-tuple-element.16.slots, s32[2]{0:T(128)S(1)} %pad_add_fusion.ids, f32[6,128,128]{2,1,0:T(8,128)S(1)} %get-tuple-element.26.refs_0_, f32[6,128,128]{2,1,0:T(8,128)S(1)} %collective-permute-done.17.refs_1_, ...), custom_call_target="tpu_custom_call", output_to_operand_aliasing={{0}: (7, {})} | custom-call | bytes 2359296 | tf_op jit(solution)/shard_map/pallas_call | solution.py:400
  123.2 1.3 %shard_map.60 = f32[24,128,128]{2,1,0:T(8,128)} custom-call(s32[24]{0:T(128)S(1)} %get-tuple-element.16.slots, s32[2]{0:T(128)S(1)} %pad_add_fusion.ids, f32[4,128,128]{2,1,0:T(8,128)S(1)} %collective-permute-done.12.refs_0_, f32[2,128,128]{2,1,0:T(8,128)S(1)} %collective-permute-done.16.refs_1_, ...), custom_call_target="tpu_custom_call", output_to_operand_aliasing={{}: (4, {})} | custom-call | bytes 786432 | tf_op jit(solution)/shard_map/pallas_call | solution.py:400
  (21 shorter events, 1.9 us)
Async XLA Ops:
  8.3 26.6 %collective-permute-start = (f32[256,128]{1,0:T(8,128)S(1)}, f32[256,128]{1,0:T(8,128)S(1)}, u32[]{:S(2)}, u32[]{:S(2)}) collective-permute-start(f32[256,128]{1,0:T(8,128)S(1)} %bitcast.9), channel_id=1, source_target_pairs={{0,9},{3,18},{4,13},{7,22},{8,17},{9,0},{11,26},{12,21},{13,4},{15... | collective-permute-start | bytes 393224 | tf_op jit(solution)/shard_map/ppermute | solution.py:244
  19.6 17.9 %collective-permute-start.1 = (f32[256,128]{1,0:T(8,128)S(1)}, f32[256,128]{1,0:T(8,128)S(1)}, u32[]{:S(2)}, u32[]{:S(2)}) collective-permute-start(f32[256,128]{1,0:T(8,128)S(1)} %bitcast.10), channel_id=1, source_target_pairs={{0,25},{3,34},{4,29},{7,38},{8,33},{11,42},{12,37},{15,46},{16,41}... | collective-permute-start | bytes 393224 | tf_op jit(solution)/shard_map/ppermute | solution.py:244
  23.4 22.5 %collective-permute-start.4 = (f32[256,128]{1,0:T(8,128)S(1)}, f32[256,128]{1,0:T(8,128)S(1)}, u32[]{:S(2)}, u32[]{:S(2)}) collective-permute-start(f32[256,128]{1,0:T(8,128)S(1)} %bitcast.11), channel_id=1, source_target_pairs={{0,205},{1,308},{2,103},{3,414},{4,209},{5,312},{6,107},{7,418},{8... | collective-permute-start | bytes 393224 | tf_op jit(solution)/shard_map/ppermute | solution.py:244
  30.9 14.9 %collective-permute-start.5 = (f32[256,128]{1,0:T(8,128)S(1)}, f32[256,128]{1,0:T(8,128)S(1)}, u32[]{:S(2)}, u32[]{:S(2)}) collective-permute-start(f32[256,128]{1,0:T(8,128)S(1)} %bitcast.12), channel_id=1, source_target_pairs={{0,5},{1,257},{2,155},{3,362},{4,260},{5,0},{6,159},{7,366},{8,13}... | collective-permute-start | bytes 393224 | tf_op jit(solution)/shard_map/ppermute | solution.py:244
  34.9 11.0 %collective-permute-start.2 = (f32[256,128]{1,0:T(8,128)S(1)}, f32[256,128]{1,0:T(8,128)S(1)}, u32[]{:S(2)}, u32[]{:S(2)}) collective-permute-start(f32[256,128]{1,0:T(8,128)S(1)} %collective-permute-done.refs_0_), channel_id=1, source_target_pairs={{0,4},{1,5},{2,6},{3,7},{4,0},{5,1},{6,2},{7,3},{8,12},{9,13},{10,... | collective-permute-start | bytes 393224 | tf_op jit(solution)/shard_map/ppermute | solution.py:244
  37.5 8.4 %collective-permute-start.3 = (f32[256,128]{1,0:T(8,128)S(1)}, f32[256,128]{1,0:T(8,128)S(1)}, u32[]{:S(2)}, u32[]{:S(2)}) collective-permute-start(f32[256,128]{1,0:T(8,128)S(1)} %collective-permute-done.1.refs_1_), channel_id=1, source_target_pairs={{0,4},{1,5},{2,6},{3,7},{4,0},{5,1},{6,2},{7,3},{8,12},{9,13},{10,... | collective-permute-start | bytes 393224 | tf_op jit(solution)/shard_map/ppermute | solution.py:244
  42.8 0.7 copy-start
  46.4 3.5 %collective-permute-start.6 = (f32[256,128]{1,0:T(8,128)S(1)}, f32[256,128]{1,0:T(8,128)S(1)}, u32[]{:S(2)}, u32[]{:S(2)}) collective-permute-start(f32[256,128]{1,0:T(8,128)S(1)} %partial.1), channel_id=1, source_target_pairs={{0,1},{1,0},{2,3},{3,2},{4,5},{5,4},{6,7},{7,6},{8,9},{9,8},{10,11... | collective-permute-start | bytes 393224 | tf_op jit(solution)/shard_map/ppermute | solution.py:244
  49.9 8.1 %collective-permute-start.7 = (f32[256,128]{1,0:T(8,128)S(1)}, f32[256,128]{1,0:T(8,128)S(1)}, u32[]{:S(2)}, u32[]{:S(2)}) collective-permute-start(f32[256,128]{1,0:T(8,128)S(1)} %add.8.half), channel_id=1, source_target_pairs={{0,2},{1,3},{2,0},{3,1},{4,6},{5,7},{6,4},{7,5},{8,10},{9,11},{10,... | collective-permute-start | bytes 393224 | tf_op jit(solution)/shard_map/ppermute | solution.py:244
  58.9 5.7 %collective-permute-start.8 = (f32[2,128,128]{2,1,0:T(8,128)S(1)}, f32[2,128,128]{2,1,0:T(8,128)S(1)}, u32[]{:S(2)}, u32[]{:S(2)}) collective-permute-start(f32[2,128,128]{2,1,0:T(8,128)S(1)} %get-tuple-element.22.side), channel_id=1, source_target_pairs={{0,4},{1,5},{2,6},{3,7},{4,0},{5,1},{6,2},{7,3},{8,12},{9,13},{10,... | collective-permute-start | bytes 393224 | tf_op jit(solution)/shard_map/ppermute | solution.py:244
  64.6 12.5 %collective-permute-start.10 = (f32[2,128,128]{2,1,0:T(8,128)S(1)}, f32[2,128,128]{2,1,0:T(8,128)S(1)}, u32[]{:S(2)}, u32[]{:S(2)}) collective-permute-start(f32[2,128,128]{2,1,0:T(8,128)S(1)} %pad_maximum_fusion.1), channel_id=1, source_target_pairs={{0,25},{3,34},{4,29},{7,38},{8,33},{11,42},{12,37},{15,46},{16,41}... | collective-permute-start | bytes 393224 | tf_op jit(solution)/shard_map/ppermute | solution.py:244
  72.1 8.4 %collective-permute-start.9 = (f32[2,128,128]{2,1,0:T(8,128)S(1)}, f32[2,128,128]{2,1,0:T(8,128)S(1)}, u32[]{:S(2)}, u32[]{:S(2)}) collective-permute-start(f32[2,128,128]{2,1,0:T(8,128)S(1)} %pad_maximum_fusion), channel_id=1, source_target_pairs={{0,9},{3,18},{4,13},{7,22},{8,17},{9,0},{11,26},{12,21},{13,4},{15... | collective-permute-start | bytes 393224 | tf_op jit(solution)/shard_map/ppermute | solution.py:244
  80.6 30.6 %collective-permute-start.11 = (f32[4,128,128]{2,1,0:T(8,128)S(1)}, f32[4,128,128]{2,1,0:T(8,128)S(1)}, u32[]{:S(2)}, u32[]{:S(2)}) collective-permute-start(f32[4,128,128]{2,1,0:T(8,128)S(1)} %update_near.1.near), channel_id=1, source_target_pairs={{0,2},{1,3},{2,0},{3,1},{4,6},{5,7},{6,4},{7,5},{8,10},{9,11},{10,... | collective-permute-start | bytes 786440 | tf_op jit(solution)/shard_map/ppermute | solution.py:244
  85.6 16.0 %collective-permute-start.13 = (f32[128,128]{1,0:T(8,128)S(1)}, f32[128,128]{1,0:T(8,128)S(1)}, u32[]{:S(2)}, u32[]{:S(2)}) collective-permute-start(f32[128,128]{1,0:T(8,128)S(1)} %get-tuple-element.23.far_1), channel_id=1, source_target_pairs={{0,205},{1,308},{2,103},{3,414},{4,209},{5,312},{6,107},{7,418},{8... | collective-permute-start | bytes 196616 | tf_op jit(solution)/shard_map/ppermute | solution.py:244
  91.4 10.2 %collective-permute-start.14 = (f32[128,128]{1,0:T(8,128)S(1)}, f32[128,128]{1,0:T(8,128)S(1)}, u32[]{:S(2)}, u32[]{:S(2)}) collective-permute-start(f32[128,128]{1,0:T(8,128)S(1)} %get-tuple-element.24.far_2), channel_id=1, source_target_pairs={{0,5},{1,257},{2,155},{3,362},{4,260},{5,0},{6,159},{7,366},{8,13}... | collective-permute-start | bytes 196616 | tf_op jit(solution)/shard_map/ppermute | solution.py:244
  101.8 19.9 %collective-permute-start.17 = (f32[6,128,128]{2,1,0:T(8,128)S(1)}, f32[6,128,128]{2,1,0:T(8,128)S(1)}, u32[]{:S(2)}, u32[]{:S(2)}) collective-permute-start(f32[6,128,128]{2,1,0:T(8,128)S(1)} %get-tuple-element.26.refs_0_), channel_id=1, source_target_pairs={{0,1},{1,0},{2,3},{3,2},{4,5},{5,4},{6,7},{7,6},{8,9},{9,8},{10,11... | collective-permute-start | bytes 1179656 | tf_op jit(solution)/shard_map/ppermute | solution.py:244
  109.3 8.4 %collective-permute-start.15 = (f32[2,128,128]{2,1,0:T(8,128)S(1)}, f32[2,128,128]{2,1,0:T(8,128)S(1)}, u32[]{:S(2)}, u32[]{:S(2)}) collective-permute-start(f32[2,128,128]{2,1,0:T(8,128)S(1)} %get-tuple-element.25), channel_id=1, source_target_pairs={{0,2},{1,3},{2,0},{3,1},{4,6},{5,7},{6,4},{7,5},{8,10},{9,11},{10,... | collective-permute-start | bytes 393224 | tf_op jit(solution)/shard_map/ppermute | solution.py:244
  111.3 12.0 %collective-permute-start.12 = (f32[4,128,128]{2,1,0:T(8,128)S(1)}, f32[4,128,128]{2,1,0:T(8,128)S(1)}, u32[]{:S(2)}, u32[]{:S(2)}) collective-permute-start(f32[4,128,128]{2,1,0:T(8,128)S(1)} %collective-permute-done.11.refs_2_), channel_id=1, source_target_pairs={{0,1},{1,0},{2,3},{3,2},{4,5},{5,4},{6,7},{7,6},{8,9},{9,8},{10,11... | collective-permute-start | bytes 786440 | tf_op jit(solution)/shard_map/ppermute | solution.py:244
  117.8 5.5 %collective-permute-start.16 = (f32[2,128,128]{2,1,0:T(8,128)S(1)}, f32[2,128,128]{2,1,0:T(8,128)S(1)}, u32[]{:S(2)}, u32[]{:S(2)}) collective-permute-start(f32[2,128,128]{2,1,0:T(8,128)S(1)} %collective-permute-done.15.refs_3_), channel_id=1, source_target_pairs={{0,1},{1,0},{2,3},{3,2},{4,5},{5,4},{6,7},{7,6},{8,9},{9,8},{10,11... | collective-permute-start | bytes 393224 | tf_op jit(solution)/shard_map/ppermute | solution.py:244
